TPU v7x, 128 devices: a whole 4x4x4 slice. The times are simulated.
128 devices in a mesh: wide: 32 (over x, z_hi, y), narrow: 4 (over z_lo, core).
Axes of the slice: x: 4, y: 4, z: 4 (z_hi: 2, z_lo: 2; z = z_hi * 2 + z_lo), core: 2. Of those that a mesh axis runs over, the one named last changes fastest.
Arguments:
- tokens: bfloat16 [49152, 512], P(('wide', 'narrow')), may hold values from -6 to 6
- cotangent: bfloat16 [49152, 512], P(('wide', 'narrow')), may hold values from -6 to 6
- lengths: int32 [32, 3], P('wide'), may hold values from 1 to 768, 1536 in all within a row
- master: float32 [3277824], P('narrow'), may hold values from -2 to 2
- first_moment: float32 [3277824], P('narrow'), may hold values from -0.6 to 0.6
- second_moment: float32 [3277824], P('narrow'), may hold values from 0.001 to 0.03
Outputs:
- output: bfloat16 [49152, 512], P(('wide', 'narrow'))
- d_tokens: bfloat16 [49152, 512], P(('wide', 'narrow'))
- gradient: float32 [3277824], P('narrow')
- new_master: float32 [3277824], P('narrow')
- new_first: float32 [3277824], P('narrow')
- new_second: float32 [3277824], P('narrow')
Inputs may be any that keep to these rules, and one draw needn't show every extreme that they name: Row g holds in order the lengths of the 3 sequences that fill group g's 1536 tokens.
All inputs are finite; a program needn't handle non-finite values.
Results may differ from a plain program's by a relative error of at most 0.015.
The roundings to bfloat16 on the way count: a program that leaves them out, or rounds other values in their place, can miss the bound.
Values may be sent and summed in bfloat16 or wider, within the bound.
A program may use at most 192 MiB of HBM per device.

v0:
```python
import math

import jax
import jax.numpy as jnp
from jax import lax
from jax.sharding import PartitionSpec as P

MODEL_WIDTH = 512
QUERY_HEADS = 15
KEYVAL_HEADS = 5
HEAD_SIZE = 64
FEEDFWD_UNITS = 1280
STEP = 4
NPARAM = 3277824


eps_norm = 1e-05
rope_base = 100000.0
beta_one = 0.9
beta_two = 0.95
learn_rate = 0.03
decay_rate = 0.1
adam_eps = 1e-08
masked_logits = -1e30


def unpack(flat):
    arrangement_list = [
        (MODEL_WIDTH, QUERY_HEADS * HEAD_SIZE),
        (MODEL_WIDTH, KEYVAL_HEADS * HEAD_SIZE),
        (MODEL_WIDTH, KEYVAL_HEADS * HEAD_SIZE),
        (QUERY_HEADS * HEAD_SIZE, MODEL_WIDTH),
        (MODEL_WIDTH, FEEDFWD_UNITS),
        (MODEL_WIDTH, FEEDFWD_UNITS),
        (FEEDFWD_UNITS, MODEL_WIDTH),
        (MODEL_WIDTH,),
        (MODEL_WIDTH,),
    ]
    pieces = []
    offset = 0
    for layout in arrangement_list:
        length = math.prod(layout)
        pieces.append(flat[offset : offset + length].reshape(layout))
        offset = offset + length
    return pieces


def place_tokens(indices, lengths_row):
    seq_ends = jnp.cumsum(lengths_row)
    seq_starts = seq_ends - lengths_row
    member = (indices[:, None] >= seq_starts[None, :]) & (indices[:, None] < seq_ends[None, :])
    numbers = jnp.arange(lengths_row.shape[0], dtype=jnp.int32)
    segment = jnp.sum(jnp.where(member, numbers[None, :], 0), axis=1)
    token_position = indices - jnp.sum(jnp.where(member, seq_starts[None, :], 0), axis=1)
    return (segment, token_position)


def normalize(values):
    inverse_rms = lax.rsqrt(jnp.mean(values * values, axis=-1, keepdims=True) + eps_norm)
    return (values * inverse_rms, inverse_rms)


def apply_rotary(values, token_position, head_count, turn_sign):
    half_dim = HEAD_SIZE // 2
    inverse = rope_base ** (-2.0 * jnp.arange(half_dim, dtype=jnp.float32) / HEAD_SIZE)
    angles = token_position.astype(jnp.float32)[:, None] * inverse[None, :]
    cosine = jnp.cos(angles)[:, None, :]
    sine = turn_sign * jnp.sin(angles)[:, None, :]
    shaped = values.reshape(values.shape[0], head_count, HEAD_SIZE)
    first_half = shaped[:, :, :half_dim]
    second_half = shaped[:, :, half_dim:]
    turned = jnp.concatenate(
        [first_half * cosine - second_half * sine, second_half * cosine + first_half * sine],
        axis=-1,
    )
    return turned.reshape(values.shape)


def keep_carry(carry):
    return carry


def body(tokens, cotangent, lengths, master, first_moment, second_moment):
    token_rows = tokens.shape[0]
    narrow_size = lax.axis_size("narrow")
    group_rows = token_rows * narrow_size
    narrow_rank = lax.axis_index("narrow")
    group_width = QUERY_HEADS // KEYVAL_HEADS
    score_scale = HEAD_SIZE ** (-0.5)
    replica = lax.all_gather(master.astype(jnp.bfloat16), "narrow", axis=0, tiled=True)
    w_query, w_key, w_value, w_out, w_gate, w_up, w_down, gain_one, gain_two = unpack(replica)
    lengths_row = lengths[0]
    local_index = narrow_rank * token_rows + jnp.arange(token_rows, dtype=jnp.int32)
    segment, token_position = place_tokens(local_index, lengths_row)
    group_index = jnp.arange(group_rows, dtype=jnp.int32)
    key_segment = place_tokens(group_index, lengths_row)[0]
    first_start = local_index[0] - token_position[0]
    last_index = local_index[token_rows - 1]
    range_rows = min(512, group_rows)
    span_starts = list(range(0, group_rows, range_rows))
    resid = tokens.astype(jnp.float32)
    normed_one, inverse_one = normalize(resid)
    hidden_one = (normed_one * gain_one.astype(jnp.float32)).astype(jnp.bfloat16)
    query = jnp.dot(hidden_one, w_query, preferred_element_type=jnp.float32)
    key_projection = jnp.dot(hidden_one, w_key, preferred_element_type=jnp.float32)
    value_proj = jnp.dot(hidden_one, w_value, preferred_element_type=jnp.float32)
    query_batch = apply_rotary(query, token_position, QUERY_HEADS, 1.0).astype(jnp.bfloat16)
    key_batch = apply_rotary(key_projection, token_position, KEYVAL_HEADS, 1.0).astype(jnp.bfloat16)
    value_batch = value_proj.astype(jnp.bfloat16)
    key_all, value_all = (
        lax.all_gather(key_batch, "narrow", axis=0, tiled=True),
        lax.all_gather(value_batch, "narrow", axis=0, tiled=True),
    )
    query_tensor_split = query_batch.reshape(token_rows, KEYVAL_HEADS, group_width, HEAD_SIZE)

    def span_setup(span_start, key_source, value_source):
        key_tensor_split = lax.slice_in_dim(
            key_source, span_start, span_start + range_rows
        ).reshape(range_rows, KEYVAL_HEADS, HEAD_SIZE)
        value_tensor_split = lax.slice_in_dim(
            value_source, span_start, span_start + range_rows
        ).reshape(range_rows, KEYVAL_HEADS, HEAD_SIZE)
        span_segment = lax.slice_in_dim(key_segment, span_start, span_start + range_rows)
        span_index = lax.slice_in_dim(group_index, span_start, span_start + range_rows)
        allowed = (segment[:, None] == span_segment[None, :]) & (
            span_index[None, :] <= local_index[:, None]
        )
        needed = (span_start <= last_index) & (span_start + range_rows - 1 >= first_start)
        return (key_tensor_split, value_tensor_split, allowed[None, None], needed)

    running_maximum = jnp.full((KEYVAL_HEADS, group_width, token_rows), masked_logits, jnp.float32)
    running_denominator = jnp.zeros((KEYVAL_HEADS, group_width, token_rows), jnp.float32)
    for span_start in span_starts:
        key_tensor_split, value_tensor_split, allowed, needed = span_setup(
            span_start, key_all, value_all
        )

        def extend(carry):
            old_top, old_total = carry
            scores = (
                jnp.einsum(
                    "qgrd,kgd->grqk",
                    query_tensor_split,
                    key_tensor_split,
                    preferred_element_type=jnp.float32,
                )
                * score_scale
            )
            new_top = jnp.maximum(
                old_top, jnp.max(jnp.where(allowed, scores, masked_logits), axis=-1)
            )
            span_sum = jnp.sum(
                jnp.where(allowed, jnp.exp(scores - new_top[..., None]), 0.0), axis=-1
            )
            return (new_top, old_total * jnp.exp(old_top - new_top) + span_sum)

        running_maximum, running_denominator = lax.cond(
            needed, extend, keep_carry, (running_maximum, running_denominator)
        )
    lse = running_maximum + jnp.log(running_denominator)
    running_total = jnp.zeros((token_rows, KEYVAL_HEADS, group_width, HEAD_SIZE), jnp.float32)
    for span_start in span_starts:
        key_tensor_split, value_tensor_split, allowed, needed = span_setup(
            span_start, key_all, value_all
        )

        def weigh_values(carry):
            scores = (
                jnp.einsum(
                    "qgrd,kgd->grqk",
                    query_tensor_split,
                    key_tensor_split,
                    preferred_element_type=jnp.float32,
                )
                * score_scale
            )
            probs_b = jnp.where(allowed, jnp.exp(scores - lse[..., None]), 0.0).astype(jnp.bfloat16)
            return carry + jnp.einsum(
                "grqk,kgd->qgrd", probs_b, value_tensor_split, preferred_element_type=jnp.float32
            )

        running_total = lax.cond(needed, weigh_values, keep_carry, running_total)
    attention_output = running_total.reshape(token_rows, QUERY_HEADS * HEAD_SIZE).astype(
        jnp.bfloat16
    )
    mixed = resid + jnp.dot(attention_output, w_out, preferred_element_type=jnp.float32)
    normed_two, inverse_two = normalize(mixed)
    hidden_two = (normed_two * gain_two.astype(jnp.float32)).astype(jnp.bfloat16)
    gate = jnp.dot(hidden_two, w_gate, preferred_element_type=jnp.float32)
    upward = jnp.dot(hidden_two, w_up, preferred_element_type=jnp.float32)
    sigma = jax.nn.sigmoid(gate)
    activated = (gate * sigma * upward).astype(jnp.bfloat16)
    output = (mixed + jnp.dot(activated, w_down, preferred_element_type=jnp.float32)).astype(
        jnp.bfloat16
    )
    d_act = jnp.dot(cotangent, w_down.T, preferred_element_type=jnp.float32)
    g_down = jnp.dot(activated.T, cotangent, preferred_element_type=jnp.float32)
    d_gate = (d_act * upward * sigma * (1.0 + gate * (1.0 - sigma))).astype(jnp.bfloat16)
    d_up = (d_act * gate * sigma).astype(jnp.bfloat16)
    g_gate = jnp.dot(hidden_two.T, d_gate, preferred_element_type=jnp.float32)
    g_up = jnp.dot(hidden_two.T, d_up, preferred_element_type=jnp.float32)
    d_hidden_two = jnp.dot(d_gate, w_gate.T, preferred_element_type=jnp.float32) + jnp.dot(
        d_up, w_up.T, preferred_element_type=jnp.float32
    )
    g_gain_two = jnp.sum(d_hidden_two * normed_two, axis=0)
    dn_two = d_hidden_two * gain_two.astype(jnp.float32)
    d_mixed = cotangent.astype(jnp.float32) + inverse_two * (
        dn_two - normed_two * jnp.mean(dn_two * normed_two, axis=-1, keepdims=True)
    )
    d_mixed_b = d_mixed.astype(jnp.bfloat16)
    g_out = jnp.dot(attention_output.T, d_mixed_b, preferred_element_type=jnp.float32)
    attention_output_gradient = jnp.dot(
        d_mixed_b, w_out.T, preferred_element_type=jnp.float32
    ).astype(jnp.bfloat16)
    split_gradient = attention_output_gradient.reshape(
        token_rows, KEYVAL_HEADS, group_width, HEAD_SIZE
    )
    attention_output_split = attention_output.reshape(
        token_rows, KEYVAL_HEADS, group_width, HEAD_SIZE
    )
    softmax_correction = jnp.sum(
        split_gradient.astype(jnp.float32) * attention_output_split.astype(jnp.float32), axis=-1
    ).transpose(1, 2, 0)
    key_back, value_back = (key_all, value_all)
    query_gradient_running = jnp.zeros(
        (token_rows, KEYVAL_HEADS, group_width, HEAD_SIZE), jnp.float32
    )
    key_contributions = []
    value_contributions = []
    for span_start in span_starts:
        key_tensor_split, value_tensor_split, allowed, needed = span_setup(
            span_start, key_back, value_back
        )

        def back_span(carry):
            scores = (
                jnp.einsum(
                    "qgrd,kgd->grqk",
                    query_tensor_split,
                    key_tensor_split,
                    preferred_element_type=jnp.float32,
                )
                * score_scale
            )
            probs = jnp.where(allowed, jnp.exp(scores - lse[..., None]), 0.0)
            probs_b = probs.astype(jnp.bfloat16)
            value_gradient_range = jnp.einsum(
                "pozf,zpom->fpm", probs_b, split_gradient, preferred_element_type=jnp.float32
            )
            d_probs = jnp.einsum(
                "qgrd,kgd->grqk",
                split_gradient,
                value_tensor_split,
                preferred_element_type=jnp.float32,
            )
            score_gradient = (
                probs * (d_probs - softmax_correction[..., None]) * score_scale
            ).astype(jnp.bfloat16)
            new_acc = carry + jnp.einsum(
                "grqk,kgd->qgrd",
                score_gradient,
                key_tensor_split,
                preferred_element_type=jnp.float32,
            )
            key_gradient_range = jnp.einsum(
                "pozf,zpom->fpm",
                score_gradient,
                query_tensor_split,
                preferred_element_type=jnp.float32,
            )
            return (new_acc, key_gradient_range, value_gradient_range)

        def skip_span(carry):
            blank_range = jnp.zeros((range_rows, KEYVAL_HEADS, HEAD_SIZE), jnp.float32)
            return (carry, blank_range, blank_range)

        query_gradient_running, key_gradient_range, value_gradient_range = lax.cond(
            needed, back_span, skip_span, query_gradient_running
        )
        key_contributions.append(key_gradient_range.reshape(range_rows, KEYVAL_HEADS * HEAD_SIZE))
        value_contributions.append(
            value_gradient_range.reshape(range_rows, KEYVAL_HEADS * HEAD_SIZE)
        )
    key_sum_in = jnp.concatenate(key_contributions, axis=0)
    value_sum_in = jnp.concatenate(value_contributions, axis=0)
    key_gradient, value_gradient = (
        lax.psum_scatter(key_sum_in, "narrow", scatter_dimension=0, tiled=True),
        lax.psum_scatter(value_sum_in, "narrow", scatter_dimension=0, tiled=True),
    )
    d_query = query_gradient_running.reshape(token_rows, QUERY_HEADS * HEAD_SIZE)
    d_query_b = apply_rotary(d_query, token_position, QUERY_HEADS, -1.0).astype(jnp.bfloat16)
    key_gradient_batch = apply_rotary(key_gradient, token_position, KEYVAL_HEADS, -1.0).astype(
        jnp.bfloat16
    )
    value_gradient_batch = value_gradient.astype(jnp.bfloat16)
    g_query = jnp.dot(hidden_one.T, d_query_b, preferred_element_type=jnp.float32)
    g_key = jnp.dot(hidden_one.T, key_gradient_batch, preferred_element_type=jnp.float32)
    g_value = jnp.dot(hidden_one.T, value_gradient_batch, preferred_element_type=jnp.float32)
    d_hidden_one = (
        jnp.dot(d_query_b, w_query.T, preferred_element_type=jnp.float32)
        + jnp.dot(key_gradient_batch, w_key.T, preferred_element_type=jnp.float32)
        + jnp.dot(value_gradient_batch, w_value.T, preferred_element_type=jnp.float32)
    )
    g_gain_one = jnp.sum(d_hidden_one * normed_one, axis=0)
    dn_one = d_hidden_one * gain_one.astype(jnp.float32)
    d_tokens = (
        d_mixed
        + inverse_one
        * (dn_one - normed_one * jnp.mean(dn_one * normed_one, axis=-1, keepdims=True))
    ).astype(jnp.bfloat16)
    local_grads = jnp.concatenate(
        [
            g_query.reshape(-1),
            g_key.reshape(-1),
            g_value.reshape(-1),
            g_out.reshape(-1),
            g_gate.reshape(-1),
            g_up.reshape(-1),
            g_down.reshape(-1),
            g_gain_one,
            g_gain_two,
        ]
    )
    shard_len = master.shape[0]
    whole_sum = lax.psum(local_grads, ("wide", "narrow"))
    summed = lax.dynamic_slice_in_dim(whole_sum, narrow_rank * shard_len, shard_len)
    token_total = token_rows * narrow_size * lax.axis_size("wide")
    gradient = summed * (1.0 / math.sqrt(token_total))
    new_first = beta_one * first_moment + (1.0 - beta_one) * gradient
    new_second = beta_two * second_moment + (1.0 - beta_two) * gradient * gradient
    first_hat = new_first / (1.0 - beta_one**STEP)
    second_hat = new_second / (1.0 - beta_two**STEP)
    entry_index = narrow_rank * shard_len + jnp.arange(shard_len, dtype=jnp.int32)
    decay = jnp.where(entry_index < NPARAM - 2 * MODEL_WIDTH, decay_rate, 0.0)
    new_master = master - learn_rate * (
        first_hat / (jnp.sqrt(second_hat) + adam_eps) + decay * master
    )
    return (output, d_tokens, gradient, new_master, new_first, new_second)


def solution(mesh):
    in_specs = (
        P(("wide", "narrow"), None),
        P(("wide", "narrow"), None),
        P("wide", None),
        P("narrow"),
        P("narrow"),
        P("narrow"),
    )
    out_specs = (
        P(("wide", "narrow"), None),
        P(("wide", "narrow"), None),
        P("narrow"),
        P("narrow"),
        P("narrow"),
        P("narrow"),
    )
    return jax.shard_map(body, mesh=mesh, in_specs=in_specs, out_specs=out_specs, check_vma=False)
```

profile of v0, /device:TPU:0, one launch (start us, length us, event | category | flops | bytes accessed | tf_op | source)
XLA Modules:
  0.0 714.5 jit_solution(10033406457233650297)
XLA Ops:
  9.4 19.5 %reshape.615 = bf16[1,1,819456]{2,1,0:T(2,128)(2,1)} reshape(bf16[819456]{0:T(1024)(128)(2,1)S(1)} %convert_element_type.166) | data formatting | bytes 3277824
  36.1 114.2 %all-gather.3.cloned.1.call-done = bf16[4,1,819456]{2,1,0:T(2,128)(2,1)} async-done(((bf16[1,1,819456]{2,1,0:T(2,128)(2,1)}), bf16[4,1,819456]{2,1,0:T(2,128)(2,1)}) %all-gather.3.cloned.1.call-update) | async-done | bytes 6555664 | tf_op jit(solution)/shard_map/all_gather | solution.py:90
  150.3 124.5 %reduce = bf16[4,819456]{1,0:T(4,128)(2,1)} reduce(bf16[4,1,819456]{2,1,0:T(2,128)(2,1)} %all-gather.3.cloned.1.call-done, bf16[]{:T(256)} %constant.144), dimensions={1}, to_apply=%all-gather.reduce_sub_computation | reduce | bytes 13111298 | tf_op jit(solution)/shard_map/all_gather | solution.py:90
  274.8 8.1 %reshape.616 = bf16[3277824]{0:T(1024)(128)(2,1)} reshape(bf16[4,819456]{1,0:T(4,128)(2,1)} %reduce) | data formatting | bytes 13111296
  287.6 4.1 fusion.144
  292.8 10.4 %all_gather.10 = bf16[1536,320]{0,1:T(8,128)(2,1)S(1)} all-gather(bf16[384,320]{0,1:T(8,128)(2,1)S(1)} %bitcast.417), channel_id=1, replica_groups=mesh['wide'=32,'narrow'=4] {'narrow'}, dimensions={0}, use_global_device_ids=true | all-gather | bytes 1228800 | tf_op jit(solution)/shard_map/all_gather | solution.py:111
  310.6 9.7 %all_gather.11 = bf16[1536,320]{0,1:T(8,128)(2,1)S(1)} all-gather(bf16[384,320]{0,1:T(8,128)(2,1)S(1)} %convolution_convert_fusion.1), channel_id=1, replica_groups=mesh['wide'=32,'narrow'=4] {'narrow'}, dimensions={0}, use_global_device_ids=true | all-gather | bytes 1228800 | tf_op jit(solution)/shard_map/all_gather | solution.py:112
  322.4 15.5 %conditional.9 = (f32[5,3,384]{2,1,0:T(4,128)}, f32[5,3,384]{2,1,0:T(4,128)S(1)}) conditional(s32[]{:T(128)} %bitcast.87, () %tuple.93, (pred[1,1,384,512]{2,3,1,0:T(8,128)(4,1)}, bf16[512,5,64]{0,2,1:T(8,128)(2,1)S(1)}, bf16[384,5,3,64]{0,3,2,1:T(8,128)(2,1)S(1)}) %tuple.198), branch_computations={%region_5.6_spmd, %region_6.9_spmd} | conditional | flops 398148480 | bytes 26021932 | solution.py:157
  338.8 9.4 %conditional.12 = (f32[384,5,3,64]{0,3,2,1:T(8,128)S(1)}) conditional(s32[]{:T(128)} %bitcast.87, () %tuple.92, (pred[1,1,384,512]{2,3,1,0:T(8,128)(4,1)}, bf16[512,5,64]{0,2,1:T(8,128)(2,1)S(1)}, bf16[384,5,3,64]{0,3,2,1:T(8,128)(2,1)S(1)}, f32[5,3,384]{2,1,0:T(4,128)S(1)}, bf16[512,5,64]{0,2,1:T(8,128)(2,1)}) %tuple.207), branch_computations={%region_17.18_spmd, %region_18.19_spmd} | conditional | flops 766771200 | bytes 4397604 | solution.py:182
  339.5 4.4 fusion.26
  354.6 3.8 reshape.601
  358.5 3.8 reshape.602
  373.5 5.0 multiply_convert_fusion
  384.1 14.3 %conditional.15 = (f32[384,5,3,64]{0,3,2,1:T(8,128)S(1)}, f32[512,320]{0,1:T(8,128)S(1)}, f32[512,320]{0,1:T(8,128)S(1)}) conditional(s32[]{:T(128)} %bitcast.87, () %tuple.100, (pred[1,1,384,512]{2,3,1,0:T(8,128)(4,1)S(1)}, bf16[512,5,64]{0,2,1:T(8,128)(2,1)S(1)}, bf16[384,5,3,64]{0,3,2,1:T(8,128)(2,1)S(1)}, f32[5,3,384]{2,1,0:T(4,128)S(1)}, ...), branch_computations={%region_26.27_spmd, %region_27.28_spmd} | conditional | flops 1919877120 | bytes 60263960 | solution.py:277
  386.3 5.5 fusion.66
  394.9 3.5 fusion.70
  401.5 5.7 conditional.17
  427.1 3.6 reshape.609
  430.7 3.6 fusion.159
  434.3 3.6 reshape.610
  443.8 36.5 %reduce-scatter.3.cloned.1.call-done = f32[384,320]{0,1:T(8,128)} async-done(((f32[1536,320]{0,1:T(8,128)}), f32[384,320]{0,1:T(8,128)}) %reduce-scatter.3.cloned.1.call-update) | async-done | bytes 491536 | tf_op jit(solution)/shard_map/reduce_scatter | solution.py:287
  484.8 26.2 %reduce-scatter.5.cloned.1.call-done = f32[384,320]{0,1:T(8,128)} async-done(((f32[1536,320]{0,1:T(8,128)}), f32[384,320]{0,1:T(8,128)}) %reduce-scatter.5.cloned.1.call-update) | async-done | bytes 491536 | tf_op jit(solution)/shard_map/reduce_scatter | solution.py:288
  532.4 165.6 %all-reduce.2.cloned.1.call-done = f32[3277824]{0:T(1024)} async-done(((f32[3277824]{0:T(1024)}), f32[3277824]{0:T(1024)}) %all-reduce.2.cloned.1.call-update) | async-done | bytes 13111312 | tf_op jit(solution)/shard_map/psum | solution.py:325
  698.0 9.4 %multiply_subtract_fusion = (f32[819456]{0:T(1024)}, f32[819456]{0:T(1024)}, f32[819456]{0:T(1024)}, f32[819456]{0:T(1024)}) fusion(f32[819456]{0:T(1024)} %param.27, s32[]{:T(128)S(6)} %mul.470, f32[3277824]{0:T(1024)} %all-reduce.2.cloned.1.call-done, s32[]{:T(128)S(6)} %select_n.58, f32[819456]{0:T(1024)} %param.28, f32[819456]{0:T(1024)} %param.29), kind=kLoop, calls=%fused_computation.115 | loop fusion | flops 15569664 | bytes 26222600 | tf_op jit(solution)/shard_map/sub | solution.py:335
  (188 shorter events, 114.1 us)
Async XLA Ops:
  7.2 21.8 %copy-start.47 = (s32[1,3]{1,0:T(1,128)S(1)}, s32[1,3]{1,0:T(1,128)}, u32[]{:S(2)}) copy-start(s32[1,3]{1,0:T(1,128)} %param.26) | copy-start | bytes 40
  7.2 26.5 %copy-start = (bf16[384,512]{1,0:T(8,128)(2,1)S(1)}, bf16[384,512]{1,0:T(8,128)(2,1)}, u32[]{:S(2)}) copy-start(bf16[384,512]{1,0:T(8,128)(2,1)} %param.24) | copy-start | bytes 1179652
  7.2 143.1 %all-gather.3.cloned.1.call-start = ((), (), s32[]{:S(2)}) async-start(), calls=%async_computation.5 | async-start | bytes 16389120 | tf_op jit(solution)/shard_map/all_gather | solution.py:90
  28.9 451.4 %reduce-scatter.3.cloned.1.call-start = ((), (), s32[]{:S(2)}) async-start(), calls=%async_computation.2 | async-start | bytes 2457600 | tf_op jit(solution)/shard_map/reduce_scatter | solution.py:287
  34.8 273.9 %copy-start.35 = (f32[384,32]{0,1:T(8,128)}, f32[384,32]{0,1:T(8,128)S(1)}, u32[]{:S(2)}) copy-start(f32[384,32]{0,1:T(8,128)S(1)} %get-tuple-element.323) | copy-start | bytes 147460
  292.1 16.6 %copy-start.18 = (bf16[512,320]{1,0:T(8,128)(2,1)}, bf16[512,320]{1,0:T(8,128)(2,1)S(1)}, u32[]{:S(2)}) copy-start(bf16[512,320]{1,0:T(8,128)(2,1)S(1)} %reshape.592) | copy-start | bytes 983044
  303.4 35.4 %copy-start.9 = (bf16[512,320]{0,1:T(8,128)(2,1)}, bf16[512,320]{0,1:T(8,128)(2,1)S(1)}, u32[]{:S(2)}) copy-start(bf16[512,320]{0,1:T(8,128)(2,1)S(1)} %get-tuple-element.310) | copy-start | bytes 983044
  303.4 44.8 %copy-start.7 = (bf16[512,320]{0,1:T(8,128)(2,1)}, bf16[512,320]{0,1:T(8,128)(2,1)S(1)}, u32[]{:S(2)}) copy-start(bf16[512,320]{0,1:T(8,128)(2,1)S(1)} %get-tuple-element.309) | copy-start | bytes 983044
  310.1 11.1 %copy-start.31 = (bf16[512,320]{1,0:T(8,128)(2,1)}, bf16[512,320]{1,0:T(8,128)(2,1)S(1)}, u32[]{:S(2)}) copy-start(bf16[512,320]{1,0:T(8,128)(2,1)S(1)} %reshape.597) | copy-start | bytes 983044
  322.4 15.5 %copy-start.20 = (pred[1,1,384,512]{2,3,1,0:T(8,128)(4,1)S(1)}, pred[1,1,384,512]{2,3,1,0:T(8,128)(4,1)}, u32[]{:S(2)}) copy-start(pred[1,1,384,512]{2,3,1,0:T(8,128)(4,1)} %get-tuple-element.320) | copy-start | bytes 589828
  338.8 9.4 %copy-start.43 = (f32[5,3,384]{2,1,0:T(4,128)}, f32[5,3,384]{2,1,0:T(4,128)S(1)}, u32[]{:S(2)}) copy-start(f32[5,3,384]{2,1,0:T(4,128)S(1)} %log_add_fusion) | copy-start | bytes 69124
  373.5 5.0 copy-start.14
  373.5 5.7 copy-start.3
  373.5 5.7 copy-start.12
  379.3 4.8 copy-start.10
  410.0 101.0 %reduce-scatter.5.cloned.1.call-start = ((), (), s32[]{:S(2)}) async-start(), calls=%async_computation.3 | async-start | bytes 2457600 | tf_op jit(solution)/shard_map/reduce_scatter | solution.py:288
  415.8 6.4 copy-start.2
  415.8 6.4 copy-start.24
  418.9 279.2 %all-reduce.2.cloned.1.call-start = ((), (), s32[]{:S(2)}) async-start(), calls=%async_computation.4 | async-start | bytes 26222592 | tf_op jit(solution)/shard_map/psum | solution.py:325
  419.2 5.5 copy-start.38
  430.7 7.2 %copy-start.34 = (bf16[384,512]{1,0:T(8,128)(2,1)S(1)}, bf16[384,512]{1,0:T(8,128)(2,1)}, u32[]{:S(2)}) copy-start(bf16[384,512]{1,0:T(8,128)(2,1)} %param.25) | copy-start | bytes 1179652
  440.1 43.2 %copy-start.19 = (bf16[512,320]{1,0:T(8,128)(2,1)S(1)}, bf16[512,320]{1,0:T(8,128)(2,1)}, u32[]{:S(2)}) copy-start(bf16[512,320]{1,0:T(8,128)(2,1)} %copy-done.18) | copy-start | bytes 983044
  512.9 6.0 copy-start.4
  512.9 7.7 %copy-start.5 = (f32[655360]{0:T(1024)S(1)}, f32[655360]{0:T(1024)}, u32[]{:S(2)}) copy-start(f32[655360]{0:T(1024)} %reshape.610) | copy-start | bytes 7864324
  (22 other events, 63.3 us)
Sparse Core Ops, SparseCore 0:
  29.0 121.2 all-gather.2
  410.1 70.1 reduce-scatter.2
  482.7 28.1 reduce-scatter.4
  527.4 170.6 all-reduce.1
where the time goes:
time: 725 us; the launch traced here: 714 us
  waiting for transfers between devices  343 us (47%)
  other arithmetic  159 us (22%)
  local copies, waits for them, and re-layouts  95.4 us (13%)
  matrix products  60.3 us (8%)
  blocking collectives  20.1 us (3%)
  loops' own time  18.4 us (3%)
  between operations  18.1 us (2%)
    psum x1, waiting for transfers between devices, body(): whole_sum = lax.psum(local_grads, ('wide', 'narrow'))  166 us
    all_gather x1, other arithmetic, body(): lax.all_gather(master.astype(jnp.bfloat16), 'narrow', axis=0, tiled=True)  124 us
    all_gather x1, waiting for transfers between devices, body(): lax.all_gather(master.astype(jnp.bfloat16), 'narrow', axis=0, tiled=True)  114 us
    unnamed x92, local copies, waits for them, and re-layouts  50.3 us
    reduce_scatter x1, waiting for transfers between devices, body(): lax.psum_scatter(key_sum_in, 'narrow', scatter_dimension=0, tiled=True)  36.5 us
    reduce_scatter x1, waiting for transfers between devices, body(): lax.psum_scatter(value_sum_in, 'narrow', scatter_dimension=0, tiled=True)  26.2 us
  transfers between devices with their start and end apart: 4, of which 4 were waited for; matrix products, arithmetic and copies ran while one was open for 6% of the time, Pallas kernels for 0%

commit v1 on v0

--- a/solution.py
+++ b/solution.py
@@ -87,7 +87,10 @@
     narrow_rank = lax.axis_index("narrow")
     group_width = QUERY_HEADS // KEYVAL_HEADS
     score_scale = HEAD_SIZE ** (-0.5)
-    replica = lax.all_gather(master.astype(jnp.bfloat16), "narrow", axis=0, tiled=True)
+    shard_len = master.shape[0]
+    replica = lax.all_gather(
+        master.astype(jnp.bfloat16).reshape(shard_len // 128, 128), "narrow", axis=0, tiled=False
+    ).reshape(-1)
     w_query, w_key, w_value, w_out, w_gate, w_up, w_down, gain_one, gain_two = unpack(replica)
     lengths_row = lengths[0]
     local_index = narrow_rank * token_rows + jnp.arange(token_rows, dtype=jnp.int32)
@@ -107,10 +110,11 @@
     query_batch = apply_rotary(query, token_position, QUERY_HEADS, 1.0).astype(jnp.bfloat16)
     key_batch = apply_rotary(key_projection, token_position, KEYVAL_HEADS, 1.0).astype(jnp.bfloat16)
     value_batch = value_proj.astype(jnp.bfloat16)
-    key_all, value_all = (
-        lax.all_gather(key_batch, "narrow", axis=0, tiled=True),
-        lax.all_gather(value_batch, "narrow", axis=0, tiled=True),
-    )
+    kv_width = KEYVAL_HEADS * HEAD_SIZE
+    kv_all = lax.all_gather(
+        jnp.concatenate([key_batch, value_batch], axis=1), "narrow", axis=0, tiled=True
+    )
+    key_all, value_all = kv_all[:, :kv_width], kv_all[:, kv_width:]
     query_tensor_split = query_batch.reshape(token_rows, KEYVAL_HEADS, group_width, HEAD_SIZE)
 
     def span_setup(span_start, key_source, value_source):
@@ -283,10 +287,10 @@
         )
     key_sum_in = jnp.concatenate(key_contributions, axis=0)
     value_sum_in = jnp.concatenate(value_contributions, axis=0)
-    key_gradient, value_gradient = (
-        lax.psum_scatter(key_sum_in, "narrow", scatter_dimension=0, tiled=True),
-        lax.psum_scatter(value_sum_in, "narrow", scatter_dimension=0, tiled=True),
-    )
+    kv_grad = lax.psum_scatter(
+        jnp.concatenate([key_sum_in, value_sum_in], axis=1), "narrow", scatter_dimension=0, tiled=True
+    )
+    key_gradient, value_gradient = kv_grad[:, :kv_width], kv_grad[:, kv_width:]
     d_query = query_gradient_running.reshape(token_rows, QUERY_HEADS * HEAD_SIZE)
     d_query_b = apply_rotary(d_query, token_position, QUERY_HEADS, -1.0).astype(jnp.bfloat16)
     key_gradient_batch = apply_rotary(key_gradient, token_position, KEYVAL_HEADS, -1.0).astype(
@@ -321,9 +325,10 @@
             g_gain_two,
         ]
     )
-    shard_len = master.shape[0]
-    whole_sum = lax.psum(local_grads, ("wide", "narrow"))
-    summed = lax.dynamic_slice_in_dim(whole_sum, narrow_rank * shard_len, shard_len)
+    narrow_sum = lax.psum_scatter(
+        local_grads.reshape(narrow_size, -1, 128), "narrow", scatter_dimension=0, tiled=True
+    )
+    summed = lax.psum(narrow_sum, "wide").reshape(-1)
     token_total = token_rows * narrow_size * lax.axis_size("wide")
     gradient = summed * (1.0 / math.sqrt(token_total))
     new_first = beta_one * first_moment + (1.0 - beta_one) * gradient

time: 725 us -> 812 us (1.12)
  waiting for transfers between devices: 343 us -> 608 us
  other arithmetic: 159 us -> 29.5 us
  blocking collectives: 20.1 us -> 0 us
  local copies, waits for them, and re-layouts: 95.4 us -> 84 us
  loops' own time: 18.4 us -> 8.05 us
    psum x1, waiting for transfers between devices: 166 us -> 362 us  [body(): summed = lax.psum(narrow_sum, 'wide').reshape(-1)]
    all_gather x1 -> x0, other arithmetic: 124 us -> none  [body(): lax.all_gather(master.astype(jnp.bfloat16), 'narrow', axis=0, tiled=True)]
    unnamed x4 -> x6, waiting for transfers between devices: 0.07 us -> 119 us
    all_gather x1 -> x2, waiting for transfers between devices: 114 us -> 67.7 us  [the longest x1 61.3 us: body(): lax.all_gather(master.astype(jnp.bfloat16).reshape(shard_len // 128, 128)...]
    unnamed x92 -> x90, local copies, waits for them, and re-layouts: 50.3 us -> 23.8 us
    all_gather x2 -> x0, blocking collectives: 20.1 us -> none  [the longest x1 10.4 us: body(): lax.all_gather(key_batch, 'narrow', axis=0, tiled=True)]
    reshape x0 -> x2, local copies, waits for them, and re-layouts: none -> 17.7 us  [the longest x1 10.3 us: body(): local_grads.reshape(narrow_size, -1, 128)]
    reduce_scatter x2 -> x1, waiting for transfers between devices: 62.6 us -> 59.2 us  [body(): lax.psum_scatter(jnp.concatenate([key_sum_in, value_sum_in], axis=1), 'na...]
  transfers between devices with their start and end apart: 4 -> 5, of which waited for: 4 -> 5; matrix products, arithmetic and copies ran while one was open for 6% -> 6% of each run, Pallas kernels for 0% -> 0%
where the time goes in v1:
time: 812 us; the launch traced here: 805 us
  waiting for transfers between devices  608 us (75%)
  local copies, waits for them, and re-layouts  84 us (10%)
  matrix products  52.2 us (6%)
  other arithmetic  29.5 us (4%)
  between operations  17.9 us (2%)
    psum x1, waiting for transfers between devices, body(): summed = lax.psum(narrow_sum, 'wide').reshape(-1)  362 us
    unnamed x6, waiting for transfers between devices  119 us
    all_gather x1, waiting for transfers between devices, body(): lax.all_gather(master.astype(jnp.bfloat16).reshape(shard_len // 128, 128)...  61.3 us
    reduce_scatter x1, waiting for transfers between devices, body(): lax.psum_scatter(jnp.concatenate([key_sum_in, value_sum_in], axis=1), 'na...  59.2 us
    unnamed x90, local copies, waits for them, and re-layouts  23.8 us
  transfers between devices with their start and end apart: 5, of which 5 were waited for; matrix products, arithmetic and copies ran while one was open for 6% of the time, Pallas kernels for 0%

profile of v1, /device:TPU:0, one launch (start us, length us, event | category | flops | bytes accessed | tf_op | source)
XLA Modules:
  0.0 805.3 jit_solution(4478773738985202452)
XLA Ops:
  7.2 3.3 convert_bitcast_fusion
  17.2 61.3 %all-gather.3.cloned.1.call-done = bf16[4,6402,128]{2,1,0:T(8,128)(2,1)} async-done(((bf16[1,6402,128]{2,1,0:T(8,128)(2,1)}), bf16[4,6402,128]{2,1,0:T(8,128)(2,1)}) %all-gather.3.cloned.1.call-update) | async-done | bytes 6555664 | tf_op jit(solution)/shard_map/all_gather | solution.py:91
  78.5 7.4 reshape.593
  98.1 3.8 reshape.603
  104.4 9.8 %slice.159 = bf16[6402,512]{1,0:T(8,128)(2,1)} reshape(bf16[4,6402,128]{2,1,0:T(8,128)(2,1)} %all-gather.3.cloned.1.call-done) | data formatting | bytes 13111296 | tf_op jit(solution)/shard_map/slice | solution.py:43
  115.3 6.4 all-gather.5.cloned.1.call-done
  124.1 6.0 conditional.9
  126.9 3.2 fusion.3
  133.7 5.2 conditional.12
  134.4 4.4 fusion.26
  142.8 3.6 multiply_convert_fusion
  148.3 3.0 convolution_convert_fusion
  154.7 14.2 %conditional.15 = (f32[384,5,3,64]{0,3,2,1:T(8,128)S(1)}, f32[512,320]{0,1:T(8,128)S(1)}, f32[512,320]{0,1:T(8,128)S(1)}) conditional(s32[]{:T(128)} %bitcast.87, () %tuple.100, (pred[1,1,384,512]{2,3,1,0:T(8,128)(4,1)S(1)}, bf16[512,5,64]{0,2,1:T(8,128)(2,1)S(1)}, bf16[384,5,3,64]{0,3,2,1:T(8,128)(2,1)S(1)}, f32[5,3,384]{2,1,0:T(4,128)S(1)}, ...), branch_computations={%region_26.27_spmd, %region_27.28_spmd} | conditional | flops 1919877120 | bytes 61574708 | solution.py:281
  156.7 5.5 fusion.66
  165.3 3.6 fusion.70
  172.1 5.1 conditional.17
  177.2 3.9 maximum_maximum_fusion
  181.1 5.6 reduce-scatter.8.cloned.1.call-start
  191.0 3.4 copy.123
  208.4 59.2 %reduce-scatter.6.cloned.1.call-done = f32[384,640]{0,1:T(8,128)} async-done(((f32[1536,640]{0,1:T(8,128)}), f32[384,640]{0,1:T(8,128)}) %reduce-scatter.6.cloned.1.call-update) | async-done | bytes 983056 | tf_op jit(solution)/shard_map/reduce_scatter | solution.py:290
  294.1 10.3 %reshape.614 = f32[4,6402,128]{2,1,0:T(8,128)} reshape(f32[3277824]{0:T(1024)} %constant_dynamic-update-slice_fusion) | data formatting | bytes 26222592 | tf_op jit(solution)/shard_map/reshape | solution.py:329
  304.6 118.8 %reduce-scatter.8.cloned.1.call-done = f32[1,6402,128]{2,1,0:T(8,128)} async-done(((f32[4,6402,128]{2,1,0:T(8,128)}), f32[1,6402,128]{2,1,0:T(8,128)}) %reduce-scatter.8.cloned.1.call-update) | async-done | bytes 3277840
  427.5 362.0 %all-reduce.3.cloned.1.call-done = f32[1,6402,128]{2,1,0:T(8,128)} async-done(((f32[1,6402,128]{2,1,0:T(8,128)}), f32[1,6402,128]{2,1,0:T(8,128)}) %all-reduce.3.cloned.1.call-update) | async-done | bytes 3277840 | tf_op jit(solution)/shard_map/psum | solution.py:331
  789.4 9.2 %multiply_subtract_fusion = (f32[819456]{0:T(1024)}, f32[819456]{0:T(1024)}, f32[819456]{0:T(1024)}, f32[819456]{0:T(1024)}) fusion(f32[819456]{0:T(1024)} %param.27, s32[]{:T(128)S(6)} %mul.492, f32[1,6402,128]{2,1,0:T(8,128)} %all-reduce.3.cloned.1.call-done, f32[819456]{0:T(1024)} %param.28, f32[819456]{0:T(1024)} %param.29), kind=kLoop, calls=%fused_computation.119 | loop fusion | flops 15569664 | bytes 26222596 | tf_op jit(solution)/shard_map/sub | solution.py:340
  (190 shorter events, 95.4 us)
Async XLA Ops:
  7.2 8.2 %copy-start = (bf16[384,512]{1,0:T(8,128)(2,1)S(1)}, bf16[384,512]{1,0:T(8,128)(2,1)}, u32[]{:S(2)}) copy-start(bf16[384,512]{1,0:T(8,128)(2,1)} %param.24) | copy-start | bytes 1179652
  7.2 71.3 %all-gather.3.cloned.1.call-start = ((), (), s32[]{:S(2)}) async-start(), calls=%async_computation.2 | async-start | bytes 8202240 | tf_op jit(solution)/shard_map/all_gather | solution.py:91
  10.6 111.1 %all-gather.5.cloned.1.call-start = ((), (), s32[]{:S(2)}) async-start(), calls=%async_computation.3 | async-start | bytes 2457600 | tf_op jit(solution)/shard_map/all_gather | solution.py:114
  15.6 98.6 %copy-start.41 = (f32[384]{0:T(512)}, f32[384]{0:T(512)S(1)}, u32[]{:S(2)}) copy-start(f32[384]{0:T(512)S(1)} %add_rsqrt_fusion.1) | copy-start | bytes 4612
  17.2 121.7 %copy-start.21 = (pred[1,1,384,512]{2,3,1,0:T(8,128)(4,1)}, pred[1,1,384,512]{2,3,1,0:T(8,128)(4,1)S(1)}, u32[]{:S(2)}) copy-start(pred[1,1,384,512]{2,3,1,0:T(8,128)(4,1)S(1)} %get-tuple-element.315) | copy-start | bytes 589828
  88.3 25.8 %copy-start.43 = (f32[512]{0:T(512)}, f32[512]{0:T(512)S(1)}, u32[]{:S(2)}) copy-start(f32[512]{0:T(512)S(1)} %get-tuple-element.292) | copy-start | bytes 6148
  91.7 175.9 %reduce-scatter.6.cloned.1.call-start = ((), (), s32[]{:S(2)}) async-start(), calls=%async_computation.4 | async-start | bytes 4915200 | tf_op jit(solution)/shard_map/reduce_scatter | solution.py:290
  114.1 10.0 %copy-start.25 = (pred[1,1,384,512]{2,3,1,0:T(8,128)(4,1)S(1)}, pred[1,1,384,512]{2,3,1,0:T(8,128)(4,1)}, u32[]{:S(2)}) copy-start(pred[1,1,384,512]{2,3,1,0:T(8,128)(4,1)} %get-tuple-element.316) | copy-start | bytes 589828
  124.1 9.5 %copy-start.9 = (bf16[512,320]{0,1:T(8,128)(2,1)}, bf16[512,320]{0,1:T(8,128)(2,1)S(1)}, u32[]{:S(2)}) copy-start(bf16[512,320]{0,1:T(8,128)(2,1)S(1)} %get-tuple-element.303) | copy-start | bytes 983044
  124.1 14.7 %copy-start.7 = (bf16[512,320]{0,1:T(8,128)(2,1)}, bf16[512,320]{0,1:T(8,128)(2,1)S(1)}, u32[]{:S(2)}) copy-start(bf16[512,320]{0,1:T(8,128)(2,1)S(1)} %get-tuple-element.302) | copy-start | bytes 983044
  141.2 6.8 copy-start.13
  148.0 6.7 copy-start.10
  148.0 6.7 copy-start.26
  148.0 6.7 copy-start.46
  148.3 6.4 copy-start.1
  177.2 10.7 %copy-start.42 = (f32[384]{0:T(512)S(1)}, f32[384]{0:T(512)}, u32[]{:S(2)}) copy-start(f32[384]{0:T(512)} %copy-done.41) | copy-start | bytes 4612
  177.2 10.7 %copy-start.44 = (f32[512]{0:T(512)S(1)}, f32[512]{0:T(512)}, u32[]{:S(2)}) copy-start(f32[512]{0:T(512)} %copy-done.43) | copy-start | bytes 6148
  181.1 242.3 %reduce-scatter.8.cloned.1.call-start = ((), (), s32[]{:S(2)}) async-start(), calls=%async_computation.6 | async-start | bytes 16404480
  206.3 63.9 %copy-start.19 = (bf16[512,320]{1,0:T(8,128)(2,1)S(1)}, bf16[512,320]{1,0:T(8,128)(2,1)}, u32[]{:S(2)}) copy-start(bf16[512,320]{1,0:T(8,128)(2,1)} %copy-done.18) | copy-start | bytes 983044
  271.5 14.5 %copy-start.4 = (f32[655360]{0:T(1024)S(1)}, f32[655360]{0:T(1024)}, u32[]{:S(2)}) copy-start(f32[655360]{0:T(1024)} %reshape.611) | copy-start | bytes 7864324
  278.9 8.8 %copy-start.5 = (f32[655360]{0:T(1024)S(1)}, f32[655360]{0:T(1024)}, u32[]{:S(2)}) copy-start(f32[655360]{0:T(1024)} %reshape.612) | copy-start | bytes 7864324
  304.5 119.0 %copy-start.14 = (f32[384,512]{1,0:T(8,128)S(1)}, f32[384,512]{1,0:T(8,128)}, u32[]{:S(2)}) copy-start(f32[384,512]{1,0:T(8,128)} %copy-done.13) | copy-start | bytes 2359300
  304.5 122.0 %copy-start.2 = (f32[384,512]{1,0:T(8,128)S(1)}, f32[384,512]{1,0:T(8,128)}, u32[]{:S(2)}) copy-start(f32[384,512]{1,0:T(8,128)} %copy-done.1) | copy-start | bytes 2359300
  304.5 484.9 %all-reduce.3.cloned.1.call-start = ((), (), s32[]{:S(2)}) async-start(), calls=%async_computation.5 | async-start | bytes 6561792 | tf_op jit(solution)/shard_map/psum | solution.py:331
  (25 other events, 71.4 us)
Sparse Core Ops, SparseCore 0:
  10.7 67.8 all-gather.2
  91.8 29.7 all-gather.4
  181.2 86.2 reduce-scatter.5
  304.6 118.7 reduce-scatter.7
  425.9 363.4 all-reduce.2

commit v2 on v1

--- a/solution.py
+++ b/solution.py
@@ -325,10 +325,8 @@
             g_gain_two,
         ]
     )
-    narrow_sum = lax.psum_scatter(
-        local_grads.reshape(narrow_size, -1, 128), "narrow", scatter_dimension=0, tiled=True
-    )
-    summed = lax.psum(narrow_sum, "wide").reshape(-1)
+    whole_sum = lax.psum(local_grads, ("wide", "narrow"))
+    summed = lax.dynamic_slice_in_dim(whole_sum, narrow_rank * shard_len, shard_len)
     token_total = token_rows * narrow_size * lax.axis_size("wide")
     gradient = summed * (1.0 / math.sqrt(token_total))
     new_first = beta_one * first_moment + (1.0 - beta_one) * gradient

time: 812 us -> 487 us (0.60)
  waiting for transfers between devices: 608 us -> 288 us
    psum x1, waiting for transfers between devices: 362 us -> 166 us  [body(): whole_sum = lax.psum(local_grads, ('wide', 'narrow'))]
    unnamed x6 -> x4, waiting for transfers between devices: 119 us -> 0.07 us
    reshape x1 -> x0, local copies, waits for them, and re-layouts: 10.3 us -> none  [body(): local_grads.reshape(narrow_size, -1, 128)]
    unnamed x90 -> x94, local copies, waits for them, and re-layouts: 23.8 us -> 23.7 us
  transfers between devices with their start and end apart: 5 -> 4, of which waited for: 5 -> 4; matrix products, arithmetic and copies ran while one was open for 6% -> 13% of each run, Pallas kernels for 0% -> 0%
where the time goes in v2:
time: 487 us; the launch traced here: 479 us
  waiting for transfers between devices  288 us (59%)
  local copies, waits for them, and re-layouts  79.3 us (16%)
  matrix products  56 us (11%)
  other arithmetic  29.9 us (6%)
  between operations  17.9 us (4%)
  loops' own time  7.87 us (2%)
    psum x1, waiting for transfers between devices, body(): whole_sum = lax.psum(local_grads, ('wide', 'narrow'))  166 us
    all_gather x1, waiting for transfers between devices, body(): lax.all_gather(master.astype(jnp.bfloat16).reshape(shard_len // 128, 128)...  60.7 us
    reduce_scatter x1, waiting for transfers between devices, body(): lax.psum_scatter(jnp.concatenate([key_sum_in, value_sum_in], axis=1), 'na...  55.1 us
    unnamed x94, local copies, waits for them, and re-layouts  23.7 us
    slice x5, local copies, waits for them, and re-layouts, unpack(): pieces.append(flat[offset:offset + length].reshape(layout))  13.9 us
  transfers between devices with their start and end apart: 4, of which 4 were waited for; matrix products, arithmetic and copies ran while one was open for 13% of the time, Pallas kernels for 0%

profile of v2, /device:TPU:0, one launch (start us, length us, event | category | flops | bytes accessed | tf_op | source)
XLA Modules:
  0.0 479.4 jit_solution(1539119901445350074)
XLA Ops:
  7.2 3.3 convert_bitcast_fusion
  17.8 60.7 %all-gather.3.cloned.1.call-done = bf16[4,6402,128]{2,1,0:T(8,128)(2,1)} async-done(((bf16[1,6402,128]{2,1,0:T(8,128)(2,1)}), bf16[4,6402,128]{2,1,0:T(8,128)(2,1)}) %all-gather.3.cloned.1.call-update) | async-done | bytes 6555664 | tf_op jit(solution)/shard_map/all_gather | solution.py:91
  78.5 7.3 %reshape.583 = bf16[3277824]{0:T(1024)(128)(2,1)} reshape(bf16[4,6402,128]{2,1,0:T(8,128)(2,1)} %all-gather.3.cloned.1.call-done) | data formatting | bytes 13111296 | tf_op jit(solution)/shard_map/reshape | solution.py:93
  97.5 3.8 reshape.593
  103.7 9.8 %slice.159 = bf16[6402,512]{1,0:T(8,128)(2,1)} reshape(bf16[4,6402,128]{2,1,0:T(8,128)(2,1)} %all-gather.3.cloned.1.call-done) | data formatting | bytes 13111296 | tf_op jit(solution)/shard_map/slice | solution.py:43
  114.6 5.9 %all-gather.5.cloned.1.call-done = bf16[1536,640]{0,1:T(8,128)(2,1)} async-done(((bf16[384,640]{0,1:T(8,128)(2,1)}), bf16[1536,640]{0,1:T(8,128)(2,1)}) %all-gather.5.cloned.1.call-update) | async-done | bytes 1966096 | tf_op jit(solution)/shard_map/all_gather | solution.py:114
  123.0 5.9 %conditional.9 = (f32[5,3,384]{2,1,0:T(4,128)}, f32[5,3,384]{2,1,0:T(4,128)S(1)}) conditional(s32[]{:T(128)} %bitcast.87, () %tuple.93, (pred[1,1,384,512]{2,3,1,0:T(8,128)(4,1)S(1)}, bf16[512,5,64]{0,2,1:T(8,128)(2,1)S(1)}, bf16[384,5,3,64]{0,3,2,1:T(8,128)(2,1)S(1)}) %tuple.204), branch_computations={%region_5.6_spmd, %region_6.9_spmd} | conditional | flops 398148480 | bytes 25235472 | solution.py:161
  131.7 5.2 %conditional.12 = (f32[384,5,3,64]{0,3,2,1:T(8,128)S(1)}) conditional(s32[]{:T(128)} %bitcast.87, () %tuple.92, (pred[1,1,384,512]{2,3,1,0:T(8,128)(4,1)S(1)}, bf16[512,5,64]{0,2,1:T(8,128)(2,1)S(1)}, bf16[384,5,3,64]{0,3,2,1:T(8,128)(2,1)S(1)}, f32[5,3,384]{2,1,0:T(4,128)S(1)}, bf16[512,5,64]{0,2,1:T(8,128)(2,1)}) %tuple.211), branch_computations={%region_17.18_spmd, %region_18.19_spmd} | conditional | flops 766771200 | bytes 5184064 | solution.py:186
  132.6 4.4 fusion.26
  141.2 3.6 multiply_convert_fusion
  153.7 14.4 %conditional.15 = (f32[384,5,3,64]{0,3,2,1:T(8,128)S(1)}, f32[512,320]{0,1:T(8,128)S(1)}, f32[512,320]{0,1:T(8,128)S(1)}) conditional(s32[]{:T(128)} %bitcast.87, () %tuple.100, (pred[1,1,384,512]{2,3,1,0:T(8,128)(4,1)S(1)}, bf16[512,5,64]{0,2,1:T(8,128)(2,1)S(1)}, bf16[384,5,3,64]{0,3,2,1:T(8,128)(2,1)S(1)}, f32[5,3,384]{2,1,0:T(4,128)S(1)}, ...), branch_computations={%region_26.27_spmd, %region_27.28_spmd} | conditional | flops 1919877120 | bytes 61574708 | solution.py:281
  155.9 5.5 %fusion.66 = bf16[5,3,384,512]{2,3,1,0:T(8,128)(2,1)S(1)} fusion(f32[5,512,384,3]{2,1,3,0:T(8,128)S(1)} %fusion.75, f32[5,3,384]{2,1,0:T(4,128)} %get-tuple-element.179, f32[5,3,384]{2,1,0:T(4,128)S(1)} %get-tuple-element.176, pred[384,512]{0,1:T(8,128)(4,1)S(1)} %bitcast.402, bf16[384,5,3,64]{0,3,2,1:T(8,128)(2,1)} %get-tuple-element.178, ...), kind=kOutput, calls=%fused_computation.67 | convolution fusion | flops 398131200 | bytes 19002368 | tf_op jit(solution)/shard_map/cond/branch_1_fun/qgrd,kgd->grqk/dot_general | solution.py:254
  164.5 3.6 fusion.70
  171.1 5.6 %conditional.17 = (f32[384,5,3,64]{0,3,2,1:T(8,128)S(1)}, f32[512,320]{0,1:T(8,128)S(1)}, f32[512,320]{0,1:T(8,128)S(1)}) conditional(s32[]{:T(128)} %bitcast.85, f32[384,5,3,64]{0,3,2,1:T(8,128)S(1)} %get-tuple-element.224, (pred[1,1,384,512]{2,3,1,0:T(8,128)(4,1)S(1)}, bf16[512,5,64]{0,2,1:T(8,128)(2,1)S(1)}, ...), branch_computations={%region_30.31_spmd, %region_31.32_spmd} | conditional | flops 1920245760 | bytes 63141456 | solution.py:281
  176.7 3.9 maximum_maximum_fusion
  183.3 5.1 %reshape.597 = f32[491520]{0:T(1024)} reshape(f32[512,960]{1,0:T(8,128)} %fusion.140) | data formatting | bytes 3932160 | tf_op jit(solution)/shard_map/reshape | solution.py:317
  188.4 3.4 copy.123
  191.8 3.6 fusion.159
  195.4 3.6 reshape.601
  201.4 3.7 reshape.602
  211.1 55.1 %reduce-scatter.2.cloned.1.call-done = f32[384,640]{0,1:T(8,128)} async-done(((f32[1536,640]{0,1:T(8,128)}), f32[384,640]{0,1:T(8,128)}) %reduce-scatter.2.cloned.1.call-update) | async-done | bytes 983056 | tf_op jit(solution)/shard_map/reduce_scatter | solution.py:290
  282.0 3.5 constant_dynamic-update-slice_fusion.4
  297.2 165.9 %all-reduce.2.cloned.1.call-done = f32[3277824]{0:T(1024)} async-done(((f32[3277824]{0:T(1024)}), f32[3277824]{0:T(1024)}) %all-reduce.2.cloned.1.call-update) | async-done | bytes 13111312 | tf_op jit(solution)/shard_map/psum | solution.py:328
  463.1 9.4 %multiply_subtract_fusion = (f32[819456]{0:T(1024)}, f32[819456]{0:T(1024)}, f32[819456]{0:T(1024)}, f32[819456]{0:T(1024)}) fusion(f32[819456]{0:T(1024)} %param.27, s32[]{:T(128)S(6)} %mul.470, f32[3277824]{0:T(1024)} %all-reduce.2.cloned.1.call-done, s32[]{:T(128)S(6)} %select_n.58, f32[819456]{0:T(1024)} %param.28, f32[819456]{0:T(1024)} %param.29), kind=kLoop, calls=%fused_computation.116 | loop fusion | flops 15569664 | bytes 26222600 | tf_op jit(solution)/shard_map/sub | solution.py:338
  (190 shorter events, 90.9 us)
Async XLA Ops:
  7.2 8.2 %copy-start = (bf16[384,512]{1,0:T(8,128)(2,1)S(1)}, bf16[384,512]{1,0:T(8,128)(2,1)}, u32[]{:S(2)}) copy-start(bf16[384,512]{1,0:T(8,128)(2,1)} %param.24) | copy-start | bytes 1179652
  7.2 71.3 %all-gather.3.cloned.1.call-start = ((), (), s32[]{:S(2)}) async-start(), calls=%async_computation.1 | async-start | bytes 8202240 | tf_op jit(solution)/shard_map/all_gather | solution.py:91
  10.6 110.0 %all-gather.5.cloned.1.call-start = ((), (), s32[]{:S(2)}) async-start(), calls=%async_computation.2 | async-start | bytes 2457600 | tf_op jit(solution)/shard_map/all_gather | solution.py:114
  16.4 97.9 %copy-start.38 = (f32[384,32]{0,1:T(8,128)}, f32[384,32]{0,1:T(8,128)S(1)}, u32[]{:S(2)}) copy-start(f32[384,32]{0,1:T(8,128)S(1)} %get-tuple-element.320) | copy-start | bytes 147460
  88.4 5.8 %copy-start.19 = (bf16[512,320]{1,0:T(8,128)(2,1)}, bf16[512,320]{1,0:T(8,128)(2,1)S(1)}, u32[]{:S(2)}) copy-start(bf16[512,320]{1,0:T(8,128)(2,1)S(1)} %reshape.584) | copy-start | bytes 983044
  90.7 175.6 %reduce-scatter.2.cloned.1.call-start = ((), (), s32[]{:S(2)}) async-start(), calls=%async_computation.3 | async-start | bytes 4915200 | tf_op jit(solution)/shard_map/reduce_scatter | solution.py:290
  113.5 9.5 %copy-start.25 = (pred[1,1,384,512]{2,3,1,0:T(8,128)(4,1)S(1)}, pred[1,1,384,512]{2,3,1,0:T(8,128)(4,1)}, u32[]{:S(2)}) copy-start(pred[1,1,384,512]{2,3,1,0:T(8,128)(4,1)} %get-tuple-element.316) | copy-start | bytes 589828
  123.0 8.7 %copy-start.8 = (bf16[512,320]{0,1:T(8,128)(2,1)}, bf16[512,320]{0,1:T(8,128)(2,1)S(1)}, u32[]{:S(2)}) copy-start(bf16[512,320]{0,1:T(8,128)(2,1)S(1)} %get-tuple-element.303) | copy-start | bytes 983044
  123.0 13.9 %copy-start.6 = (bf16[512,320]{0,1:T(8,128)(2,1)}, bf16[512,320]{0,1:T(8,128)(2,1)S(1)}, u32[]{:S(2)}) copy-start(bf16[512,320]{0,1:T(8,128)(2,1)S(1)} %get-tuple-element.302) | copy-start | bytes 983044
  123.0 6.0 %copy-start.23 = (pred[1,1,384,512]{2,3,1,0:T(8,128)(4,1)S(1)}, pred[1,1,384,512]{2,3,1,0:T(8,128)(4,1)}, u32[]{:S(2)}) copy-start(pred[1,1,384,512]{2,3,1,0:T(8,128)(4,1)} %get-tuple-element.317) | copy-start | bytes 589828
  131.7 5.2 %copy-start.46 = (f32[5,3,384]{2,1,0:T(4,128)}, f32[5,3,384]{2,1,0:T(4,128)S(1)}, u32[]{:S(2)}) copy-start(f32[5,3,384]{2,1,0:T(4,128)S(1)} %log_add_fusion) | copy-start | bytes 69124
  139.6 6.8 %copy-start.13 = (f32[384,512]{1,0:T(8,128)}, f32[384,512]{1,0:T(8,128)S(1)}, u32[]{:S(2)}) copy-start(f32[384,512]{1,0:T(8,128)S(1)} %get-tuple-element.324) | copy-start | bytes 2359300
  146.4 7.3 %copy-start.9 = (bf16[512,320]{0,1:T(8,128)(2,1)S(1)}, bf16[512,320]{0,1:T(8,128)(2,1)}, u32[]{:S(2)}) copy-start(bf16[512,320]{0,1:T(8,128)(2,1)} %copy-done.8) | copy-start | bytes 983044
  146.4 7.3 %copy-start.26 = (pred[1,1,384,512]{2,3,1,0:T(8,128)(4,1)S(1)}, pred[1,1,384,512]{2,3,1,0:T(8,128)(4,1)}, u32[]{:S(2)}) copy-start(pred[1,1,384,512]{2,3,1,0:T(8,128)(4,1)} %get-tuple-element.316) | copy-start | bytes 589828
  146.4 7.3 %copy-start.47 = (f32[5,3,384]{2,1,0:T(4,128)S(1)}, f32[5,3,384]{2,1,0:T(4,128)}, u32[]{:S(2)}) copy-start(f32[5,3,384]{2,1,0:T(4,128)} %copy-done.46) | copy-start | bytes 69124
  146.7 7.0 %copy-start.1 = (f32[384,512]{1,0:T(8,128)}, f32[384,512]{1,0:T(8,128)S(1)}, u32[]{:S(2)}) copy-start(f32[384,512]{1,0:T(8,128)S(1)} %multiply_add_fusion.5) | copy-start | bytes 2359300
  180.7 282.4 %all-reduce.2.cloned.1.call-start = ((), (), s32[]{:S(2)}) async-start(), calls=%async_computation.4 | async-start | bytes 26222592 | tf_op jit(solution)/shard_map/psum | solution.py:328
  181.1 14.4 %copy-start.28 = (bf16[384,15,64]{0,2,1:T(8,128)(2,1)}, bf16[384,15,64]{0,2,1:T(8,128)(2,1)S(1)}, u32[]{:S(2)}) copy-start(bf16[384,15,64]{0,2,1:T(8,128)(2,1)S(1)} %maximum_convert_fusion) | copy-start | bytes 2211844
  191.8 7.2 %copy-start.18 = (bf16[384,1280]{1,0:T(8,128)(2,1)S(1)}, bf16[384,1280]{1,0:T(8,128)(2,1)}, u32[]{:S(2)}) copy-start(bf16[384,1280]{1,0:T(8,128)(2,1)} %copy-done.17) | copy-start | bytes 2949124
  199.0 6.0 %copy-start.37 = (bf16[384,512]{1,0:T(8,128)(2,1)S(1)}, bf16[384,512]{1,0:T(8,128)(2,1)}, u32[]{:S(2)}) copy-start(bf16[384,512]{1,0:T(8,128)(2,1)} %param.25) | copy-start | bytes 1179652
  208.2 60.7 %copy-start.20 = (bf16[512,320]{1,0:T(8,128)(2,1)S(1)}, bf16[512,320]{1,0:T(8,128)(2,1)}, u32[]{:S(2)}) copy-start(bf16[512,320]{1,0:T(8,128)(2,1)} %copy-done.19) | copy-start | bytes 983044
  267.3 13.4 %copy-start.11 = (f32[120,4,8,128]{3,1,2,0:T(4,128)S(1)}, f32[120,4,8,128]{3,1,2,0:T(4,128)}, u32[]{:S(2)}) copy-start(f32[120,4,8,128]{3,1,2,0:T(4,128)} %copy.123) | copy-start | bytes 5898244
  277.6 8.0 %copy-start.4 = (f32[655360]{0:T(1024)S(1)}, f32[655360]{0:T(1024)}, u32[]{:S(2)}) copy-start(f32[655360]{0:T(1024)} %reshape.602) | copy-start | bytes 7864324
  282.0 5.2 %copy-start.5 = (f32[160,4,8,128]{3,1,2,0:T(4,128)S(1)}, f32[160,4,8,128]{3,1,2,0:T(4,128)}, u32[]{:S(2)}) copy-start(f32[160,4,8,128]{3,1,2,0:T(4,128)} %copy.124) | copy-start | bytes 7864324
  (26 other events, 72.8 us)
Sparse Core Ops, SparseCore 0:
  10.7 67.8 all-gather.2
  90.8 29.7 all-gather.4
  180.8 85.3 reduce-scatter.1
  292.2 170.8 all-reduce.1

commit v3 on v2

--- a/solution.py
+++ b/solution.py
@@ -213,6 +213,11 @@
     )
     d_mixed_b = d_mixed.astype(jnp.bfloat16)
     g_out = jnp.dot(attention_output.T, d_mixed_b, preferred_element_type=jnp.float32)
+    early_grads = jnp.concatenate(
+        [g_out.reshape(-1), g_gate.reshape(-1), g_up.reshape(-1), g_down.reshape(-1), g_gain_two]
+    )
+    early_grads, d_mixed_b = lax.optimization_barrier((early_grads, d_mixed_b))
+    early_sum = lax.psum(early_grads, ("wide", "narrow"))
     attention_output_gradient = jnp.dot(
         d_mixed_b, w_out.T, preferred_element_type=jnp.float32
     ).astype(jnp.bfloat16)
@@ -287,9 +292,17 @@
         )
     key_sum_in = jnp.concatenate(key_contributions, axis=0)
     value_sum_in = jnp.concatenate(value_contributions, axis=0)
-    kv_grad = lax.psum_scatter(
-        jnp.concatenate([key_sum_in, value_sum_in], axis=1), "narrow", scatter_dimension=0, tiled=True
-    )
+    kv_sum_in = jnp.concatenate([key_sum_in, value_sum_in], axis=1).reshape(
+        narrow_size, token_rows, 2 * kv_width
+    )
+    kv_grad = kv_sum_in[narrow_rank]
+    for shift in range(1, narrow_size):
+        sender_block = kv_sum_in[lax.rem(narrow_rank + narrow_size - shift, narrow_size)]
+        kv_grad = kv_grad + lax.ppermute(
+            sender_block,
+            "narrow",
+            [(source, source - shift) for source in range(shift, narrow_size)],
+        )
     key_gradient, value_gradient = kv_grad[:, :kv_width], kv_grad[:, kv_width:]
     d_query = query_gradient_running.reshape(token_rows, QUERY_HEADS * HEAD_SIZE)
     d_query_b = apply_rotary(d_query, token_position, QUERY_HEADS, -1.0).astype(jnp.bfloat16)
@@ -312,20 +325,21 @@
         + inverse_one
         * (dn_one - normed_one * jnp.mean(dn_one * normed_one, axis=-1, keepdims=True))
     ).astype(jnp.bfloat16)
-    local_grads = jnp.concatenate(
+    late_grads = jnp.concatenate(
+        [g_query.reshape(-1), g_key.reshape(-1), g_value.reshape(-1), g_gain_one]
+    )
+    late_grads, early_sum = lax.optimization_barrier((late_grads, early_sum))
+    late_sum = lax.psum(late_grads, ("wide", "narrow"))
+    late_split = late_grads.shape[0] - MODEL_WIDTH
+    early_split = early_grads.shape[0] - MODEL_WIDTH
+    whole_sum = jnp.concatenate(
         [
-            g_query.reshape(-1),
-            g_key.reshape(-1),
-            g_value.reshape(-1),
-            g_out.reshape(-1),
-            g_gate.reshape(-1),
-            g_up.reshape(-1),
-            g_down.reshape(-1),
-            g_gain_one,
-            g_gain_two,
+            late_sum[:late_split],
+            early_sum[:early_split],
+            late_sum[late_split:],
+            early_sum[early_split:],
         ]
     )
-    whole_sum = lax.psum(local_grads, ("wide", "narrow"))
     summed = lax.dynamic_slice_in_dim(whole_sum, narrow_rank * shard_len, shard_len)
     token_total = token_rows * narrow_size * lax.axis_size("wide")
     gradient = summed * (1.0 / math.sqrt(token_total))

time: 487 us -> 639 us (1.31)
  waiting for transfers between devices: 288 us -> 408 us
  local copies, waits for them, and re-layouts: 79.3 us -> 95.6 us
  loops' own time: 7.87 us -> 16.6 us
  other arithmetic: 29.9 us -> 37.8 us
    psum x1 -> x2, waiting for transfers between devices: 166 us -> 289 us  [the longest x1 145 us: body(): early_sum = lax.psum(early_grads, ('wide', 'narrow'))]
    reduce_scatter x1 -> x0, waiting for transfers between devices: 55.1 us -> none  [body(): lax.psum_scatter(jnp.concatenate([key_sum_in, value_sum_in], axis=1), 'na...]
    ppermute x0 -> x3, waiting for transfers between devices: none -> 52.3 us  [body(): lax.ppermute(sender_block, 'narrow', [(source, source - shift) for source...]
    dynamic_slice x0 -> x1, local copies, waits for them, and re-layouts: none -> 10.9 us  [body(): kv_grad = kv_sum_in[narrow_rank]]
    slice x0 -> x6, local copies, waits for them, and re-layouts: none -> 10.8 us  [the longest x1 8.46 us: body(): early_sum[:early_split]]
    unnamed x94 -> x71, local copies, waits for them, and re-layouts: 23.7 us -> 16.9 us
  transfers between devices with their start and end apart: 4 -> 7, of which waited for: 4 -> 6; matrix products, arithmetic and copies ran while one was open for 13% -> 10% of each run, Pallas kernels for 0% -> 0%
where the time goes in v3:
time: 639 us; the launch traced here: 633 us
  waiting for transfers between devices  408 us (64%)
  local copies, waits for them, and re-layouts  95.6 us (15%)
  matrix products  52.4 us (8%)
  other arithmetic  37.8 us (6%)
  between operations  18 us (3%)
  loops' own time  16.6 us (3%)
    psum x1, waiting for transfers between devices, body(): early_sum = lax.psum(early_grads, ('wide', 'narrow'))  145 us
    psum x1, waiting for transfers between devices, body(): late_sum = lax.psum(late_grads, ('wide', 'narrow'))  143 us
    all_gather x1, waiting for transfers between devices, body(): lax.all_gather(master.astype(jnp.bfloat16).reshape(shard_len // 128, 128)...  60.7 us
    ppermute x3, waiting for transfers between devices, body(): lax.ppermute(sender_block, 'narrow', [(source, source - shift) for source...  52.3 us
    unnamed x71, local copies, waits for them, and re-layouts  16.9 us
    slice x5, local copies, waits for them, and re-layouts, unpack(): pieces.append(flat[offset:offset + length].reshape(layout))  13.9 us
  transfers between devices with their start and end apart: 7, of which 6 were waited for; matrix products, arithmetic and copies ran while one was open for 10% of the time, Pallas kernels for 0%

profile of v3, /device:TPU:0, one launch (start us, length us, event | category | flops | bytes accessed | tf_op | source)
XLA Modules:
  0.0 633.2 jit_solution(14551768688576539909)
XLA Ops:
  17.8 60.7 %all-gather.3.cloned.1.call-done = bf16[4,6402,128]{2,1,0:T(8,128)(2,1)} async-done(((bf16[1,6402,128]{2,1,0:T(8,128)(2,1)}), bf16[4,6402,128]{2,1,0:T(8,128)(2,1)}) %all-gather.3.cloned.1.call-update) | async-done | bytes 6555664 | tf_op jit(solution)/shard_map/all_gather | solution.py:91
  78.5 7.3 %reshape.586 = bf16[3277824]{0:T(1024)(128)(2,1)} reshape(bf16[4,6402,128]{2,1,0:T(8,128)(2,1)} %all-gather.3.cloned.1.call-done) | data formatting | bytes 13111296 | tf_op jit(solution)/shard_map/reshape | solution.py:93
  97.7 3.8 reshape.596
  103.9 9.8 %slice.171 = bf16[6402,512]{1,0:T(8,128)(2,1)} reshape(bf16[4,6402,128]{2,1,0:T(8,128)(2,1)} %all-gather.3.cloned.1.call-done) | data formatting | bytes 13111296 | tf_op jit(solution)/shard_map/slice | solution.py:43
  114.8 6.2 all-gather.5.cloned.1.call-done
  123.6 6.3 conditional.9
  132.5 5.2 conditional.12
  133.4 4.4 fusion.26
  144.6 3.6 multiply_convert_fusion
  158.7 3.6 reshape.599
  162.3 3.6 reshape.600
  178.7 15.5 %conditional.15 = (f32[384,5,3,64]{0,3,2,1:T(8,128)S(1)}, f32[512,320]{0,1:T(8,128)S(1)}, f32[512,320]{0,1:T(8,128)S(1)}) conditional(s32[]{:T(128)} %bitcast.87, () %tuple.102, (pred[1,1,384,512]{2,3,1,0:T(8,128)(4,1)}, bf16[512,5,64]{0,2,1:T(8,128)(2,1)}, bf16[384,5,3,64]{0,3,2,1:T(8,128)(2,1)S(1)}, f32[5,3,384]{2,1,0:T(4,128)S(1)}, ...), branch_computations={%region_27.28_spmd, %region_28.29_spmd} | conditional | flops 1919877120 | bytes 63671916 | solution.py:286
  181.9 5.6 fusion.66
  190.6 3.6 fusion.70
  197.2 10.6 %conditional.17 = (f32[384,5,3,64]{0,3,2,1:T(8,128)S(1)}, f32[512,320]{0,1:T(8,128)S(1)}, f32[512,320]{0,1:T(8,128)S(1)}) conditional(s32[]{:T(128)} %bitcast.85, f32[384,5,3,64]{0,3,2,1:T(8,128)S(1)} %get-tuple-element.229, (pred[1,1,384,512]{2,3,1,0:T(8,128)(4,1)}, bf16[512,5,64]{0,2,1:T(8,128)(2,1)}, bf16[384,5,3,64]{0,3,2,1:T(8,128)(2,1)S(1)}, ...), branch_computations={%region_31.32_spmd, %region_32.33_spmd} | conditional | flops 1920245760 | bytes 65146476 | solution.py:286
  207.8 3.9 maximum_maximum_fusion
  211.7 5.2 reshape.603
  216.9 10.9 %constant_dynamic-slice_fusion.2 = (f32[1,384,640]{1,0,2:T(1,128)}, f32[1,384,640]{1,0,2:T(1,128)S(1)}, f32[1,384,640]{1,0,2:T(1,128)S(1)}, f32[1,384,640]{1,0,2:T(1,128)S(1)}) fusion(f32[4,384,640]{1,0,2:T(4,128)} %reshape.603, s32[]{:T(128)S(6)} %select_n.70, s32[]{:T(128)S(6)} %select_n.73, s32[]{:T(128)S(6)} %select_n.72, s32[]{:T(128)S(6)} %select_n.71), kind=kLoop, calls=%fused_computation.225 | loop fusion | bytes 7864336 | tf_op jit(solution)/shard_map/dynamic_slice | solution.py:298
  242.1 45.2 %collective-permute-done.2 = f32[384,640]{0,1:T(8,128)} collective-permute-done((f32[384,640]{0,1:T(8,128)}, f32[384,640]{0,1:T(8,128)}, u32[]{:S(2)}, u32[]{:S(2)}) %collective-permute-start.2) | collective-permute-done | bytes 983072 | tf_op jit(solution)/shard_map/ppermute | solution.py:301
  287.2 7.2 %collective-permute-done.1 = f32[384,640]{0,1:T(8,128)} collective-permute-done((f32[384,640]{0,1:T(8,128)}, f32[384,640]{0,1:T(8,128)}, u32[]{:S(2)}, u32[]{:S(2)}) %collective-permute-start.1) | collective-permute-done | bytes 983072 | tf_op jit(solution)/shard_map/ppermute | solution.py:301
  309.4 145.4 %all-reduce.3.cloned.1.call-done = f32[2458112]{0:T(1024)} async-done(((f32[2458112]{0:T(1024)}), f32[2458112]{0:T(1024)}) %all-reduce.3.cloned.1.call-update) | async-done | bytes 9832464 | tf_op jit(solution)/shard_map/psum | solution.py:220
  459.0 8.5 %slice.184 = f32[2457600]{0:T(1024)} slice(f32[2458112]{0:T(1024)} %all-reduce.3.cloned.1.call-done), slice={[0:2457600]} | slice | bytes 19660800 | tf_op jit(solution)/shard_map/slice | solution.py:338
  467.5 143.4 %all-reduce.5.cloned.1.call-done = f32[819712]{0:T(1024)} async-done(((f32[819712]{0:T(1024)}), f32[819712]{0:T(1024)}) %all-reduce.5.cloned.1.call-update) | async-done | bytes 3278864 | tf_op jit(solution)/shard_map/psum | solution.py:332
  613.8 12.6 %multiply_subtract_fusion = (f32[819456]{0:T(1024)}, f32[819456]{0:T(1024)}, f32[819456]{0:T(1024)}, f32[819456]{0:T(1024)}) fusion(f32[819456]{0:T(1024)S(1)} %copy-done.1, s32[]{:T(128)S(6)} %mul.470, f32[819456]{0:T(1024)} %param.28, f32[819456]{0:T(1024)} %param.29, s32[]{:T(128)S(6)} %select_n.74, f32[512]{0:T(512)S(1)} %slice-done.1, ...), kind=kLoop, calls=%fused_computation.124 | loop fusion | flops 18028032 | bytes 36056072 | tf_op jit(solution)/shard_map/sub | solution.py:352
  (187 shorter events, 110.3 us)
Async XLA Ops:
  7.2 8.2 %copy-start = (bf16[384,512]{1,0:T(8,128)(2,1)S(1)}, bf16[384,512]{1,0:T(8,128)(2,1)}, u32[]{:S(2)}) copy-start(bf16[384,512]{1,0:T(8,128)(2,1)} %param.24) | copy-start | bytes 1179652
  7.2 71.3 %all-gather.3.cloned.1.call-start = ((), (), s32[]{:S(2)}) async-start(), calls=%async_computation | async-start | bytes 8202240 | tf_op jit(solution)/shard_map/all_gather | solution.py:91
  10.6 110.5 %all-gather.5.cloned.1.call-start = ((), (), s32[]{:S(2)}) async-start(), calls=%async_computation.1 | async-start | bytes 2457600 | tf_op jit(solution)/shard_map/all_gather | solution.py:114
  17.8 120.0 %copy-start.23 = (pred[1,1,384,512]{2,3,1,0:T(8,128)(4,1)}, pred[1,1,384,512]{2,3,1,0:T(8,128)(4,1)S(1)}, u32[]{:S(2)}) copy-start(pred[1,1,384,512]{2,3,1,0:T(8,128)(4,1)S(1)} %get-tuple-element.327) | copy-start | bytes 589828
  91.1 363.7 %all-reduce.3.cloned.1.call-start = ((), (), s32[]{:S(2)}) async-start(), calls=%async_computation.2 | async-start | bytes 19668992 | tf_op jit(solution)/shard_map/psum | solution.py:220
  113.7 9.8 %copy-start.27 = (pred[1,1,384,512]{2,3,1,0:T(8,128)(4,1)S(1)}, pred[1,1,384,512]{2,3,1,0:T(8,128)(4,1)}, u32[]{:S(2)}) copy-start(pred[1,1,384,512]{2,3,1,0:T(8,128)(4,1)} %get-tuple-element.328) | copy-start | bytes 589828
  123.5 9.0 %copy-start.9 = (bf16[512,320]{0,1:T(8,128)(2,1)}, bf16[512,320]{0,1:T(8,128)(2,1)S(1)}, u32[]{:S(2)}) copy-start(bf16[512,320]{0,1:T(8,128)(2,1)S(1)} %get-tuple-element.315) | copy-start | bytes 983044
  123.5 14.2 %copy-start.7 = (bf16[512,320]{0,1:T(8,128)(2,1)}, bf16[512,320]{0,1:T(8,128)(2,1)S(1)}, u32[]{:S(2)}) copy-start(bf16[512,320]{0,1:T(8,128)(2,1)S(1)} %get-tuple-element.314) | copy-start | bytes 983044
  123.5 14.2 %copy-start.5 = (bf16[512,320]{0,1:T(8,128)(2,1)}, bf16[512,320]{0,1:T(8,128)(2,1)S(1)}, u32[]{:S(2)}) copy-start(bf16[512,320]{0,1:T(8,128)(2,1)S(1)} %get-tuple-element.313) | copy-start | bytes 983044
  123.5 6.3 copy-start.25
  181.9 5.6 copy-start.11
  216.9 17.8 %copy-start.37 = (f32[384,32]{0,1:T(8,128)S(1)}, f32[384,32]{0,1:T(8,128)}, u32[]{:S(2)}) copy-start(f32[384,32]{0,1:T(8,128)} %get-tuple-element.330) | copy-start | bytes 147460
  228.8 58.4 %collective-permute-start.2 = (f32[384,640]{0,1:T(8,128)}, f32[384,640]{0,1:T(8,128)}, u32[]{:S(2)}, u32[]{:S(2)}) collective-permute-start(f32[384,640]{0,1:T(8,128)} %bitcast.381), channel_id=1, source_target_pairs={{3,0},{7,4},{11,8},{15,12},{19,16},{23,20},{27,24},{31,28},{35,32}... | collective-permute-start | bytes 2949128 | tf_op jit(solution)/shard_map/ppermute | solution.py:301
  231.1 63.3 %collective-permute-start.1 = (f32[384,640]{0,1:T(8,128)}, f32[384,640]{0,1:T(8,128)}, u32[]{:S(2)}, u32[]{:S(2)}) collective-permute-start(f32[384,640]{0,1:T(8,128)} %bitcast.382), channel_id=1, source_target_pairs={{2,0},{3,1},{6,4},{7,5},{10,8},{11,9},{14,12},{15,13},{18,16},{19,... | collective-permute-start | bytes 2949128 | tf_op jit(solution)/shard_map/ppermute | solution.py:301
  233.4 61.0 %collective-permute-start = (f32[384,640]{0,1:T(8,128)}, f32[384,640]{0,1:T(8,128)}, u32[]{:S(2)}, u32[]{:S(2)}) collective-permute-start(f32[384,640]{0,1:T(8,128)} %bitcast.383), channel_id=1, source_target_pairs={{1,0},{2,1},{3,2},{5,4},{6,5},{7,6},{9,8},{10,9},{11,10},{13,12},{... | collective-permute-start | bytes 2949128 | tf_op jit(solution)/shard_map/ppermute | solution.py:301
  239.0 55.4 %copy-start.17 = (f32[1,384,640]{1,0,2:T(1,128)S(1)}, f32[1,384,640]{1,0,2:T(1,128)}, u32[]{:S(2)}) copy-start(f32[1,384,640]{1,0,2:T(1,128)} %get-tuple-element.303) | copy-start | bytes 2949124
  239.1 371.8 %all-reduce.5.cloned.1.call-start = ((), (), s32[]{:S(2)}) async-start(), calls=%async_computation.3 | async-start | bytes 6561792 | tf_op jit(solution)/shard_map/psum | solution.py:332
  240.3 59.2 %copy-start.19 = (bf16[512,320]{1,0:T(8,128)(2,1)S(1)}, bf16[512,320]{1,0:T(8,128)(2,1)}, u32[]{:S(2)}) copy-start(bf16[512,320]{1,0:T(8,128)(2,1)} %copy-done.18) | copy-start | bytes 983044
  294.4 5.5 copy-start.36
  296.5 9.6 %copy-start.12 = (f32[491520]{0:T(1024)S(1)}, f32[491520]{0:T(1024)}, u32[]{:S(2)}) copy-start(f32[491520]{0:T(1024)} %reshape.605) | copy-start | bytes 5898244
  309.3 148.5 %copy-start.14 = (f32[384,512]{1,0:T(8,128)S(1)}, f32[384,512]{1,0:T(8,128)}, u32[]{:S(2)}) copy-start(f32[384,512]{1,0:T(8,128)} %copy-done.13) | copy-start | bytes 2359300
  309.3 148.5 %copy-start.21 = (bf16[384,512]{1,0:T(8,128)(2,1)S(1)}, bf16[384,512]{1,0:T(8,128)(2,1)}, u32[]{:S(2)}) copy-start(bf16[384,512]{1,0:T(8,128)(2,1)} %param.25) | copy-start | bytes 1179652
  309.4 148.5 %copy-start.22 = (f32[384,512]{1,0:T(8,128)S(1)}, f32[384,512]{1,0:T(8,128)}, u32[]{:S(2)}) copy-start(f32[384,512]{1,0:T(8,128)} %get-tuple-element.338) | copy-start | bytes 2359300
  467.5 145.7 %slice-start.1 = ((f32[2458112]{0:T(1024)}), f32[512]{0:T(512)S(1)}, s32[]{:S(2)}) async-start(f32[2458112]{0:T(1024)} %all-reduce.3.cloned.1.call-done), calls=%async_computation.5 | async-start | bytes 4096 | tf_op jit(solution)/shard_map/slice | solution.py:340
  (22 other events, 43.5 us)
Sparse Core Ops, SparseCore 0:
  10.7 67.8 all-gather.2
  91.2 29.7 all-gather.4
  239.2 215.5 all-reduce.2
  460.1 150.7 all-reduce.4

commit v4 on v2

--- a/solution.py
+++ b/solution.py
@@ -287,9 +287,17 @@
         )
     key_sum_in = jnp.concatenate(key_contributions, axis=0)
     value_sum_in = jnp.concatenate(value_contributions, axis=0)
-    kv_grad = lax.psum_scatter(
-        jnp.concatenate([key_sum_in, value_sum_in], axis=1), "narrow", scatter_dimension=0, tiled=True
-    )
+    kv_sum_in = jnp.concatenate([key_sum_in, value_sum_in], axis=1).reshape(
+        narrow_size, token_rows, 2 * kv_width
+    )
+    kv_grad = kv_sum_in[narrow_rank]
+    for shift in range(1, narrow_size):
+        sender_block = kv_sum_in[lax.rem(narrow_rank + narrow_size - shift, narrow_size)]
+        kv_grad = kv_grad + lax.ppermute(
+            sender_block,
+            "narrow",
+            [(source, source - shift) for source in range(shift, narrow_size)],
+        )
     key_gradient, value_gradient = kv_grad[:, :kv_width], kv_grad[:, kv_width:]
     d_query = query_gradient_running.reshape(token_rows, QUERY_HEADS * HEAD_SIZE)
     d_query_b = apply_rotary(d_query, token_position, QUERY_HEADS, -1.0).astype(jnp.bfloat16)

time: 487 us -> 508 us (1.043)
  local copies, waits for them, and re-layouts: 79.3 us -> 93.1 us
    reduce_scatter x1 -> x0, waiting for transfers between devices: 55.1 us -> none  [body(): lax.psum_scatter(jnp.concatenate([key_sum_in, value_sum_in], axis=1), 'na...]
    psum x1, waiting for transfers between devices: 166 us -> 203 us  [body(): whole_sum = lax.psum(local_grads, ('wide', 'narrow'))]
    ppermute x0 -> x3, waiting for transfers between devices: none -> 20.1 us  [body(): lax.ppermute(sender_block, 'narrow', [(source, source - shift) for source...]
    dynamic_slice x0 -> x1, local copies, waits for them, and re-layouts: none -> 10.9 us  [body(): kv_grad = kv_sum_in[narrow_rank]]
    reshape x0 -> x1, local copies, waits for them, and re-layouts: none -> 5.25 us  [body(): jnp.concatenate([key_sum_in, value_sum_in], axis=1)]
    unnamed x94 -> x95, local copies, waits for them, and re-layouts: 23.7 us -> 28.3 us
  transfers between devices with their start and end apart: 4 -> 6, of which waited for: 4 -> 5; matrix products, arithmetic and copies ran while one was open for 13% -> 11% of each run, Pallas kernels for 0% -> 0%
where the time goes in v4:
time: 508 us; the launch traced here: 502 us
  waiting for transfers between devices  291 us (57%)
  local copies, waits for them, and re-layouts  93.1 us (18%)
  matrix products  51.6 us (10%)
  other arithmetic  31.8 us (6%)
  between operations  17.9 us (4%)
  loops' own time  12.5 us (2%)
    psum x1, waiting for transfers between devices, body(): whole_sum = lax.psum(local_grads, ('wide', 'narrow'))  203 us
    all_gather x1, waiting for transfers between devices, body(): lax.all_gather(master.astype(jnp.bfloat16).reshape(shard_len // 128, 128)...  61.3 us
    unnamed x95, local copies, waits for them, and re-layouts  28.3 us
    ppermute x3, waiting for transfers between devices, body(): lax.ppermute(sender_block, 'narrow', [(source, source - shift) for source...  20.1 us
    slice x5, local copies, waits for them, and re-layouts, unpack(): pieces.append(flat[offset:offset + length].reshape(layout))  13.8 us
    dynamic_slice x1, local copies, waits for them, and re-layouts, body(): kv_grad = kv_sum_in[narrow_rank]  10.9 us
  transfers between devices with their start and end apart: 6, of which 5 were waited for; matrix products, arithmetic and copies ran while one was open for 11% of the time, Pallas kernels for 0%

profile of v4, /device:TPU:0, one launch (start us, length us, event | category | flops | bytes accessed | tf_op | source)
XLA Modules:
  0.0 501.9 jit_solution(4180616306139066854)
XLA Ops:
  7.2 3.3 convert_bitcast_fusion
  17.2 61.3 %all-gather.3.cloned.1.call-done = bf16[4,6402,128]{2,1,0:T(8,128)(2,1)} async-done(((bf16[1,6402,128]{2,1,0:T(8,128)(2,1)}), bf16[4,6402,128]{2,1,0:T(8,128)(2,1)}) %all-gather.3.cloned.1.call-update) | async-done | bytes 6555664 | tf_op jit(solution)/shard_map/all_gather | solution.py:91
  78.5 7.4 %reshape.586 = bf16[3277824]{0:T(1024)(128)(2,1)} reshape(bf16[4,6402,128]{2,1,0:T(8,128)(2,1)} %all-gather.3.cloned.1.call-done) | data formatting | bytes 13111296 | tf_op jit(solution)/shard_map/reshape | solution.py:93
  98.1 3.8 reshape.596
  104.3 9.8 %slice.159 = bf16[6402,512]{1,0:T(8,128)(2,1)} reshape(bf16[4,6402,128]{2,1,0:T(8,128)(2,1)} %all-gather.3.cloned.1.call-done) | data formatting | bytes 13111296 | tf_op jit(solution)/shard_map/slice | solution.py:43
  115.2 6.4 %all-gather.5.cloned.1.call-done = bf16[1536,640]{0,1:T(8,128)(2,1)} async-done(((bf16[384,640]{0,1:T(8,128)(2,1)}), bf16[1536,640]{0,1:T(8,128)(2,1)}) %all-gather.5.cloned.1.call-update) | async-done | bytes 1966096 | tf_op jit(solution)/shard_map/all_gather | solution.py:114
  124.1 6.0 %conditional.9 = (f32[5,3,384]{2,1,0:T(4,128)}, f32[5,3,384]{2,1,0:T(4,128)S(1)}) conditional(s32[]{:T(128)} %bitcast.87, () %tuple.93, (pred[1,1,384,512]{2,3,1,0:T(8,128)(4,1)S(1)}, bf16[512,5,64]{0,2,1:T(8,128)(2,1)S(1)}, bf16[384,5,3,64]{0,3,2,1:T(8,128)(2,1)S(1)}) %tuple.203), branch_computations={%region_5.6_spmd, %region_6.9_spmd} | conditional | flops 398148480 | bytes 25235472 | solution.py:161
  126.9 3.2 fusion.3
  133.6 5.2 %conditional.12 = (f32[384,5,3,64]{0,3,2,1:T(8,128)S(1)}) conditional(s32[]{:T(128)} %bitcast.87, () %tuple.92, (pred[1,1,384,512]{2,3,1,0:T(8,128)(4,1)S(1)}, bf16[512,5,64]{0,2,1:T(8,128)(2,1)S(1)}, bf16[384,5,3,64]{0,3,2,1:T(8,128)(2,1)S(1)}, f32[5,3,384]{2,1,0:T(4,128)}, bf16[512,5,64]{0,2,1:T(8,128)(2,1)}) %tuple.210), branch_computations={%region_17.18_spmd, %region_18.19_spmd} | conditional | flops 766771200 | bytes 5184064 | solution.py:186
  134.4 4.4 fusion.26
  143.0 3.6 multiply_convert_fusion
  150.9 3.0 convolution_convert_fusion
  155.3 14.1 %conditional.15 = (f32[384,5,3,64]{0,3,2,1:T(8,128)S(1)}, f32[512,320]{0,1:T(8,128)S(1)}, f32[512,320]{0,1:T(8,128)S(1)}) conditional(s32[]{:T(128)} %bitcast.87, () %tuple.100, (pred[1,1,384,512]{2,3,1,0:T(8,128)(4,1)S(1)}, bf16[512,5,64]{0,2,1:T(8,128)(2,1)S(1)}, bf16[384,5,3,64]{0,3,2,1:T(8,128)(2,1)S(1)}, f32[5,3,384]{2,1,0:T(4,128)S(1)}, ...), branch_computations={%region_26.27_spmd, %region_27.28_spmd} | conditional | flops 1919877120 | bytes 60263960 | solution.py:281
  157.3 5.5 %fusion.66 = bf16[5,3,384,512]{2,3,1,0:T(8,128)(2,1)S(1)} fusion(f32[5,512,384,3]{2,1,3,0:T(8,128)S(1)} %fusion.75, f32[5,3,384]{2,1,0:T(4,128)S(1)} %get-tuple-element.179, f32[5,3,384]{2,1,0:T(4,128)S(1)} %get-tuple-element.176, pred[384,512]{0,1:T(8,128)(4,1)S(1)} %bitcast.419, bf16[384,5,3,64]{0,3,2,1:T(8,128)(2,1)} %get-tuple-element.178, ...), kind=kOutput, calls=%fused_computation.67 | convolution fusion | flops 398131200 | bytes 19002368 | tf_op jit(solution)/shard_map/cond/branch_1_fun/qgrd,kgd->grqk/dot_general | solution.py:254
  165.9 3.6 fusion.70
  172.6 9.6 %conditional.17 = (f32[384,5,3,64]{0,3,2,1:T(8,128)S(1)}, f32[512,320]{0,1:T(8,128)S(1)}, f32[512,320]{0,1:T(8,128)S(1)}) conditional(s32[]{:T(128)} %bitcast.85, f32[384,5,3,64]{0,3,2,1:T(8,128)S(1)} %get-tuple-element.224, (pred[1,1,384,512]{2,3,1,0:T(8,128)(4,1)}, bf16[512,5,64]{0,2,1:T(8,128)(2,1)S(1)}, bf16[384,5,3,64]{0,3,2,1:T(8,128)(2,1)S(1)}, ...), branch_computations={%region_30.31_spmd, %region_31.32_spmd} | conditional | flops 1920245760 | bytes 63835728 | solution.py:281
  182.2 3.9 maximum_maximum_fusion
  186.1 5.2 %reshape.599 = f32[4,384,640]{1,0,2:T(4,128)} reshape(f32[1536,640]{0,1:T(8,128)} %maximum_maximum_fusion) | data formatting | bytes 7864320 | tf_op jit(solution)/shard_map/reshape | solution.py:290
  191.3 10.9 %constant_dynamic-slice_fusion.2 = (f32[1,384,640]{1,0,2:T(1,128)}, f32[1,384,640]{1,0,2:T(1,128)S(1)}, f32[1,384,640]{1,0,2:T(1,128)S(1)}, f32[1,384,640]{1,0,2:T(1,128)S(1)}) fusion(f32[4,384,640]{1,0,2:T(4,128)} %reshape.599, s32[]{:T(128)S(6)} %select_n.70, s32[]{:T(128)S(6)} %select_n.73, s32[]{:T(128)S(6)} %select_n.72, s32[]{:T(128)S(6)} %select_n.71), kind=kLoop, calls=%fused_computation.223 | loop fusion | bytes 7864336 | tf_op jit(solution)/shard_map/dynamic_slice | solution.py:293
  213.6 3.1 constant_dynamic-update-slice_fusion.8
  231.1 14.4 %collective-permute-done.2 = f32[384,640]{0,1:T(8,128)} collective-permute-done((f32[384,640]{0,1:T(8,128)}, f32[384,640]{0,1:T(8,128)}, u32[]{:S(2)}, u32[]{:S(2)}) %collective-permute-start.2) | collective-permute-done | bytes 983072 | tf_op jit(solution)/shard_map/ppermute | solution.py:296
  245.5 5.7 %collective-permute-done.1 = f32[384,640]{0,1:T(8,128)} collective-permute-done((f32[384,640]{0,1:T(8,128)}, f32[384,640]{0,1:T(8,128)}, u32[]{:S(2)}, u32[]{:S(2)}) %collective-permute-start.1) | collective-permute-done | bytes 983072 | tf_op jit(solution)/shard_map/ppermute | solution.py:296
  282.9 202.8 %all-reduce.2.cloned.1.call-done = f32[3277824]{0:T(1024)} async-done(((f32[3277824]{0:T(1024)}), f32[3277824]{0:T(1024)}) %all-reduce.2.cloned.1.call-update) | async-done | bytes 13111312 | tf_op jit(solution)/shard_map/psum | solution.py:336
  485.7 9.4 %multiply_subtract_fusion = (f32[819456]{0:T(1024)}, f32[819456]{0:T(1024)}, f32[819456]{0:T(1024)}, f32[819456]{0:T(1024)}) fusion(f32[819456]{0:T(1024)} %param.27, s32[]{:T(128)S(6)} %mul.470, f32[3277824]{0:T(1024)} %all-reduce.2.cloned.1.call-done, s32[]{:T(128)S(6)} %select_n.74, f32[819456]{0:T(1024)} %param.28, f32[819456]{0:T(1024)} %param.29), kind=kLoop, calls=%fused_computation.116 | loop fusion | flops 15569664 | bytes 26222600 | tf_op jit(solution)/shard_map/sub | solution.py:346
  (195 shorter events, 104.4 us)
Async XLA Ops:
  7.2 8.2 %copy-start = (bf16[384,512]{1,0:T(8,128)(2,1)S(1)}, bf16[384,512]{1,0:T(8,128)(2,1)}, u32[]{:S(2)}) copy-start(bf16[384,512]{1,0:T(8,128)(2,1)} %param.24) | copy-start | bytes 1179652
  7.2 71.3 %all-gather.3.cloned.1.call-start = ((), (), s32[]{:S(2)}) async-start(), calls=%async_computation | async-start | bytes 8202240 | tf_op jit(solution)/shard_map/all_gather | solution.py:91
  10.6 111.0 %all-gather.5.cloned.1.call-start = ((), (), s32[]{:S(2)}) async-start(), calls=%async_computation.1 | async-start | bytes 2457600 | tf_op jit(solution)/shard_map/all_gather | solution.py:114
  15.6 98.5 %copy-start.41 = (f32[384]{0:T(512)}, f32[384]{0:T(512)S(1)}, u32[]{:S(2)}) copy-start(f32[384]{0:T(512)S(1)} %add_rsqrt_fusion.1) | copy-start | bytes 4612
  17.2 121.6 %copy-start.22 = (pred[1,1,384,512]{2,3,1,0:T(8,128)(4,1)}, pred[1,1,384,512]{2,3,1,0:T(8,128)(4,1)S(1)}, u32[]{:S(2)}) copy-start(pred[1,1,384,512]{2,3,1,0:T(8,128)(4,1)S(1)} %get-tuple-element.319) | copy-start | bytes 589828
  88.3 25.8 %copy-start.43 = (f32[512]{0:T(512)}, f32[512]{0:T(512)S(1)}, u32[]{:S(2)}) copy-start(f32[512]{0:T(512)S(1)} %get-tuple-element.292) | copy-start | bytes 6148
  91.6 394.1 %all-reduce.2.cloned.1.call-start = ((), (), s32[]{:S(2)}) async-start(), calls=%async_computation.2 | async-start | bytes 26222592 | tf_op jit(solution)/shard_map/psum | solution.py:336
  114.1 10.0 %copy-start.26 = (pred[1,1,384,512]{2,3,1,0:T(8,128)(4,1)S(1)}, pred[1,1,384,512]{2,3,1,0:T(8,128)(4,1)}, u32[]{:S(2)}) copy-start(pred[1,1,384,512]{2,3,1,0:T(8,128)(4,1)} %get-tuple-element.320) | copy-start | bytes 589828
  124.1 9.5 %copy-start.10 = (bf16[512,320]{0,1:T(8,128)(2,1)}, bf16[512,320]{0,1:T(8,128)(2,1)S(1)}, u32[]{:S(2)}) copy-start(bf16[512,320]{0,1:T(8,128)(2,1)S(1)} %get-tuple-element.307) | copy-start | bytes 983044
  124.1 14.7 %copy-start.8 = (bf16[512,320]{0,1:T(8,128)(2,1)}, bf16[512,320]{0,1:T(8,128)(2,1)S(1)}, u32[]{:S(2)}) copy-start(bf16[512,320]{0,1:T(8,128)(2,1)S(1)} %get-tuple-element.306) | copy-start | bytes 983044
  124.1 6.0 %copy-start.24 = (pred[1,1,384,512]{2,3,1,0:T(8,128)(4,1)S(1)}, pred[1,1,384,512]{2,3,1,0:T(8,128)(4,1)}, u32[]{:S(2)}) copy-start(pred[1,1,384,512]{2,3,1,0:T(8,128)(4,1)} %get-tuple-element.321) | copy-start | bytes 589828
  141.4 9.2 %copy-start.13 = (f32[384,512]{1,0:T(8,128)}, f32[384,512]{1,0:T(8,128)S(1)}, u32[]{:S(2)}) copy-start(f32[384,512]{1,0:T(8,128)S(1)} %get-tuple-element.328) | copy-start | bytes 2359300
  149.7 5.6 %copy-start.27 = (pred[1,1,384,512]{2,3,1,0:T(8,128)(4,1)S(1)}, pred[1,1,384,512]{2,3,1,0:T(8,128)(4,1)}, u32[]{:S(2)}) copy-start(pred[1,1,384,512]{2,3,1,0:T(8,128)(4,1)} %get-tuple-element.320) | copy-start | bytes 589828
  149.7 5.6 %copy-start.46 = (f32[5,3,384]{2,1,0:T(4,128)S(1)}, f32[5,3,384]{2,1,0:T(4,128)}, u32[]{:S(2)}) copy-start(f32[5,3,384]{2,1,0:T(4,128)} %log_add_fusion) | copy-start | bytes 69124
  202.2 8.3 %copy-start.42 = (f32[384]{0:T(512)S(1)}, f32[384]{0:T(512)}, u32[]{:S(2)}) copy-start(f32[384]{0:T(512)} %copy-done.41) | copy-start | bytes 4612
  202.2 8.3 %copy-start.44 = (f32[512]{0:T(512)S(1)}, f32[512]{0:T(512)}, u32[]{:S(2)}) copy-start(f32[512]{0:T(512)} %copy-done.43) | copy-start | bytes 6148
  203.2 42.3 %collective-permute-start.2 = (f32[384,640]{0,1:T(8,128)}, f32[384,640]{0,1:T(8,128)}, u32[]{:S(2)}, u32[]{:S(2)}) collective-permute-start(f32[384,640]{0,1:T(8,128)} %bitcast.379), channel_id=1, source_target_pairs={{3,0},{7,4},{11,8},{15,12},{19,16},{23,20},{27,24},{31,28},{35,32}... | collective-permute-start | bytes 2949128 | tf_op jit(solution)/shard_map/ppermute | solution.py:296
  205.6 45.7 %collective-permute-start.1 = (f32[384,640]{0,1:T(8,128)}, f32[384,640]{0,1:T(8,128)}, u32[]{:S(2)}, u32[]{:S(2)}) collective-permute-start(f32[384,640]{0,1:T(8,128)} %bitcast.380), channel_id=1, source_target_pairs={{2,0},{3,1},{6,4},{7,5},{10,8},{11,9},{14,12},{15,13},{18,16},{19,... | collective-permute-start | bytes 2949128 | tf_op jit(solution)/shard_map/ppermute | solution.py:296
  207.9 43.4 %collective-permute-start = (f32[384,640]{0,1:T(8,128)}, f32[384,640]{0,1:T(8,128)}, u32[]{:S(2)}, u32[]{:S(2)}) collective-permute-start(f32[384,640]{0,1:T(8,128)} %bitcast.381), channel_id=1, source_target_pairs={{1,0},{2,1},{3,2},{5,4},{6,5},{7,6},{9,8},{10,9},{11,10},{13,12},{... | collective-permute-start | bytes 2949128 | tf_op jit(solution)/shard_map/ppermute | solution.py:296
  213.6 7.0 %copy-start.1 = (f32[512,1280]{1,0:T(8,128)S(1)}, f32[512,1280]{1,0:T(8,128)}, u32[]{:S(2)}) copy-start(f32[512,1280]{1,0:T(8,128)} %fusion.161) | copy-start | bytes 7864324
  226.0 25.2 %copy-start.17 = (f32[1,384,640]{1,0,2:T(1,128)S(1)}, f32[1,384,640]{1,0,2:T(1,128)}, u32[]{:S(2)}) copy-start(f32[1,384,640]{1,0,2:T(1,128)} %get-tuple-element.295) | copy-start | bytes 2949124
  230.5 25.8 %copy-start.20 = (bf16[512,320]{1,0:T(8,128)(2,1)S(1)}, bf16[512,320]{1,0:T(8,128)(2,1)}, u32[]{:S(2)}) copy-start(bf16[512,320]{1,0:T(8,128)(2,1)} %copy-done.19) | copy-start | bytes 983044
  256.8 13.2 %copy-start.5 = (f32[655360]{0:T(1024)S(1)}, f32[655360]{0:T(1024)}, u32[]{:S(2)}) copy-start(f32[655360]{0:T(1024)} %reshape.605) | copy-start | bytes 7864324
  262.9 8.8 %copy-start.6 = (f32[655360]{0:T(1024)S(1)}, f32[655360]{0:T(1024)}, u32[]{:S(2)}) copy-start(f32[655360]{0:T(1024)} %reshape.606) | copy-start | bytes 7864324
  (26 other events, 76.0 us)
Sparse Core Ops, SparseCore 0:
  10.7 67.8 all-gather.2
  91.8 29.7 all-gather.4
  277.9 207.7 all-reduce.1

commit v5 on v4

--- a/solution.py
+++ b/solution.py
@@ -3,6 +3,8 @@
 import jax
 import jax.numpy as jnp
 from jax import lax
+from jax.experimental import pallas as pl
+from jax.experimental.pallas import tpu as pltpu
 from jax.sharding import PartitionSpec as P
 
 MODEL_WIDTH = 512
@@ -76,6 +78,64 @@
     return turned.reshape(values.shape)
 
 
+def gather_kernel(src_ref, out_ref, send_sems, recv_sems):
+    narrow = lax.axis_index("narrow")
+    wide = lax.axis_index("wide")
+    z_lo = narrow // 2
+    core = narrow % 2
+    z_hi = (wide // 4) % 2
+    flipped = wide + 4 - 8 * z_hi
+    half = src_ref.shape[0] // 2
+    sibling = (wide, z_lo * 2 + 1 - core)
+    across = [(wide, (1 - z_lo) * 2 + c) for c in (0, 1)]
+    around = [(flipped, (1 - z_lo) * 2 + c) for c in (0, 1)]
+    barrier = pltpu.get_barrier_semaphore()
+    for peer in [sibling] + across + around:
+        pl.semaphore_signal(barrier, 1, device_id=peer, device_id_type=pl.DeviceIdType.MESH)
+    pl.semaphore_wait(barrier, 5)
+    sends = [(sibling, 0), (sibling, 1)] + [(p, 0) for p in across] + [(p, 1) for p in around]
+    copies = []
+    for number, (peer, part) in enumerate(sends):
+        rows = pl.ds(part * half, half)
+        copy = pltpu.make_async_remote_copy(
+            src_ref=src_ref.at[rows],
+            dst_ref=out_ref.at[narrow, rows],
+            send_sem=send_sems.at[number],
+            recv_sem=recv_sems.at[narrow, part],
+            device_id=peer,
+            device_id_type=pl.DeviceIdType.MESH,
+        )
+        copy.start()
+        copies.append(copy)
+    out_ref[narrow] = src_ref[...]
+    for copy in copies:
+        copy.wait_send()
+    for step in range(1, 4):
+        owner = lax.rem(narrow + step, 4)
+        for part in (0, 1):
+            rows = pl.ds(part * half, half)
+            pltpu.make_async_remote_copy(
+                src_ref=src_ref.at[rows],
+                dst_ref=out_ref.at[owner, rows],
+                send_sem=send_sems.at[0],
+                recv_sem=recv_sems.at[owner, part],
+                device_id=sibling,
+                device_id_type=pl.DeviceIdType.MESH,
+            ).wait_recv()
+
+
+def gather_replica(shard_rows):
+    count, width = shard_rows.shape
+    return pl.pallas_call(
+        gather_kernel,
+        out_shape=jax.ShapeDtypeStruct((4, count, width), shard_rows.dtype),
+        in_specs=[pl.BlockSpec(memory_space=pltpu.VMEM)],
+        out_specs=pl.BlockSpec(memory_space=pltpu.VMEM),
+        scratch_shapes=[pltpu.SemaphoreType.DMA((6,)), pltpu.SemaphoreType.DMA((4, 2))],
+        compiler_params=pltpu.CompilerParams(collective_id=0, has_side_effects=True),
+    )(shard_rows)
+
+
 def keep_carry(carry):
     return carry
 
@@ -88,9 +148,14 @@
     group_width = QUERY_HEADS // KEYVAL_HEADS
     score_scale = HEAD_SIZE ** (-0.5)
     shard_len = master.shape[0]
-    replica = lax.all_gather(
-        master.astype(jnp.bfloat16).reshape(shard_len // 128, 128), "narrow", axis=0, tiled=False
-    ).reshape(-1)
+    shard_rows = shard_len // 128
+    padded_rows = -(-shard_rows // 32) * 32
+    replica = gather_replica(
+        jnp.pad(
+            master.astype(jnp.bfloat16).reshape(shard_rows, 128),
+            ((0, padded_rows - shard_rows), (0, 0)),
+        )
+    )[:, :shard_rows].reshape(-1)
     w_query, w_key, w_value, w_out, w_gate, w_up, w_down, gain_one, gain_two = unpack(replica)
     lengths_row = lengths[0]
     local_index = narrow_rank * token_rows + jnp.arange(token_rows, dtype=jnp.int32)

time: 508 us -> 490 us (0.965)
  waiting for transfers between devices: 291 us -> 223 us
  Pallas kernels: 0 us -> 44.3 us
  local copies, waits for them, and re-layouts: 93.1 us -> 99.8 us
    all_gather x1 -> x0, waiting for transfers between devices: 61.3 us -> none  [body(): lax.all_gather(master.astype(jnp.bfloat16).reshape(shard_len // 128, 128)...]
    pallas_call x0 -> x1, Pallas kernels: none -> 44.3 us  [gather_replica(): pl.pallas_call(gather_kernel, out_shape=jax.ShapeDtypeStruct((4, count, w...]
    slice x0 -> x1, local copies, waits for them, and re-layouts: none -> 6.09 us  [body(): gather_replica(jnp.pad(master.astype(jnp.bfloat16).reshape(shard_rows, 12...]
    all_gather x1, waiting for transfers between devices: 6.37 us -> 0.81 us  [body(): lax.all_gather(jnp.concatenate([key_batch, value_batch], axis=1), 'narrow...]
  transfers between devices with their start and end apart: 6 -> 5, of which waited for: 5 -> 4; matrix products, arithmetic and copies ran while one was open for 11% -> 11% of each run, Pallas kernels for 0% -> 0%
where the time goes in v5:
time: 490 us; the launch traced here: 484 us
  waiting for transfers between devices  223 us (46%)
  local copies, waits for them, and re-layouts  99.8 us (20%)
  matrix products  51.7 us (11%)
  Pallas kernels  44.3 us (9%)
  other arithmetic  30 us (6%)
  between operations  18.1 us (4%)
  loops' own time  12.6 us (3%)
    psum x1, waiting for transfers between devices, body(): whole_sum = lax.psum(local_grads, ('wide', 'narrow'))  202 us
    pallas_call x1, Pallas kernels, gather_replica(): pl.pallas_call(gather_kernel, out_shape=jax.ShapeDtypeStruct((4, count, w...  44.3 us
    unnamed x95, local copies, waits for them, and re-layouts  27.7 us
    ppermute x3, waiting for transfers between devices, body(): lax.ppermute(sender_block, 'narrow', [(source, source - shift) for source...  20.2 us
    slice x5, local copies, waits for them, and re-layouts, unpack(): pieces.append(flat[offset:offset + length].reshape(layout))  13.9 us
    dynamic_slice x1, local copies, waits for them, and re-layouts, body(): kv_grad = kv_sum_in[narrow_rank]  10.8 us
    another operation x3, loops' own time, body(): lax.cond(needed, back_span, skip_span, query_gradient_running)  9.96 us
  transfers between devices with their start and end apart: 5, of which 4 were waited for; matrix products, arithmetic and copies ran while one was open for 11% of the time, Pallas kernels for 0%

profile of v5, /device:TPU:0, one launch (start us, length us, event | category | flops | bytes accessed | tf_op | source)
XLA Modules:
  0.0 484.1 jit_solution(7806469608034723491)
XLA Ops:
  10.6 44.3 %shard_map.109 = bf16[4,6432,128]{2,1,0:T(8,128)(2,1)} custom-call(bf16[6432,128]{1,0:T(8,128)(2,1)} %pad.4.src_ref), custom_call_target="tpu_custom_call" | custom-call | tf_op jit(solution)/shard_map/pallas_call | solution.py:129
  54.8 6.1 %slice.144 = bf16[4,6402,128]{2,1,0:T(8,128)(2,1)} slice(bf16[4,6432,128]{2,1,0:T(8,128)(2,1)} %shard_map.109), slice={[0:4], [0:6402], [0:128]} | slice | bytes 13111296 | tf_op jit(solution)/shard_map/slice | solution.py:153
  60.9 7.3 %reshape.590 = bf16[3277824]{0:T(1024)(128)(2,1)} reshape(bf16[4,6402,128]{2,1,0:T(8,128)(2,1)} %slice.144) | data formatting | bytes 13111296 | tf_op jit(solution)/shard_map/reshape | solution.py:158
  77.5 9.8 %slice.163 = bf16[6402,512]{1,0:T(8,128)(2,1)} reshape(bf16[4,6402,128]{2,1,0:T(8,128)(2,1)} %slice.144) | data formatting | bytes 13111296 | tf_op jit(solution)/shard_map/slice | solution.py:45
  94.9 3.9 reshape.600
  106.5 6.0 %conditional.9 = (f32[5,3,384]{2,1,0:T(4,128)}, f32[5,3,384]{2,1,0:T(4,128)S(1)}) conditional(s32[]{:T(128)} %bitcast.87, () %tuple.93, (pred[1,1,384,512]{2,3,1,0:T(8,128)(4,1)S(1)}, bf16[512,5,64]{0,2,1:T(8,128)(2,1)S(1)}, bf16[384,5,3,64]{0,3,2,1:T(8,128)(2,1)S(1)}) %tuple.196), branch_computations={%region_5.6_spmd, %region_6.9_spmd} | conditional | flops 398148480 | bytes 25235472 | solution.py:226
  109.2 3.2 fusion.3
  116.0 5.2 %conditional.12 = (f32[384,5,3,64]{0,3,2,1:T(8,128)S(1)}) conditional(s32[]{:T(128)} %bitcast.87, () %tuple.92, (pred[1,1,384,512]{2,3,1,0:T(8,128)(4,1)S(1)}, bf16[512,5,64]{0,2,1:T(8,128)(2,1)S(1)}, bf16[384,5,3,64]{0,3,2,1:T(8,128)(2,1)S(1)}, f32[5,3,384]{2,1,0:T(4,128)}, bf16[512,5,64]{0,2,1:T(8,128)(2,1)}) %tuple.207), branch_computations={%region_17.18_spmd, %region_18.19_spmd} | conditional | flops 766771200 | bytes 5184064 | solution.py:251
  116.8 4.4 fusion.26
  125.4 3.6 multiply_convert_fusion
  133.3 3.0 convolution_convert_fusion
  137.7 14.1 %conditional.15 = (f32[384,5,3,64]{0,3,2,1:T(8,128)S(1)}, f32[512,320]{0,1:T(8,128)S(1)}, f32[512,320]{0,1:T(8,128)S(1)}) conditional(s32[]{:T(128)} %bitcast.87, () %tuple.100, (pred[1,1,384,512]{2,3,1,0:T(8,128)(4,1)S(1)}, bf16[512,5,64]{0,2,1:T(8,128)(2,1)S(1)}, bf16[384,5,3,64]{0,3,2,1:T(8,128)(2,1)S(1)}, f32[5,3,384]{2,1,0:T(4,128)S(1)}, ...), branch_computations={%region_26.27_spmd, %region_27.28_spmd} | conditional | flops 1919877120 | bytes 60263960 | solution.py:346
  139.7 5.5 %fusion.66 = bf16[5,3,384,512]{2,3,1,0:T(8,128)(2,1)S(1)} fusion(f32[5,512,384,3]{2,1,3,0:T(8,128)S(1)} %fusion.75, f32[5,3,384]{2,1,0:T(4,128)S(1)} %get-tuple-element.179, f32[5,3,384]{2,1,0:T(4,128)S(1)} %get-tuple-element.176, pred[384,512]{0,1:T(8,128)(4,1)S(1)} %bitcast.421, bf16[384,5,3,64]{0,3,2,1:T(8,128)(2,1)} %get-tuple-element.178, ...), kind=kOutput, calls=%fused_computation.67 | convolution fusion | flops 398131200 | bytes 19002368 | tf_op jit(solution)/shard_map/cond/branch_1_fun/qgrd,kgd->grqk/dot_general | solution.py:319
  148.3 3.6 fusion.70
  155.0 9.6 %conditional.17 = (f32[384,5,3,64]{0,3,2,1:T(8,128)S(1)}, f32[512,320]{0,1:T(8,128)S(1)}, f32[512,320]{0,1:T(8,128)S(1)}) conditional(s32[]{:T(128)} %bitcast.85, f32[384,5,3,64]{0,3,2,1:T(8,128)S(1)} %get-tuple-element.224, (pred[1,1,384,512]{2,3,1,0:T(8,128)(4,1)}, bf16[512,5,64]{0,2,1:T(8,128)(2,1)S(1)}, bf16[384,5,3,64]{0,3,2,1:T(8,128)(2,1)S(1)}, ...), branch_computations={%region_30.31_spmd, %region_31.32_spmd} | conditional | flops 1920245760 | bytes 63835728 | solution.py:346
  164.6 3.9 maximum_maximum_fusion
  168.5 5.2 %reshape.603 = f32[4,384,640]{1,0,2:T(4,128)} reshape(f32[1536,640]{0,1:T(8,128)} %maximum_maximum_fusion) | data formatting | bytes 7864320 | tf_op jit(solution)/shard_map/reshape | solution.py:355
  173.7 10.8 %constant_dynamic-slice_fusion.2 = (f32[1,384,640]{1,0,2:T(1,128)}, f32[1,384,640]{1,0,2:T(1,128)S(1)}, f32[1,384,640]{1,0,2:T(1,128)S(1)}, f32[1,384,640]{1,0,2:T(1,128)S(1)}) fusion(f32[4,384,640]{1,0,2:T(4,128)} %reshape.603, s32[]{:T(128)S(6)} %select_n.70, s32[]{:T(128)S(6)} %select_n.73, s32[]{:T(128)S(6)} %select_n.72, s32[]{:T(128)S(6)} %select_n.71), kind=kLoop, calls=%fused_computation.223 | loop fusion | bytes 7864336 | tf_op jit(solution)/shard_map/dynamic_slice | solution.py:358
  195.9 3.1 constant_dynamic-update-slice_fusion.8
  213.4 16.6 %collective-permute-done.2 = f32[384,640]{0,1:T(8,128)} collective-permute-done((f32[384,640]{0,1:T(8,128)}, f32[384,640]{0,1:T(8,128)}, u32[]{:S(2)}, u32[]{:S(2)}) %collective-permute-start.2) | collective-permute-done | bytes 983072 | tf_op jit(solution)/shard_map/ppermute | solution.py:361
  230.0 3.6 collective-permute-done.1
  261.3 3.0 fusion.109
  265.3 202.3 %all-reduce.3.cloned.1.call-done = f32[3277824]{0:T(1024)} async-done(((f32[3277824]{0:T(1024)}), f32[3277824]{0:T(1024)}) %all-reduce.3.cloned.1.call-update) | async-done | bytes 13111312 | tf_op jit(solution)/shard_map/psum | solution.py:401
  467.6 9.4 %multiply_subtract_fusion = (f32[819456]{0:T(1024)}, f32[819456]{0:T(1024)}, f32[819456]{0:T(1024)}, f32[819456]{0:T(1024)}) fusion(f32[819456]{0:T(1024)} %param.27, s32[]{:T(128)S(6)} %mul.470, f32[3277824]{0:T(1024)} %all-reduce.3.cloned.1.call-done, s32[]{:T(128)S(6)} %select_n.74, f32[819456]{0:T(1024)} %param.28, f32[819456]{0:T(1024)} %param.29), kind=kLoop, calls=%fused_computation.116 | loop fusion | flops 15569664 | bytes 26222600 | tf_op jit(solution)/shard_map/sub | solution.py:411
  (195 shorter events, 104.3 us)
Async XLA Ops:
  7.2 96.8 %all-gather.2.cloned.1.call-start = ((), (), s32[]{:S(2)}) async-start(), calls=%async_computation | async-start | bytes 2457600 | tf_op jit(solution)/shard_map/all_gather | solution.py:179
  60.9 9.8 %copy-start.47 = (s32[1,3]{1,0:T(1,128)S(1)}, s32[1,3]{1,0:T(1,128)}, u32[]{:S(2)}) copy-start(s32[1,3]{1,0:T(1,128)} %param.26) | copy-start | bytes 40
  60.9 10.5 %copy-start = (bf16[384,512]{1,0:T(8,128)(2,1)S(1)}, bf16[384,512]{1,0:T(8,128)(2,1)}, u32[]{:S(2)}) copy-start(bf16[384,512]{1,0:T(8,128)(2,1)} %param.24) | copy-start | bytes 1179652
  70.7 30.5 %copy-start.41 = (f32[512]{0:T(512)}, f32[512]{0:T(512)S(1)}, u32[]{:S(2)}) copy-start(f32[512]{0:T(512)S(1)} %get-tuple-element.292) | copy-start | bytes 6148
  71.4 6.1 %copy-start.35 = (bf16[512,320]{1,0:T(8,128)(2,1)}, bf16[512,320]{1,0:T(8,128)(2,1)S(1)}, u32[]{:S(2)}) copy-start(bf16[512,320]{1,0:T(8,128)(2,1)S(1)} %reshape.592) | copy-start | bytes 983044
  71.6 29.7 %copy-start.43 = (f32[384]{0:T(512)}, f32[384]{0:T(512)S(1)}, u32[]{:S(2)}) copy-start(f32[384]{0:T(512)S(1)} %add_rsqrt_fusion.1) | copy-start | bytes 4612
  74.3 393.3 %all-reduce.3.cloned.1.call-start = ((), (), s32[]{:S(2)}) async-start(), calls=%async_computation.1 | async-start | bytes 26222592 | tf_op jit(solution)/shard_map/psum | solution.py:401
  77.5 14.1 %slice-start = ((bf16[3277824]{0:T(1024)(128)(2,1)}), bf16[491520]{0:T(1024)(128)(2,1)S(1)}, s32[]{:S(2)}) async-start(bf16[3277824]{0:T(1024)(128)(2,1)} %reshape.590), calls=%async_computation.2 | async-start | bytes 1966080 | tf_op jit(solution)/shard_map/slice | solution.py:45
  103.1 9.4 %copy-start.24 = (pred[1,1,384,512]{2,3,1,0:T(8,128)(4,1)}, pred[1,1,384,512]{2,3,1,0:T(8,128)(4,1)S(1)}, u32[]{:S(2)}) copy-start(pred[1,1,384,512]{2,3,1,0:T(8,128)(4,1)S(1)} %get-tuple-element.321) | copy-start | bytes 589828
  103.1 12.9 %copy-start.26 = (pred[1,1,384,512]{2,3,1,0:T(8,128)(4,1)}, pred[1,1,384,512]{2,3,1,0:T(8,128)(4,1)S(1)}, u32[]{:S(2)}) copy-start(pred[1,1,384,512]{2,3,1,0:T(8,128)(4,1)S(1)} %get-tuple-element.320) | copy-start | bytes 589828
  103.1 18.1 %copy-start.22 = (pred[1,1,384,512]{2,3,1,0:T(8,128)(4,1)}, pred[1,1,384,512]{2,3,1,0:T(8,128)(4,1)S(1)}, u32[]{:S(2)}) copy-start(pred[1,1,384,512]{2,3,1,0:T(8,128)(4,1)S(1)} %get-tuple-element.319) | copy-start | bytes 589828
  106.5 9.6 %copy-start.10 = (bf16[512,320]{0,1:T(8,128)(2,1)}, bf16[512,320]{0,1:T(8,128)(2,1)S(1)}, u32[]{:S(2)}) copy-start(bf16[512,320]{0,1:T(8,128)(2,1)S(1)} %get-tuple-element.307) | copy-start | bytes 983044
  106.5 14.7 %copy-start.8 = (bf16[512,320]{0,1:T(8,128)(2,1)}, bf16[512,320]{0,1:T(8,128)(2,1)S(1)}, u32[]{:S(2)}) copy-start(bf16[512,320]{0,1:T(8,128)(2,1)S(1)} %get-tuple-element.306) | copy-start | bytes 983044
  123.8 9.2 %copy-start.13 = (f32[384,512]{1,0:T(8,128)}, f32[384,512]{1,0:T(8,128)S(1)}, u32[]{:S(2)}) copy-start(f32[384,512]{1,0:T(8,128)S(1)} %get-tuple-element.328) | copy-start | bytes 2359300
  184.5 8.3 %copy-start.42 = (f32[512]{0:T(512)S(1)}, f32[512]{0:T(512)}, u32[]{:S(2)}) copy-start(f32[512]{0:T(512)} %copy-done.41) | copy-start | bytes 6148
  184.5 8.3 %copy-start.44 = (f32[384]{0:T(512)S(1)}, f32[384]{0:T(512)}, u32[]{:S(2)}) copy-start(f32[384]{0:T(512)} %copy-done.43) | copy-start | bytes 4612
  185.6 44.5 %collective-permute-start.2 = (f32[384,640]{0,1:T(8,128)}, f32[384,640]{0,1:T(8,128)}, u32[]{:S(2)}, u32[]{:S(2)}) collective-permute-start(f32[384,640]{0,1:T(8,128)} %bitcast.381), channel_id=1, source_target_pairs={{3,0},{7,4},{11,8},{15,12},{19,16},{23,20},{27,24},{31,28},{35,32}... | collective-permute-start | bytes 2949128 | tf_op jit(solution)/shard_map/ppermute | solution.py:361
  187.9 45.8 %collective-permute-start.1 = (f32[384,640]{0,1:T(8,128)}, f32[384,640]{0,1:T(8,128)}, u32[]{:S(2)}, u32[]{:S(2)}) collective-permute-start(f32[384,640]{0,1:T(8,128)} %bitcast.382), channel_id=1, source_target_pairs={{2,0},{3,1},{6,4},{7,5},{10,8},{11,9},{14,12},{15,13},{18,16},{19,... | collective-permute-start | bytes 2949128 | tf_op jit(solution)/shard_map/ppermute | solution.py:361
  190.2 43.5 %collective-permute-start = (f32[384,640]{0,1:T(8,128)}, f32[384,640]{0,1:T(8,128)}, u32[]{:S(2)}, u32[]{:S(2)}) collective-permute-start(f32[384,640]{0,1:T(8,128)} %bitcast.383), channel_id=1, source_target_pairs={{1,0},{2,1},{3,2},{5,4},{6,5},{7,6},{9,8},{10,9},{11,10},{13,12},{... | collective-permute-start | bytes 2949128 | tf_op jit(solution)/shard_map/ppermute | solution.py:361
  195.9 7.0 %copy-start.1 = (f32[512,1280]{1,0:T(8,128)S(1)}, f32[512,1280]{1,0:T(8,128)}, u32[]{:S(2)}) copy-start(f32[512,1280]{1,0:T(8,128)} %fusion.160) | copy-start | bytes 7864324
  208.3 25.3 %copy-start.17 = (f32[1,384,640]{1,0,2:T(1,128)S(1)}, f32[1,384,640]{1,0,2:T(1,128)}, u32[]{:S(2)}) copy-start(f32[1,384,640]{1,0,2:T(1,128)} %get-tuple-element.295) | copy-start | bytes 2949124
  212.8 26.0 %copy-start.20 = (bf16[512,320]{1,0:T(8,128)(2,1)S(1)}, bf16[512,320]{1,0:T(8,128)(2,1)}, u32[]{:S(2)}) copy-start(bf16[512,320]{1,0:T(8,128)(2,1)} %copy-done.19) | copy-start | bytes 983044
  239.2 13.2 %copy-start.5 = (f32[655360]{0:T(1024)S(1)}, f32[655360]{0:T(1024)}, u32[]{:S(2)}) copy-start(f32[655360]{0:T(1024)} %reshape.609) | copy-start | bytes 7864324
  245.4 8.7 %copy-start.6 = (f32[655360]{0:T(1024)S(1)}, f32[655360]{0:T(1024)}, u32[]{:S(2)}) copy-start(f32[655360]{0:T(1024)} %reshape.610) | copy-start | bytes 7864324
  (25 other events, 83.2 us)
Sparse Core Ops, SparseCore 0:
  74.4 29.4 all-gather.1
  260.3 207.2 all-reduce.2

commit v6 on v5

--- a/solution.py
+++ b/solution.py
@@ -85,7 +85,8 @@
     core = narrow % 2
     z_hi = (wide // 4) % 2
     flipped = wide + 4 - 8 * z_hi
-    half = src_ref.shape[0] // 2
+    split = (src_ref.shape[0] // 32) * 16
+    halves = [pl.ds(0, split), pl.ds(split, src_ref.shape[0] - split)]
     sibling = (wide, z_lo * 2 + 1 - core)
     across = [(wide, (1 - z_lo) * 2 + c) for c in (0, 1)]
     around = [(flipped, (1 - z_lo) * 2 + c) for c in (0, 1)]
@@ -96,7 +97,7 @@
     sends = [(sibling, 0), (sibling, 1)] + [(p, 0) for p in across] + [(p, 1) for p in around]
     copies = []
     for number, (peer, part) in enumerate(sends):
-        rows = pl.ds(part * half, half)
+        rows = halves[part]
         copy = pltpu.make_async_remote_copy(
             src_ref=src_ref.at[rows],
             dst_ref=out_ref.at[narrow, rows],
@@ -113,7 +114,7 @@
     for step in range(1, 4):
         owner = lax.rem(narrow + step, 4)
         for part in (0, 1):
-            rows = pl.ds(part * half, half)
+            rows = halves[part]
             pltpu.make_async_remote_copy(
                 src_ref=src_ref.at[rows],
                 dst_ref=out_ref.at[owner, rows],
@@ -148,14 +149,7 @@
     group_width = QUERY_HEADS // KEYVAL_HEADS
     score_scale = HEAD_SIZE ** (-0.5)
     shard_len = master.shape[0]
-    shard_rows = shard_len // 128
-    padded_rows = -(-shard_rows // 32) * 32
-    replica = gather_replica(
-        jnp.pad(
-            master.astype(jnp.bfloat16).reshape(shard_rows, 128),
-            ((0, padded_rows - shard_rows), (0, 0)),
-        )
-    )[:, :shard_rows].reshape(-1)
+    replica = gather_replica(master.astype(jnp.bfloat16).reshape(shard_len // 128, 128)).reshape(-1)
     w_query, w_key, w_value, w_out, w_gate, w_up, w_down, gain_one, gain_two = unpack(replica)
     lengths_row = lengths[0]
     local_index = narrow_rank * token_rows + jnp.arange(token_rows, dtype=jnp.int32)
@@ -164,7 +158,7 @@
     key_segment = place_tokens(group_index, lengths_row)[0]
     first_start = local_index[0] - token_position[0]
     last_index = local_index[token_rows - 1]
-    range_rows = min(512, group_rows)
+    range_rows = token_rows
     span_starts = list(range(0, group_rows, range_rows))
     resid = tokens.astype(jnp.float32)
     normed_one, inverse_one = normalize(resid)
@@ -350,10 +344,8 @@
         value_contributions.append(
             value_gradient_range.reshape(range_rows, KEYVAL_HEADS * HEAD_SIZE)
         )
-    key_sum_in = jnp.concatenate(key_contributions, axis=0)
-    value_sum_in = jnp.concatenate(value_contributions, axis=0)
-    kv_sum_in = jnp.concatenate([key_sum_in, value_sum_in], axis=1).reshape(
-        narrow_size, token_rows, 2 * kv_width
+    kv_sum_in = jnp.stack(
+        [jnp.concatenate(pair, axis=1) for pair in zip(key_contributions, value_contributions)]
     )
     kv_grad = kv_sum_in[narrow_rank]
     for shift in range(1, narrow_size):

time: 490 us -> 447 us (0.912)
  local copies, waits for them, and re-layouts: 99.8 us -> 76.4 us
  waiting for transfers between devices: 223 us -> 206 us
  matrix products: 51.7 us -> 46.5 us
    psum x1, waiting for transfers between devices: 202 us -> 187 us  [body(): whole_sum = lax.psum(local_grads, ('wide', 'narrow'))]
    dynamic_slice x1 -> x0, local copies, waits for them, and re-layouts: 10.8 us -> none  [body(): kv_grad = kv_sum_in[narrow_rank]]
    slice x1 -> x0, local copies, waits for them, and re-layouts: 6.09 us -> none  [body(): gather_replica(jnp.pad(master.astype(jnp.bfloat16).reshape(shard_rows, 12...]
    reshape x2 -> x1, local copies, waits for them, and re-layouts: 12.6 us -> 7.39 us  [body(): gather_replica(master.astype(jnp.bfloat16).reshape(shard_len // 128, 128))]
    unnamed x95 -> x124, local copies, waits for them, and re-layouts: 27.7 us -> 26.5 us
    another operation x3 -> x4, loops' own time: 9.96 us -> 10.3 us  [body(): lax.cond(needed, back_span, skip_span, query_gradient_running)]
  transfers between devices with their start and end apart: 5 -> 5, of which waited for: 4 -> 2; matrix products, arithmetic and copies ran while one was open for 11% -> 11% of each run, Pallas kernels for 0% -> 0%
where the time goes in v6:
time: 447 us; the launch traced here: 442 us
  waiting for transfers between devices  206 us (46%)
  local copies, waits for them, and re-layouts  76.4 us (17%)
  matrix products  46.5 us (10%)
  Pallas kernels  44.1 us (10%)
  other arithmetic  30.5 us (7%)
  between operations  19 us (4%)
  loops' own time  13.8 us (3%)
  starting transfers between devices  4.78 us (1%)
    psum x1, waiting for transfers between devices, body(): whole_sum = lax.psum(local_grads, ('wide', 'narrow'))  187 us
    pallas_call x1, Pallas kernels, gather_replica(): pl.pallas_call(gather_kernel, out_shape=jax.ShapeDtypeStruct((4, count, w...  44.1 us
    unnamed x124, local copies, waits for them, and re-layouts  26.5 us
    ppermute x3, waiting for transfers between devices, body(): lax.ppermute(sender_block, 'narrow', [(source, source - shift) for source...  19.4 us
    slice x5, local copies, waits for them, and re-layouts, unpack(): pieces.append(flat[offset:offset + length].reshape(layout))  13.9 us
    another operation x4, loops' own time, body(): lax.cond(needed, back_span, skip_span, query_gradient_running)  10.3 us
    sub x1, other arithmetic, body(): master - learn_rate * (first_hat / (jnp.sqrt(second_hat) + adam_eps) + de...  9.45 us
  transfers between devices with their start and end apart: 5, of which 2 were waited for; matrix products, arithmetic and copies ran while one was open for 11% of the time, Pallas kernels for 0%

profile of v6, /device:TPU:0, one launch (start us, length us, event | category | flops | bytes accessed | tf_op | source)
XLA Modules:
  0.0 441.5 jit_solution(12332929258094553071)
XLA Ops:
  7.2 3.3 convert_bitcast_fusion.src_ref
  10.5 44.1 %shard_map.109 = bf16[4,6402,128]{2,1,0:T(8,128)(2,1)} custom-call(bf16[6402,128]{1,0:T(8,128)(2,1)} %convert_bitcast_fusion.src_ref), custom_call_target="tpu_custom_call" | custom-call | tf_op jit(solution)/shard_map/pallas_call | solution.py:130
  54.6 7.4 %reshape.707 = bf16[3277824]{0:T(1024)(128)(2,1)} reshape(bf16[4,6402,128]{2,1,0:T(8,128)(2,1)} %shard_map.109) | data formatting | bytes 13111296 | tf_op jit(solution)/shard_map/reshape | solution.py:152
  69.3 2.9 fusion.185
  72.2 9.9 %slice.184 = bf16[6402,512]{1,0:T(8,128)(2,1)} reshape(bf16[4,6402,128]{2,1,0:T(8,128)(2,1)} %shard_map.109) | data formatting | bytes 13111296 | tf_op jit(solution)/shard_map/slice | solution.py:45
  90.3 3.9 reshape.719
  98.5 2.8 fusion.187
  101.3 4.9 %conditional.12 = (f32[5,3,384]{2,1,0:T(4,128)}, f32[5,3,384]{2,1,0:T(4,128)S(1)}) conditional(s32[]{:T(128)} %bitcast.115, () %tuple.117, (pred[1,1,384,384]{2,3,1,0:T(8,128)(4,1)S(1)}, bf16[384,5,64]{0,2,1:T(8,128)(2,1)S(1)}, bf16[384,5,3,64]{0,3,2,1:T(8,128)(2,1)S(1)}) %tuple.244), branch_computations={%region_5.6_spmd, %region_6.9_spmd} | conditional | flops 298615680 | bytes 19157008 | solution.py:220
  106.3 2.9 conditional.15
  109.9 4.3 conditional.16
  110.7 3.5 fusion.32
  119.6 3.6 multiply_convert_fusion
  128.0 3.1 convolution_convert_fusion
  133.1 11.0 %conditional.20 = (f32[384,5,3,64]{0,3,2,1:T(8,128)S(1)}, f32[384,320]{0,1:T(8,128)S(1)}, f32[384,320]{0,1:T(8,128)S(1)}) conditional(s32[]{:T(128)} %bitcast.115, () %tuple.126, (pred[1,1,384,384]{2,3,1,0:T(8,128)(4,1)S(1)}, bf16[384,5,64]{0,2,1:T(8,128)(2,1)S(1)}, bf16[384,5,3,64]{0,3,2,1:T(8,128)(2,1)S(1)}, f32[5,3,384]{2,1,0:T(4,128)S(1)}, ...), branch_computations={%region_32.33_spmd, %region_33.34_spmd} | conditional | flops 1439907840 | bytes 46321176 | solution.py:340
  134.6 4.1 fusion.87
  141.2 2.9 fusion.91
  146.3 4.6 %conditional.22 = (f32[384,5,3,64]{0,3,2,1:T(8,128)S(1)}, f32[384,320]{0,1:T(8,128)S(1)}, f32[384,320]{0,1:T(8,128)S(1)}) conditional(s32[]{:T(128)} %bitcast.113, f32[384,5,3,64]{0,3,2,1:T(8,128)S(1)} %get-tuple-element.299, (pred[1,1,384,384]{2,3,1,0:T(8,128)(4,1)S(1)}, bf16[384,5,64]{0,2,1:T(8,128)(2,1)}, ...), branch_computations={%region_36.37_spmd, %region_37.38_spmd} | conditional | flops 1440276480 | bytes 49854060 | solution.py:340
  151.8 5.4 %conditional.23 = (f32[384,5,3,64]{0,3,2,1:T(8,128)S(1)}, f32[384,320]{0,1:T(8,128)S(1)}, f32[384,320]{0,1:T(8,128)S(1)}) conditional(s32[]{:T(128)} %bitcast.112, f32[384,5,3,64]{0,3,2,1:T(8,128)S(1)} %get-tuple-element.300, (pred[1,1,384,384]{2,3,1,0:T(8,128)(4,1)S(1)}, bf16[384,5,64]{0,2,1:T(8,128)(2,1)S(1)}, ...), branch_computations={%region_38.39_spmd, %region_39.40_spmd} | conditional | flops 1440276480 | bytes 48870992 | solution.py:340
  170.6 3.1 constant_dynamic-update-slice_fusion.8
  186.7 19.4 %collective-permute-done.2 = f32[384,640]{0,1:T(8,128)} collective-permute-done((f32[384,640]{0,1:T(8,128)}, f32[384,640]{0,1:T(8,128)}, u32[]{:S(2)}, u32[]{:S(2)}) %collective-permute-start.2) | collective-permute-done | bytes 983072 | tf_op jit(solution)/shard_map/ppermute | solution.py:353
  222.0 3.1 constant_dynamic-update-slice_fusion.5
  234.0 3.0 fusion.145
  238.1 186.9 %all-reduce.2.cloned.1.call-done = f32[3277824]{0:T(1024)} async-done(((f32[3277824]{0:T(1024)}), f32[3277824]{0:T(1024)}) %all-reduce.2.cloned.1.call-update) | async-done | bytes 13111312 | tf_op jit(solution)/shard_map/psum | solution.py:393
  425.0 9.4 %multiply_subtract_fusion = (f32[819456]{0:T(1024)}, f32[819456]{0:T(1024)}, f32[819456]{0:T(1024)}, f32[819456]{0:T(1024)}) fusion(f32[819456]{0:T(1024)} %param.33, s32[]{:T(128)S(6)} %mul.497, f32[3277824]{0:T(1024)} %all-reduce.2.cloned.1.call-done, s32[]{:T(128)S(6)} %select_n.86, f32[819456]{0:T(1024)} %param.34, f32[819456]{0:T(1024)} %param.35), kind=kLoop, calls=%fused_computation.154 | loop fusion | flops 15569664 | bytes 26222600 | tf_op jit(solution)/shard_map/sub | solution.py:403
  (230 shorter events, 92.8 us)
Async XLA Ops:
  7.2 91.3 %all-gather.2.cloned.1.call-start = ((), (), s32[]{:S(2)}) async-start(), calls=%async_computation | async-start | bytes 2457600 | tf_op jit(solution)/shard_map/all_gather | solution.py:173
  54.6 9.9 %copy-start.67 = (s32[1,3]{1,0:T(1,128)S(1)}, s32[1,3]{1,0:T(1,128)}, u32[]{:S(2)}) copy-start(s32[1,3]{1,0:T(1,128)} %param.32) | copy-start | bytes 40
  54.6 10.6 %copy-start = (bf16[384,512]{1,0:T(8,128)(2,1)S(1)}, bf16[384,512]{1,0:T(8,128)(2,1)}, u32[]{:S(2)}) copy-start(bf16[384,512]{1,0:T(8,128)(2,1)} %param.30) | copy-start | bytes 1179652
  64.5 32.0 %copy-start.56 = (f32[512]{0:T(512)}, f32[512]{0:T(512)S(1)}, u32[]{:S(2)}) copy-start(f32[512]{0:T(512)S(1)} %get-tuple-element.384) | copy-start | bytes 6148
  65.3 7.0 %copy-start.44 = (bf16[512,320]{1,0:T(8,128)(2,1)}, bf16[512,320]{1,0:T(8,128)(2,1)S(1)}, u32[]{:S(2)}) copy-start(bf16[512,320]{1,0:T(8,128)(2,1)S(1)} %reshape.709) | copy-start | bytes 983044
  65.5 31.1 %copy-start.58 = (f32[384]{0:T(512)}, f32[384]{0:T(512)S(1)}, u32[]{:S(2)}) copy-start(f32[384]{0:T(512)S(1)} %add_rsqrt_fusion.1) | copy-start | bytes 4612
  65.8 6.4 %copy-start.22 = (bf16[512,320]{1,0:T(8,128)(2,1)}, bf16[512,320]{1,0:T(8,128)(2,1)S(1)}, u32[]{:S(2)}) copy-start(bf16[512,320]{1,0:T(8,128)(2,1)S(1)} %reshape.708) | copy-start | bytes 983044
  67.8 29.5 %copy-start.48 = (f32[384,32]{0,1:T(8,128)}, f32[384,32]{0,1:T(8,128)S(1)}, u32[]{:S(2)}) copy-start(f32[384,32]{0,1:T(8,128)S(1)} %get-tuple-element.419) | copy-start | bytes 147460
  68.8 356.2 %all-reduce.2.cloned.1.call-start = ((), (), s32[]{:S(2)}) async-start(), calls=%async_computation.1 | async-start | bytes 26222592 | tf_op jit(solution)/shard_map/psum | solution.py:393
  72.2 14.8 %slice-start = ((bf16[3277824]{0:T(1024)(128)(2,1)}), bf16[491520]{0:T(1024)(128)(2,1)S(1)}, s32[]{:S(2)}) async-start(bf16[3277824]{0:T(1024)(128)(2,1)} %reshape.707), calls=%async_computation.2 | async-start | bytes 1966080 | tf_op jit(solution)/shard_map/slice | solution.py:45
  98.4 7.8 %copy-start.31 = (pred[1,1,384,384]{2,3,1,0:T(8,128)(4,1)}, pred[1,1,384,384]{2,3,1,0:T(8,128)(4,1)S(1)}, u32[]{:S(2)}) copy-start(pred[1,1,384,384]{2,3,1,0:T(8,128)(4,1)S(1)} %get-tuple-element.416) | copy-start | bytes 442372
  98.4 7.8 %copy-start.29 = (pred[1,1,384,384]{2,3,1,0:T(8,128)(4,1)}, pred[1,1,384,384]{2,3,1,0:T(8,128)(4,1)S(1)}, u32[]{:S(2)}) copy-start(pred[1,1,384,384]{2,3,1,0:T(8,128)(4,1)S(1)} %get-tuple-element.414) | copy-start | bytes 442372
  98.4 11.5 %copy-start.33 = (pred[1,1,384,384]{2,3,1,0:T(8,128)(4,1)}, pred[1,1,384,384]{2,3,1,0:T(8,128)(4,1)S(1)}, u32[]{:S(2)}) copy-start(pred[1,1,384,384]{2,3,1,0:T(8,128)(4,1)S(1)} %get-tuple-element.415) | copy-start | bytes 442372
  101.3 8.7 %copy-start.14 = (bf16[384,320]{0,1:T(8,128)(2,1)}, bf16[384,320]{0,1:T(8,128)(2,1)S(1)}, u32[]{:S(2)}) copy-start(bf16[384,320]{0,1:T(8,128)(2,1)S(1)} %get-tuple-element.400) | copy-start | bytes 737284
  101.3 13.0 %copy-start.12 = (bf16[384,320]{0,1:T(8,128)(2,1)}, bf16[384,320]{0,1:T(8,128)(2,1)S(1)}, u32[]{:S(2)}) copy-start(bf16[384,320]{0,1:T(8,128)(2,1)S(1)} %get-tuple-element.399) | copy-start | bytes 737284
  101.3 13.0 %copy-start.10 = (bf16[384,320]{0,1:T(8,128)(2,1)}, bf16[384,320]{0,1:T(8,128)(2,1)S(1)}, u32[]{:S(2)}) copy-start(bf16[384,320]{0,1:T(8,128)(2,1)S(1)} %get-tuple-element.398) | copy-start | bytes 737284
  118.0 9.7 %copy-start.17 = (f32[384,512]{1,0:T(8,128)}, f32[384,512]{1,0:T(8,128)S(1)}, u32[]{:S(2)}) copy-start(f32[384,512]{1,0:T(8,128)S(1)} %get-tuple-element.423) | copy-start | bytes 2359300
  160.3 7.2 %copy-start.57 = (f32[512]{0:T(512)S(1)}, f32[512]{0:T(512)}, u32[]{:S(2)}) copy-start(f32[512]{0:T(512)} %copy-done.56) | copy-start | bytes 6148
  160.3 7.2 %copy-start.59 = (f32[384]{0:T(512)S(1)}, f32[384]{0:T(512)}, u32[]{:S(2)}) copy-start(f32[384]{0:T(512)} %copy-done.58) | copy-start | bytes 4612
  162.0 44.1 %collective-permute-start.2 = (f32[384,640]{0,1:T(8,128)}, f32[384,640]{0,1:T(8,128)}, u32[]{:S(2)}, u32[]{:S(2)}) collective-permute-start(f32[384,640]{0,1:T(8,128)} %get-tuple-element.388), channel_id=1, source_target_pairs={{3,0},{7,4},{11,8},{15,12},{19,16},{23,20},{27,24},{31,28},{35,32}... | collective-permute-start | bytes 2949128 | tf_op jit(solution)/shard_map/ppermute | solution.py:353
  163.3 42.8 %collective-permute-start.1 = (f32[384,640]{0,1:T(8,128)}, f32[384,640]{0,1:T(8,128)}, u32[]{:S(2)}, u32[]{:S(2)}) collective-permute-start(f32[384,640]{0,1:T(8,128)} %get-tuple-element.389), channel_id=1, source_target_pairs={{2,0},{3,1},{6,4},{7,5},{10,8},{11,9},{14,12},{15,13},{18,16},{19,... | collective-permute-start | bytes 2949128 | tf_op jit(solution)/shard_map/ppermute | solution.py:353
  164.6 41.5 %collective-permute-start = (f32[384,640]{0,1:T(8,128)}, f32[384,640]{0,1:T(8,128)}, u32[]{:S(2)}, u32[]{:S(2)}) collective-permute-start(f32[384,640]{0,1:T(8,128)} %get-tuple-element.387), channel_id=1, source_target_pairs={{1,0},{2,1},{3,2},{5,4},{6,5},{7,6},{9,8},{10,9},{11,10},{13,12},{... | collective-permute-start | bytes 2949128 | tf_op jit(solution)/shard_map/ppermute | solution.py:353
  186.6 24.7 %copy-start.23 = (bf16[512,320]{1,0:T(8,128)(2,1)S(1)}, bf16[512,320]{1,0:T(8,128)(2,1)}, u32[]{:S(2)}) copy-start(bf16[512,320]{1,0:T(8,128)(2,1)} %copy-done.22) | copy-start | bytes 983044
  213.2 12.0 %copy-start.7 = (f32[655360]{0:T(1024)S(1)}, f32[655360]{0:T(1024)}, u32[]{:S(2)}) copy-start(f32[655360]{0:T(1024)} %reshape.727) | copy-start | bytes 7864324
  (41 other events, 125.8 us)
Sparse Core Ops, SparseCore 0:
  68.9 29.4 all-gather.1
  233.1 191.9 all-reduce.1

commit v7 on v6

--- a/solution.py
+++ b/solution.py
@@ -377,21 +377,27 @@
         + inverse_one
         * (dn_one - normed_one * jnp.mean(dn_one * normed_one, axis=-1, keepdims=True))
     ).astype(jnp.bfloat16)
-    local_grads = jnp.concatenate(
-        [
-            g_query.reshape(-1),
-            g_key.reshape(-1),
-            g_value.reshape(-1),
-            g_out.reshape(-1),
-            g_gate.reshape(-1),
-            g_up.reshape(-1),
-            g_down.reshape(-1),
-            g_gain_one,
-            g_gain_two,
-        ]
-    )
-    whole_sum = lax.psum(local_grads, ("wide", "narrow"))
-    summed = lax.dynamic_slice_in_dim(whole_sum, narrow_rank * shard_len, shard_len)
+    down_and_gains = jnp.concatenate([g_down, g_gain_one[None], g_gain_two[None]], axis=0)
+    grad_pieces = lax.psum(
+        (g_query, g_key, g_value, g_out, g_gate, g_up, down_and_gains), ("wide", "narrow")
+    )
+
+    def shard_of(rank):
+        def build(pieces):
+            parts = []
+            offset = 0
+            low, high = rank * shard_len, (rank + 1) * shard_len
+            for piece in pieces:
+                size = piece.size
+                start, stop = max(low, offset), min(high, offset + size)
+                if start < stop:
+                    parts.append(piece.reshape(-1)[start - offset : stop - offset])
+                offset = offset + size
+            return jnp.concatenate(parts)
+
+        return build
+
+    summed = lax.switch(narrow_rank, [shard_of(rank) for rank in range(narrow_size)], grad_pieces)
     token_total = token_rows * narrow_size * lax.axis_size("wide")
     gradient = summed * (1.0 / math.sqrt(token_total))
     new_first = beta_one * first_moment + (1.0 - beta_one) * gradient

time: 447 us -> 446 us (level)
  local copies, waits for them, and re-layouts: 76.4 us -> 59.5 us
  waiting for transfers between devices: 206 us -> 217 us
    unnamed x124 -> x82, local copies, waits for them, and re-layouts: 26.5 us -> 5 us
    ppermute x3, waiting for transfers between devices: 19.4 us -> 26.8 us  [body(): lax.ppermute(sender_block, 'narrow', [(source, source - shift) for source...]
    concatenate x1, local copies, waits for them, and re-layouts: 1.27 us -> 7.35 us  [body(): jnp.concatenate([g_down, g_gain_one[None], g_gain_two[None]], axis=0)]
    reshape x5 -> x3, local copies, waits for them, and re-layouts: 10.5 us -> 4.69 us  [build(): parts.append(piece.reshape(-1)[start - offset:stop - offset])]
  transfers between devices with their start and end apart: 5 -> 5, of which waited for: 2 -> 2; matrix products, arithmetic and copies ran while one was open for 11% -> 9% of each run, Pallas kernels for 0% -> 0%
where the time goes in v7:
time: 446 us; the launch traced here: 440 us
  waiting for transfers between devices  217 us (49%)
  local copies, waits for them, and re-layouts  59.5 us (13%)
  matrix products  47.5 us (11%)
  Pallas kernels  44.2 us (10%)
  other arithmetic  32.4 us (7%)
  between operations  18.9 us (4%)
  loops' own time  14 us (3%)
  starting transfers between devices  6.57 us (1%)
    psum x1, waiting for transfers between devices, body(): lax.psum((g_query, g_key, g_value, g_out, g_gate, g_up, down_and_gains),...  190 us
    pallas_call x1, Pallas kernels, gather_replica(): pl.pallas_call(gather_kernel, out_shape=jax.ShapeDtypeStruct((4, count, w...  44.2 us
    ppermute x3, waiting for transfers between devices, body(): lax.ppermute(sender_block, 'narrow', [(source, source - shift) for source...  26.8 us
    slice x5, local copies, waits for them, and re-layouts, unpack(): pieces.append(flat[offset:offset + length].reshape(layout))  14 us
    another operation x4, loops' own time, body(): lax.cond(needed, back_span, skip_span, query_gradient_running)  10.6 us
    sub x1, other arithmetic, body(): master - learn_rate * (first_hat / (jnp.sqrt(second_hat) + adam_eps) + de...  9.19 us
  transfers between devices with their start and end apart: 5, of which 2 were waited for; matrix products, arithmetic and copies ran while one was open for 9% of the time, Pallas kernels for 0%

profile of v7, /device:TPU:0, one launch (start us, length us, event | category | flops | bytes accessed | tf_op | source)
XLA Modules:
  0.0 440.3 jit_solution(2692089234358852169)
XLA Ops:
  7.2 3.3 convert_bitcast_fusion.src_ref
  10.5 44.2 %shard_map.109 = bf16[4,6402,128]{2,1,0:T(8,128)(2,1)} custom-call(bf16[6402,128]{1,0:T(8,128)(2,1)} %convert_bitcast_fusion.src_ref), custom_call_target="tpu_custom_call" | custom-call | tf_op jit(solution)/shard_map/pallas_call | solution.py:130
  54.7 7.3 %reshape.716 = bf16[3277824]{0:T(1024)(128)(2,1)} reshape(bf16[4,6402,128]{2,1,0:T(8,128)(2,1)} %shard_map.109) | data formatting | bytes 13111296 | tf_op jit(solution)/shard_map/reshape | solution.py:152
  69.2 2.9 fusion.186
  72.2 9.9 %slice.202 = bf16[6402,512]{1,0:T(8,128)(2,1)} reshape(bf16[4,6402,128]{2,1,0:T(8,128)(2,1)} %shard_map.109) | data formatting | bytes 13111296 | tf_op jit(solution)/shard_map/slice | solution.py:45
  90.3 3.8 reshape.728
  101.4 4.9 %conditional.13 = (f32[5,3,384]{2,1,0:T(4,128)}, f32[5,3,384]{2,1,0:T(4,128)S(1)}) conditional(s32[]{:T(128)} %bitcast.115, () %tuple.129, (pred[1,1,384,384]{2,3,1,0:T(8,128)(4,1)S(1)}, bf16[384,5,64]{0,2,1:T(8,128)(2,1)S(1)}, bf16[384,5,3,64]{0,3,2,1:T(8,128)(2,1)S(1)}) %tuple.268), branch_computations={%region_5.6_spmd, %region_6.9_spmd} | conditional | flops 298615680 | bytes 19157008 | solution.py:220
  110.6 4.3 conditional.17
  111.4 3.6 fusion.32
  119.9 3.6 multiply_convert_fusion
  125.4 3.1 convolution_convert_fusion
  132.4 11.3 %conditional.21 = (f32[384,5,3,64]{0,3,2,1:T(8,128)S(1)}, f32[384,320]{0,1:T(8,128)S(1)}, f32[384,320]{0,1:T(8,128)S(1)}) conditional(s32[]{:T(128)} %bitcast.115, () %tuple.138, (pred[1,1,384,384]{2,3,1,0:T(8,128)(4,1)S(1)}, bf16[384,5,64]{0,2,1:T(8,128)(2,1)S(1)}, bf16[384,5,3,64]{0,3,2,1:T(8,128)(2,1)S(1)}, f32[5,3,384]{2,1,0:T(4,128)S(1)}, ...), branch_computations={%region_32.33_spmd, %region_33.34_spmd} | conditional | flops 1439907840 | bytes 46321176 | solution.py:340
  134.3 4.1 fusion.87
  140.8 2.9 fusion.91
  145.9 4.5 %conditional.23 = (f32[384,5,3,64]{0,3,2,1:T(8,128)S(1)}, f32[384,320]{0,1:T(8,128)S(1)}, f32[384,320]{0,1:T(8,128)S(1)}) conditional(s32[]{:T(128)} %bitcast.113, f32[384,5,3,64]{0,3,2,1:T(8,128)S(1)} %get-tuple-element.334, (pred[1,1,384,384]{2,3,1,0:T(8,128)(4,1)}, bf16[384,5,64]{0,2,1:T(8,128)(2,1)S(1)}, ...), branch_computations={%region_36.37_spmd, %region_37.38_spmd} | conditional | flops 1440276480 | bytes 49460844 | solution.py:340
  151.4 5.5 %conditional.24 = (f32[384,5,3,64]{0,3,2,1:T(8,128)S(1)}, f32[384,320]{0,1:T(8,128)S(1)}, f32[384,320]{0,1:T(8,128)S(1)}) conditional(s32[]{:T(128)} %bitcast.112, f32[384,5,3,64]{0,3,2,1:T(8,128)S(1)} %get-tuple-element.335, (pred[1,1,384,384]{2,3,1,0:T(8,128)(4,1)}, bf16[384,5,64]{0,2,1:T(8,128)(2,1)S(1)}, ...), branch_computations={%region_38.39_spmd, %region_39.40_spmd} | conditional | flops 1440276480 | bytes 49460844 | solution.py:340
  162.9 3.3 collective-permute-start
  176.4 26.8 %collective-permute-done.2 = f32[384,640]{0,1:T(8,128)S(1)} collective-permute-done((f32[384,640]{0,1:T(8,128)S(1)}, f32[384,640]{0,1:T(8,128)S(1)}, u32[]{:S(2)}, u32[]{:S(2)}) %collective-permute-start.2) | collective-permute-done | bytes 983072 | tf_op jit(solution)/shard_map/ppermute | solution.py:353
  207.1 7.4 %concatenate.53 = f32[1282,512]{1,0:T(8,128)} concatenate(f32[1280,512]{1,0:T(8,128)} %fusion.201, f32[1,512]{1,0:T(1,128)S(1)} %bitcast.564, f32[1,512]{1,0:T(1,128)S(1)} %bitcast.563), dimensions={0} | concatenate | bytes 5251072 | tf_op jit(solution)/shard_map/concatenate | solution.py:380
  215.6 3.0 fusion.145
  219.6 190.3 %all-reduce.3.cloned.1.call-done = (f32[512,960]{0,1:T(8,128)}, f32[512,320]{0,1:T(8,128)}, f32[512,320]{0,1:T(8,128)}, f32[960,512]{1,0:T(8,128)}, f32[512,1280...) async-done(((f32[512,960]{0,1:T(8,128)}, f32[512,320]{0,1:T(8,128)}, f32[512,320]{0,1:T(8,128)}, f32[960,512]{1,0:T(8,128)}, f32[512,1280]{1,0:T(8,128)}, ...) | async-done | bytes 13111312 | tf_op jit(solution)/shard_map/psum | solution.py:381
  410.0 14.1 %conditional.25 = (f32[819456]{0:T(1024)}) conditional(s32[]{:T(128)} %clamp.3, (f32[512,960]{0,1:T(8,128)}, f32[512,320]{0,1:T(8,128)}, f32[512,320]{0,1:T(8,128)}, f32[960,512]{1,0:T(8,128)}) %tuple.143, (f32[960,512]{1,0:T(8,128)}, f32[512,1280]{1,0:T(8,128)}) %tuple.144, (f32[512,1280]{1,0:T(8,128)}, ...), branch_computations={%region_50.51_spmd, %region_51.52_spmd, %region_52.53_spmd, %regio... | conditional | flops 2458368 | bytes 31467580 | solution.py:400
  420.4 3.7 pad_maximum_fusion
  424.1 9.2 %multiply_subtract_fusion = (f32[819456]{0:T(1024)}, f32[819456]{0:T(1024)}, f32[819456]{0:T(1024)}, f32[819456]{0:T(1024)}) fusion(f32[819456]{0:T(1024)} %param.37, s32[]{:T(128)S(6)} %mul.507, f32[819456]{0:T(1024)} %get-tuple-element.539, f32[819456]{0:T(1024)} %param.38, f32[819456]{0:T(1024)} %param.39), kind=kLoop, calls=%fused_computation.158 | loop fusion | flops 15569664 | bytes 26222596 | tf_op jit(solution)/shard_map/sub | solution.py:409
  (197 shorter events, 78.4 us)
Async XLA Ops:
  7.2 91.4 %all-gather.2.cloned.1.call-start = ((), (), s32[]{:S(2)}) async-start(), calls=%async_computation | async-start | bytes 2457600 | tf_op jit(solution)/shard_map/all_gather | solution.py:173
  54.7 9.2 %copy-start.55 = (s32[1,3]{1,0:T(1,128)S(1)}, s32[1,3]{1,0:T(1,128)}, u32[]{:S(2)}) copy-start(s32[1,3]{1,0:T(1,128)} %param.36) | copy-start | bytes 40
  54.7 10.5 %copy-start = (bf16[384,512]{1,0:T(8,128)(2,1)S(1)}, bf16[384,512]{1,0:T(8,128)(2,1)}, u32[]{:S(2)}) copy-start(bf16[384,512]{1,0:T(8,128)(2,1)} %param.34) | copy-start | bytes 1179652
  65.2 7.0 %copy-start.36 = (bf16[512,320]{1,0:T(8,128)(2,1)}, bf16[512,320]{1,0:T(8,128)(2,1)S(1)}, u32[]{:S(2)}) copy-start(bf16[512,320]{1,0:T(8,128)(2,1)S(1)} %reshape.718) | copy-start | bytes 983044
  65.7 6.4 %copy-start.16 = (bf16[512,320]{1,0:T(8,128)(2,1)}, bf16[512,320]{1,0:T(8,128)(2,1)S(1)}, u32[]{:S(2)}) copy-start(bf16[512,320]{1,0:T(8,128)(2,1)S(1)} %reshape.717) | copy-start | bytes 983044
  68.7 341.3 %all-reduce.3.cloned.1.call-start = ((), (), s32[]{:S(2)}) async-start(), calls=%async_computation.1 | async-start | bytes 26247168 | tf_op jit(solution)/shard_map/psum | solution.py:381
  72.1 14.9 %slice-start = ((bf16[3277824]{0:T(1024)(128)(2,1)}), bf16[491520]{0:T(1024)(128)(2,1)S(1)}, s32[]{:S(2)}) async-start(bf16[3277824]{0:T(1024)(128)(2,1)} %reshape.716), calls=%async_computation.2 | async-start | bytes 1966080 | tf_op jit(solution)/shard_map/slice | solution.py:45
  98.5 7.9 %copy-start.23 = (pred[1,1,384,384]{2,3,1,0:T(8,128)(4,1)}, pred[1,1,384,384]{2,3,1,0:T(8,128)(4,1)S(1)}, u32[]{:S(2)}) copy-start(pred[1,1,384,384]{2,3,1,0:T(8,128)(4,1)S(1)} %get-tuple-element.470) | copy-start | bytes 442372
  98.5 7.9 %copy-start.21 = (pred[1,1,384,384]{2,3,1,0:T(8,128)(4,1)}, pred[1,1,384,384]{2,3,1,0:T(8,128)(4,1)S(1)}, u32[]{:S(2)}) copy-start(pred[1,1,384,384]{2,3,1,0:T(8,128)(4,1)S(1)} %get-tuple-element.468) | copy-start | bytes 442372
  98.5 12.1 %copy-start.25 = (pred[1,1,384,384]{2,3,1,0:T(8,128)(4,1)}, pred[1,1,384,384]{2,3,1,0:T(8,128)(4,1)S(1)}, u32[]{:S(2)}) copy-start(pred[1,1,384,384]{2,3,1,0:T(8,128)(4,1)S(1)} %get-tuple-element.469) | copy-start | bytes 442372
  98.5 17.4 %copy-start.19 = (pred[1,1,384,384]{2,3,1,0:T(8,128)(4,1)}, pred[1,1,384,384]{2,3,1,0:T(8,128)(4,1)S(1)}, u32[]{:S(2)}) copy-start(pred[1,1,384,384]{2,3,1,0:T(8,128)(4,1)S(1)} %get-tuple-element.467) | copy-start | bytes 442372
  101.4 9.2 %copy-start.7 = (bf16[384,320]{0,1:T(8,128)(2,1)}, bf16[384,320]{0,1:T(8,128)(2,1)S(1)}, u32[]{:S(2)}) copy-start(bf16[384,320]{0,1:T(8,128)(2,1)S(1)} %get-tuple-element.454) | copy-start | bytes 737284
  101.4 13.5 %copy-start.5 = (bf16[384,320]{0,1:T(8,128)(2,1)}, bf16[384,320]{0,1:T(8,128)(2,1)S(1)}, u32[]{:S(2)}) copy-start(bf16[384,320]{0,1:T(8,128)(2,1)S(1)} %get-tuple-element.453) | copy-start | bytes 737284
  118.3 6.8 %copy-start.10 = (f32[384,512]{1,0:T(8,128)}, f32[384,512]{1,0:T(8,128)S(1)}, u32[]{:S(2)}) copy-start(f32[384,512]{1,0:T(8,128)S(1)} %get-tuple-element.477) | copy-start | bytes 2359300
  125.4 7.0 %copy-start.1 = (f32[384,512]{1,0:T(8,128)}, f32[384,512]{1,0:T(8,128)S(1)}, u32[]{:S(2)}) copy-start(f32[384,512]{1,0:T(8,128)S(1)} %multiply_add_fusion.6) | copy-start | bytes 2359300
  125.4 7.0 %copy-start.8 = (bf16[384,320]{0,1:T(8,128)(2,1)S(1)}, bf16[384,320]{0,1:T(8,128)(2,1)}, u32[]{:S(2)}) copy-start(bf16[384,320]{0,1:T(8,128)(2,1)} %copy-done.7) | copy-start | bytes 737284
  125.4 7.0 %copy-start.26 = (pred[1,1,384,384]{2,3,1,0:T(8,128)(4,1)S(1)}, pred[1,1,384,384]{2,3,1,0:T(8,128)(4,1)}, u32[]{:S(2)}) copy-start(pred[1,1,384,384]{2,3,1,0:T(8,128)(4,1)} %copy-done.25) | copy-start | bytes 442372
  125.4 7.0 %copy-start.49 = (bf16[384,320]{0,1:T(8,128)(2,1)S(1)}, bf16[384,320]{0,1:T(8,128)(2,1)}, u32[]{:S(2)}) copy-start(bf16[384,320]{0,1:T(8,128)(2,1)} %get-tuple-element.450) | copy-start | bytes 737284
  125.4 7.0 %copy-start.50 = (f32[5,3,384]{2,1,0:T(4,128)S(1)}, f32[5,3,384]{2,1,0:T(4,128)}, u32[]{:S(2)}) copy-start(f32[5,3,384]{2,1,0:T(4,128)} %log_add_fusion) | copy-start | bytes 69124
  160.2 8.5 %copy-start.13 = (bf16[512,960]{1,0:T(8,128)(2,1)S(1)}, bf16[512,960]{1,0:T(8,128)(2,1)}, u32[]{:S(2)}) copy-start(bf16[512,960]{1,0:T(8,128)(2,1)} %reshape.720) | copy-start | bytes 2949124
  160.2 43.0 %collective-permute-start.2 = (f32[384,640]{0,1:T(8,128)S(1)}, f32[384,640]{0,1:T(8,128)S(1)}, u32[]{:S(2)}, u32[]{:S(2)}) collective-permute-start(f32[384,640]{0,1:T(8,128)S(1)} %get-tuple-element.442), channel_id=1, source_target_pairs={{3,0},{7,4},{11,8},{15,12},{19,16},{23,20},{27,24},{31,28},{35,32}... | collective-permute-start | bytes 2949128 | tf_op jit(solution)/shard_map/ppermute | solution.py:353
  161.6 41.6 %collective-permute-start.1 = (f32[384,640]{0,1:T(8,128)S(1)}, f32[384,640]{0,1:T(8,128)S(1)}, u32[]{:S(2)}, u32[]{:S(2)}) collective-permute-start(f32[384,640]{0,1:T(8,128)S(1)} %get-tuple-element.443), channel_id=1, source_target_pairs={{2,0},{3,1},{6,4},{7,5},{10,8},{11,9},{14,12},{15,13},{18,16},{19,... | collective-permute-start | bytes 2949128 | tf_op jit(solution)/shard_map/ppermute | solution.py:353
  162.9 40.3 %collective-permute-start = (f32[384,640]{0,1:T(8,128)S(1)}, f32[384,640]{0,1:T(8,128)S(1)}, u32[]{:S(2)}, u32[]{:S(2)}) collective-permute-start(f32[384,640]{0,1:T(8,128)S(1)} %get-tuple-element.441), channel_id=1, source_target_pairs={{1,0},{2,1},{3,2},{5,4},{6,5},{7,6},{9,8},{10,9},{11,10},{13,12},{... | collective-permute-start | bytes 2949128 | tf_op jit(solution)/shard_map/ppermute | solution.py:353
  176.4 29.7 %copy-start.17 = (bf16[512,320]{1,0:T(8,128)(2,1)S(1)}, bf16[512,320]{1,0:T(8,128)(2,1)}, u32[]{:S(2)}) copy-start(bf16[512,320]{1,0:T(8,128)(2,1)} %copy-done.16) | copy-start | bytes 983044
  (27 other events, 63.8 us)
Sparse Core Ops, SparseCore 0:
  68.8 29.4 all-gather.1
  214.6 195.3 all-reduce.2

commit v8 on v7

--- a/solution.py
+++ b/solution.py
@@ -363,8 +363,11 @@
     )
     value_gradient_batch = value_gradient.astype(jnp.bfloat16)
     g_query = jnp.dot(hidden_one.T, d_query_b, preferred_element_type=jnp.float32)
-    g_key = jnp.dot(hidden_one.T, key_gradient_batch, preferred_element_type=jnp.float32)
-    g_value = jnp.dot(hidden_one.T, value_gradient_batch, preferred_element_type=jnp.float32)
+    g_key_value = jnp.dot(
+        hidden_one.T,
+        jnp.concatenate([key_gradient_batch, value_gradient_batch], axis=1),
+        preferred_element_type=jnp.float32,
+    )
     d_hidden_one = (
         jnp.dot(d_query_b, w_query.T, preferred_element_type=jnp.float32)
         + jnp.dot(key_gradient_batch, w_key.T, preferred_element_type=jnp.float32)
@@ -377,21 +380,43 @@
         + inverse_one
         * (dn_one - normed_one * jnp.mean(dn_one * normed_one, axis=-1, keepdims=True))
     ).astype(jnp.bfloat16)
-    down_and_gains = jnp.concatenate([g_down, g_gain_one[None], g_gain_two[None]], axis=0)
+    out_and_gains = jnp.concatenate([g_out, g_gain_one[None], g_gain_two[None]], axis=0)
     grad_pieces = lax.psum(
-        (g_query, g_key, g_value, g_out, g_gate, g_up, down_and_gains), ("wide", "narrow")
-    )
+        (g_query, g_key_value, out_and_gains, g_gate, g_up, g_down), ("wide", "narrow")
+    )
+    out_rows = QUERY_HEADS * HEAD_SIZE
+    kv_width_total = KEYVAL_HEADS * HEAD_SIZE
+    flat_pieces = [
+        (0, 0, None),
+        (1, 0, kv_width_total),
+        (1, kv_width_total, kv_width_total),
+        (2, 0, out_rows),
+        (3, 0, None),
+        (4, 0, None),
+        (5, 0, None),
+        (2, out_rows, 2),
+    ]
 
     def shard_of(rank):
         def build(pieces):
             parts = []
             offset = 0
             low, high = rank * shard_len, (rank + 1) * shard_len
-            for piece in pieces:
-                size = piece.size
+            for index, column, width in flat_pieces:
+                piece = pieces[index]
+                if index == 2:
+                    piece = piece[column : column + width]
+                elif width is not None:
+                    piece = piece[:, column : column + width]
+                rows, cols = piece.shape
+                size = rows * cols
                 start, stop = max(low, offset), min(high, offset + size)
                 if start < stop:
-                    parts.append(piece.reshape(-1)[start - offset : stop - offset])
+                    first_row = (start - offset) // cols
+                    last_row = -(-(stop - offset) // cols)
+                    block = piece[first_row:last_row].reshape(-1)
+                    base = offset + first_row * cols
+                    parts.append(block[start - base : stop - base])
                 offset = offset + size
             return jnp.concatenate(parts)
 

time: 446 us -> 436 us (0.978)
  local copies, waits for them, and re-layouts: 59.5 us -> 50.8 us
    psum x1, waiting for transfers between devices: 190 us -> 182 us  [body(): lax.psum((g_query, g_key_value, out_and_gains, g_gate, g_up, g_down), ('w...]
    concatenate x1 -> x0, local copies, waits for them, and re-layouts: 7.35 us -> none  [body(): jnp.concatenate([g_down, g_gain_one[None], g_gain_two[None]], axis=0)]
    ppermute x3, waiting for transfers between devices: 26.8 us -> 32.1 us  [body(): lax.ppermute(sender_block, 'narrow', [(source, source - shift) for source...]
where the time goes in v8:
time: 436 us; the launch traced here: 430 us
  waiting for transfers between devices  214 us (49%)
  local copies, waits for them, and re-layouts  50.8 us (12%)
  matrix products  46.8 us (11%)
  Pallas kernels  44.2 us (10%)
  other arithmetic  33.9 us (8%)
  between operations  19.1 us (4%)
  loops' own time  14 us (3%)
  starting transfers between devices  6.66 us (2%)
    psum x1, waiting for transfers between devices, body(): lax.psum((g_query, g_key_value, out_and_gains, g_gate, g_up, g_down), ('w...  182 us
    pallas_call x1, Pallas kernels, gather_replica(): pl.pallas_call(gather_kernel, out_shape=jax.ShapeDtypeStruct((4, count, w...  44.2 us
    ppermute x3, waiting for transfers between devices, body(): lax.ppermute(sender_block, 'narrow', [(source, source - shift) for source...  32.1 us
    slice x5, local copies, waits for them, and re-layouts, unpack(): pieces.append(flat[offset:offset + length].reshape(layout))  14 us
    another operation x4, loops' own time, body(): lax.cond(needed, back_span, skip_span, query_gradient_running)  10.5 us
    sub x1, other arithmetic, body(): master - learn_rate * (first_hat / (jnp.sqrt(second_hat) + adam_eps) + de...  9.19 us
  transfers between devices with their start and end apart: 5, of which 2 were waited for; matrix products, arithmetic and copies ran while one was open for 9% of the time, Pallas kernels for 0%

profile of v8, /device:TPU:0, one launch (start us, length us, event | category | flops | bytes accessed | tf_op | source)
XLA Modules:
  0.0 429.7 jit_solution(5383735557595672180)
XLA Ops:
  7.2 3.3 convert_bitcast_fusion.src_ref
  10.5 44.2 %shard_map.109 = bf16[4,6402,128]{2,1,0:T(8,128)(2,1)} custom-call(bf16[6402,128]{1,0:T(8,128)(2,1)} %convert_bitcast_fusion.src_ref), custom_call_target="tpu_custom_call" | custom-call | tf_op jit(solution)/shard_map/pallas_call | solution.py:130
  54.7 7.3 %reshape.718 = bf16[3277824]{0:T(1024)(128)(2,1)} reshape(bf16[4,6402,128]{2,1,0:T(8,128)(2,1)} %shard_map.109) | data formatting | bytes 13111296 | tf_op jit(solution)/shard_map/reshape | solution.py:152
  68.9 2.9 fusion.189
  71.8 9.9 %slice.233 = bf16[6402,512]{1,0:T(8,128)(2,1)} reshape(bf16[4,6402,128]{2,1,0:T(8,128)(2,1)} %shard_map.109) | data formatting | bytes 13111296 | tf_op jit(solution)/shard_map/slice | solution.py:45
  90.2 3.9 reshape.730
  101.2 5.0 %conditional.13 = (f32[5,3,384]{2,1,0:T(4,128)}, f32[5,3,384]{2,1,0:T(4,128)S(1)}) conditional(s32[]{:T(128)} %bitcast.116, () %tuple.129, (pred[1,1,384,384]{2,3,1,0:T(8,128)(4,1)S(1)}, bf16[384,5,64]{0,2,1:T(8,128)(2,1)S(1)}, bf16[384,5,3,64]{0,3,2,1:T(8,128)(2,1)S(1)}) %tuple.269), branch_computations={%region_5.6_spmd, %region_6.9_spmd} | conditional | flops 298615680 | bytes 19157008 | solution.py:220
  106.2 3.0 conditional.16
  110.7 4.3 %conditional.17 = (f32[384,5,3,64]{0,3,2,1:T(8,128)S(1)}) conditional(s32[]{:T(128)} %bitcast.116, () %tuple.128, (pred[1,1,384,384]{2,3,1,0:T(8,128)(4,1)S(1)}, bf16[384,5,64]{0,2,1:T(8,128)(2,1)S(1)}, bf16[384,5,3,64]{0,3,2,1:T(8,128)(2,1)S(1)}, f32[5,3,384]{2,1,0:T(4,128)}, bf16[384,5,64]{0,2,1:T(8,128)(2,1)}) %tuple.284), branch_computations={%region_21.22_spmd, %region_22.23_spmd} | conditional | flops 575078400 | bytes 4446784 | solution.py:245
  111.4 3.6 fusion.32
  119.9 3.6 multiply_convert_fusion
  125.4 3.2 convolution_convert_fusion
  132.5 11.0 %conditional.21 = (f32[384,5,3,64]{0,3,2,1:T(8,128)S(1)}, f32[384,320]{0,1:T(8,128)S(1)}, f32[384,320]{0,1:T(8,128)S(1)}) conditional(s32[]{:T(128)} %bitcast.116, () %tuple.138, (pred[1,1,384,384]{2,3,1,0:T(8,128)(4,1)S(1)}, bf16[384,5,64]{0,2,1:T(8,128)(2,1)S(1)}, bf16[384,5,3,64]{0,3,2,1:T(8,128)(2,1)S(1)}, f32[5,3,384]{2,1,0:T(4,128)S(1)}, ...), branch_computations={%region_32.33_spmd, %region_33.34_spmd} | conditional | flops 1439907840 | bytes 46321176 | solution.py:340
  134.1 4.1 fusion.87
  140.6 2.9 fusion.91
  145.8 4.8 %conditional.23 = (f32[384,5,3,64]{0,3,2,1:T(8,128)S(1)}, f32[384,320]{0,1:T(8,128)S(1)}, f32[384,320]{0,1:T(8,128)S(1)}) conditional(s32[]{:T(128)} %bitcast.114, f32[384,5,3,64]{0,3,2,1:T(8,128)S(1)} %get-tuple-element.334, (pred[1,1,384,384]{2,3,1,0:T(8,128)(4,1)}, bf16[384,5,64]{0,2,1:T(8,128)(2,1)S(1)}, ...), branch_computations={%region_36.37_spmd, %region_37.38_spmd} | conditional | flops 1440276480 | bytes 49460844 | solution.py:340
  151.6 5.3 %conditional.24 = (f32[384,5,3,64]{0,3,2,1:T(8,128)S(1)}, f32[384,320]{0,1:T(8,128)S(1)}, f32[384,320]{0,1:T(8,128)S(1)}) conditional(s32[]{:T(128)} %bitcast.113, f32[384,5,3,64]{0,3,2,1:T(8,128)S(1)} %get-tuple-element.335, (pred[1,1,384,384]{2,3,1,0:T(8,128)(4,1)}, bf16[384,5,64]{0,2,1:T(8,128)(2,1)S(1)}, ...), branch_computations={%region_38.39_spmd, %region_39.40_spmd} | conditional | flops 1440276480 | bytes 49460844 | solution.py:340
  162.9 3.7 collective-permute-start
  176.7 32.1 %collective-permute-done.2 = f32[384,640]{0,1:T(8,128)S(1)} collective-permute-done((f32[384,640]{0,1:T(8,128)S(1)}, f32[384,640]{0,1:T(8,128)S(1)}, u32[]{:S(2)}, u32[]{:S(2)}) %collective-permute-start.2) | collective-permute-done | bytes 983072 | tf_op jit(solution)/shard_map/ppermute | solution.py:353
  214.7 3.0 fusion.145
  218.7 182.1 %all-reduce.3.cloned.1.call-done = (f32[512,960]{0,1:T(8,128)}, f32[512,640]{1,0:T(8,128)}, f32[962,512]{1,0:T(8,128)}, f32[512,1280]{1,0:T(8,128)}, f32[512,1280]{1,0:T(8,128)}, /*index=5*/f32[1280,512]{1,0:T(8,128)}) async-done(((f32[512,960]{0,1:T(8,128)}, f32[512,640]{1,0:T(8,128)}, f32[962,512]{1,0:T(8,128)}, f32[512,1280]{1,0:T(8,128)}, f32[512,1280]{1,0:T(8,128)}, /*index=5*/f32[1280,512]{1,0:T(8,128)}), ...) | async-done | bytes 13111312 | tf_op jit(solution)/shard_map/psum | solution.py:384
  400.8 12.7 %conditional.25 = (f32[819456]{0:T(1024)}) conditional(s32[]{:T(128)} %clamp.3, (f32[512,960]{0,1:T(8,128)}, f32[512,640]{1,0:T(8,128)}, f32[962,512]{1,0:T(8,128)}) %tuple.143, (f32[962,512]{1,0:T(8,128)}, f32[512,1280]{1,0:T(8,128)}) %tuple.144, (f32[512,1280]{1,0:T(8,128)}, f32[512,1280]{1,0:T(8,128)}) %tuple.145, ...), branch_computations={%region_49.50_spmd, %region_50.51_spmd, %region_51.52_spmd, %regio... | conditional | flops 2458368 | bytes 38695996 | solution.py:425
  409.8 3.7 pad_maximum_fusion
  413.5 9.2 %multiply_subtract_fusion = (f32[819456]{0:T(1024)}, f32[819456]{0:T(1024)}, f32[819456]{0:T(1024)}, f32[819456]{0:T(1024)}) fusion(f32[819456]{0:T(1024)} %param.37, s32[]{:T(128)S(6)} %mul.507, f32[819456]{0:T(1024)} %get-tuple-element.536, f32[819456]{0:T(1024)} %param.38, f32[819456]{0:T(1024)} %param.39), kind=kLoop, calls=%fused_computation.160 | loop fusion | flops 15569664 | bytes 26222596 | tf_op jit(solution)/shard_map/sub | solution.py:434
  (195 shorter events, 74.7 us)
Async XLA Ops:
  7.2 91.2 %all-gather.2.cloned.1.call-start = ((), (), s32[]{:S(2)}) async-start(), calls=%async_computation | async-start | bytes 2457600 | tf_op jit(solution)/shard_map/all_gather | solution.py:173
  54.7 9.2 %copy-start.55 = (s32[1,3]{1,0:T(1,128)S(1)}, s32[1,3]{1,0:T(1,128)}, u32[]{:S(2)}) copy-start(s32[1,3]{1,0:T(1,128)} %param.36) | copy-start | bytes 40
  54.7 10.5 %copy-start = (bf16[384,512]{1,0:T(8,128)(2,1)S(1)}, bf16[384,512]{1,0:T(8,128)(2,1)}, u32[]{:S(2)}) copy-start(bf16[384,512]{1,0:T(8,128)(2,1)} %param.34) | copy-start | bytes 1179652
  68.7 332.1 %all-reduce.3.cloned.1.call-start = ((), (), s32[]{:S(2)}) async-start(), calls=%async_computation.1 | async-start | bytes 26247168 | tf_op jit(solution)/shard_map/psum | solution.py:384
  71.8 15.0 %slice-start = ((bf16[3277824]{0:T(1024)(128)(2,1)}), bf16[491520]{0:T(1024)(128)(2,1)S(1)}, s32[]{:S(2)}) async-start(bf16[3277824]{0:T(1024)(128)(2,1)} %reshape.718), calls=%async_computation.2 | async-start | bytes 1966080 | tf_op jit(solution)/shard_map/slice | solution.py:45
  98.3 7.9 %copy-start.24 = (pred[1,1,384,384]{2,3,1,0:T(8,128)(4,1)}, pred[1,1,384,384]{2,3,1,0:T(8,128)(4,1)S(1)}, u32[]{:S(2)}) copy-start(pred[1,1,384,384]{2,3,1,0:T(8,128)(4,1)S(1)} %get-tuple-element.468) | copy-start | bytes 442372
  98.3 7.9 %copy-start.22 = (pred[1,1,384,384]{2,3,1,0:T(8,128)(4,1)}, pred[1,1,384,384]{2,3,1,0:T(8,128)(4,1)S(1)}, u32[]{:S(2)}) copy-start(pred[1,1,384,384]{2,3,1,0:T(8,128)(4,1)S(1)} %get-tuple-element.466) | copy-start | bytes 442372
  98.3 12.4 %copy-start.26 = (pred[1,1,384,384]{2,3,1,0:T(8,128)(4,1)}, pred[1,1,384,384]{2,3,1,0:T(8,128)(4,1)S(1)}, u32[]{:S(2)}) copy-start(pred[1,1,384,384]{2,3,1,0:T(8,128)(4,1)S(1)} %get-tuple-element.467) | copy-start | bytes 442372
  98.3 17.6 %copy-start.20 = (pred[1,1,384,384]{2,3,1,0:T(8,128)(4,1)}, pred[1,1,384,384]{2,3,1,0:T(8,128)(4,1)S(1)}, u32[]{:S(2)}) copy-start(pred[1,1,384,384]{2,3,1,0:T(8,128)(4,1)S(1)} %get-tuple-element.465) | copy-start | bytes 442372
  101.2 9.5 %copy-start.7 = (bf16[384,320]{0,1:T(8,128)(2,1)}, bf16[384,320]{0,1:T(8,128)(2,1)S(1)}, u32[]{:S(2)}) copy-start(bf16[384,320]{0,1:T(8,128)(2,1)S(1)} %get-tuple-element.452) | copy-start | bytes 737284
  101.2 13.8 %copy-start.5 = (bf16[384,320]{0,1:T(8,128)(2,1)}, bf16[384,320]{0,1:T(8,128)(2,1)S(1)}, u32[]{:S(2)}) copy-start(bf16[384,320]{0,1:T(8,128)(2,1)S(1)} %get-tuple-element.451) | copy-start | bytes 737284
  118.3 6.8 %copy-start.10 = (f32[384,512]{1,0:T(8,128)}, f32[384,512]{1,0:T(8,128)S(1)}, u32[]{:S(2)}) copy-start(f32[384,512]{1,0:T(8,128)S(1)} %get-tuple-element.475) | copy-start | bytes 2359300
  125.3 7.1 %copy-start.1 = (f32[384,512]{1,0:T(8,128)}, f32[384,512]{1,0:T(8,128)S(1)}, u32[]{:S(2)}) copy-start(f32[384,512]{1,0:T(8,128)S(1)} %multiply_add_fusion.6) | copy-start | bytes 2359300
  125.3 7.1 %copy-start.8 = (bf16[384,320]{0,1:T(8,128)(2,1)S(1)}, bf16[384,320]{0,1:T(8,128)(2,1)}, u32[]{:S(2)}) copy-start(bf16[384,320]{0,1:T(8,128)(2,1)} %copy-done.7) | copy-start | bytes 737284
  125.4 7.1 %copy-start.27 = (pred[1,1,384,384]{2,3,1,0:T(8,128)(4,1)S(1)}, pred[1,1,384,384]{2,3,1,0:T(8,128)(4,1)}, u32[]{:S(2)}) copy-start(pred[1,1,384,384]{2,3,1,0:T(8,128)(4,1)} %copy-done.26) | copy-start | bytes 442372
  125.4 7.1 %copy-start.49 = (bf16[384,320]{0,1:T(8,128)(2,1)S(1)}, bf16[384,320]{0,1:T(8,128)(2,1)}, u32[]{:S(2)}) copy-start(bf16[384,320]{0,1:T(8,128)(2,1)} %get-tuple-element.448) | copy-start | bytes 737284
  125.4 7.1 %copy-start.50 = (f32[5,3,384]{2,1,0:T(4,128)S(1)}, f32[5,3,384]{2,1,0:T(4,128)}, u32[]{:S(2)}) copy-start(f32[5,3,384]{2,1,0:T(4,128)} %log_add_fusion) | copy-start | bytes 69124
  159.9 6.7 %copy-start.44 = (f32[384,32]{0,1:T(8,128)S(1)}, f32[384,32]{0,1:T(8,128)}, u32[]{:S(2)}) copy-start(f32[384,32]{0,1:T(8,128)} %get-tuple-element.469) | copy-start | bytes 147460
  160.1 8.8 %copy-start.13 = (bf16[512,960]{1,0:T(8,128)(2,1)S(1)}, bf16[512,960]{1,0:T(8,128)(2,1)}, u32[]{:S(2)}) copy-start(bf16[512,960]{1,0:T(8,128)(2,1)} %reshape.722) | copy-start | bytes 2949124
  160.2 48.7 %collective-permute-start.2 = (f32[384,640]{0,1:T(8,128)S(1)}, f32[384,640]{0,1:T(8,128)S(1)}, u32[]{:S(2)}, u32[]{:S(2)}) collective-permute-start(f32[384,640]{0,1:T(8,128)S(1)} %get-tuple-element.440), channel_id=1, source_target_pairs={{3,0},{7,4},{11,8},{15,12},{19,16},{23,20},{27,24},{31,28},{35,32}... | collective-permute-start | bytes 2949128 | tf_op jit(solution)/shard_map/ppermute | solution.py:353
  161.6 47.2 %collective-permute-start.1 = (f32[384,640]{0,1:T(8,128)S(1)}, f32[384,640]{0,1:T(8,128)S(1)}, u32[]{:S(2)}, u32[]{:S(2)}) collective-permute-start(f32[384,640]{0,1:T(8,128)S(1)} %get-tuple-element.441), channel_id=1, source_target_pairs={{2,0},{3,1},{6,4},{7,5},{10,8},{11,9},{14,12},{15,13},{18,16},{19,... | collective-permute-start | bytes 2949128 | tf_op jit(solution)/shard_map/ppermute | solution.py:353
  162.9 45.9 %collective-permute-start = (f32[384,640]{0,1:T(8,128)S(1)}, f32[384,640]{0,1:T(8,128)S(1)}, u32[]{:S(2)}, u32[]{:S(2)}) collective-permute-start(f32[384,640]{0,1:T(8,128)S(1)} %get-tuple-element.439), channel_id=1, source_target_pairs={{1,0},{2,1},{3,2},{5,4},{6,5},{7,6},{9,8},{10,9},{11,10},{13,12},{... | collective-permute-start | bytes 2949128 | tf_op jit(solution)/shard_map/ppermute | solution.py:353
  176.7 32.5 %copy-start.17 = (bf16[512,320]{1,0:T(8,128)(2,1)S(1)}, bf16[512,320]{1,0:T(8,128)(2,1)}, u32[]{:S(2)}) copy-start(bf16[512,320]{1,0:T(8,128)(2,1)} %copy-done.16) | copy-start | bytes 983044
  176.7 32.9 %copy-start.38 = (bf16[512,320]{1,0:T(8,128)(2,1)S(1)}, bf16[512,320]{1,0:T(8,128)(2,1)}, u32[]{:S(2)}) copy-start(bf16[512,320]{1,0:T(8,128)(2,1)} %copy-done.37) | copy-start | bytes 983044
  (27 other events, 65.4 us)
Sparse Core Ops, SparseCore 0:
  68.8 29.4 all-gather.1
  213.7 187.0 all-reduce.2

commit v9 on v8

--- a/solution.py
+++ b/solution.py
@@ -422,17 +422,31 @@
 
         return build
 
-    summed = lax.switch(narrow_rank, [shard_of(rank) for rank in range(narrow_size)], grad_pieces)
     token_total = token_rows * narrow_size * lax.axis_size("wide")
-    gradient = summed * (1.0 / math.sqrt(token_total))
-    new_first = beta_one * first_moment + (1.0 - beta_one) * gradient
-    new_second = beta_two * second_moment + (1.0 - beta_two) * gradient * gradient
-    first_hat = new_first / (1.0 - beta_one**STEP)
-    second_hat = new_second / (1.0 - beta_two**STEP)
-    entry_index = narrow_rank * shard_len + jnp.arange(shard_len, dtype=jnp.int32)
-    decay = jnp.where(entry_index < NPARAM - 2 * MODEL_WIDTH, decay_rate, 0.0)
-    new_master = master - learn_rate * (
-        first_hat / (jnp.sqrt(second_hat) + adam_eps) + decay * master
+
+    def update_of(rank):
+        def update(pieces, master, first_moment, second_moment):
+            gradient = shard_of(rank)(pieces) * (1.0 / math.sqrt(token_total))
+            new_first = beta_one * first_moment + (1.0 - beta_one) * gradient
+            new_second = beta_two * second_moment + (1.0 - beta_two) * gradient * gradient
+            first_hat = new_first / (1.0 - beta_one**STEP)
+            second_hat = new_second / (1.0 - beta_two**STEP)
+            entry_index = rank * shard_len + jnp.arange(shard_len, dtype=jnp.int32)
+            decay = jnp.where(entry_index < NPARAM - 2 * MODEL_WIDTH, decay_rate, 0.0)
+            new_master = master - learn_rate * (
+                first_hat / (jnp.sqrt(second_hat) + adam_eps) + decay * master
+            )
+            return (gradient, new_master, new_first, new_second)
+
+        return update
+
+    gradient, new_master, new_first, new_second = lax.switch(
+        narrow_rank,
+        [update_of(rank) for rank in range(narrow_size)],
+        grad_pieces,
+        master,
+        first_moment,
+        second_moment,
     )
     return (output, d_tokens, gradient, new_master, new_first, new_second)
 

time: 436 us -> 443 us (1.016)
  waiting for transfers between devices: 214 us -> 222 us
  other arithmetic: 33.9 us -> 28.1 us
  local copies, waits for them, and re-layouts: 50.8 us -> 56.1 us
  transfers between devices with their start and end apart: 5 -> 5, of which waited for: 2 -> 4; matrix products, arithmetic and copies ran while one was open for 9% -> 9% of each run, Pallas kernels for 0% -> 0%
where the time goes in v9:
time: 443 us; the launch traced here: 436 us
  waiting for transfers between devices  222 us (50%)
  local copies, waits for them, and re-layouts  56.1 us (13%)
  matrix products  45.4 us (10%)
  Pallas kernels  44.2 us (10%)
  other arithmetic  28.1 us (6%)
  between operations  19.1 us (4%)
  loops' own time  14.7 us (3%)
  starting transfers between devices  6.77 us (2%)
    psum x1, waiting for transfers between devices, body(): lax.psum((g_query, g_key_value, out_and_gains, g_gate, g_up, g_down), ('w...  186 us
    pallas_call x1, Pallas kernels, gather_replica(): pl.pallas_call(gather_kernel, out_shape=jax.ShapeDtypeStruct((4, count, w...  44.2 us
    ppermute x3, waiting for transfers between devices, body(): lax.ppermute(sender_block, 'narrow', [(source, source - shift) for source...  35.7 us
    slice x5, local copies, waits for them, and re-layouts, unpack(): pieces.append(flat[offset:offset + length].reshape(layout))  14.3 us
    another operation x4, loops' own time, body(): lax.cond(needed, back_span, skip_span, query_gradient_running)  11 us
    sub x1, other arithmetic, update(): master - learn_rate * (first_hat / (jnp.sqrt(second_hat) + adam_eps) + de...  9.79 us
    reshape x5, local copies, waits for them, and re-layouts, unpack(): pieces.append(flat[offset:offset + length].reshape(layout))  9.21 us
  transfers between devices with their start and end apart: 5, of which 4 were waited for; matrix products, arithmetic and copies ran while one was open for 9% of the time, Pallas kernels for 0%

profile of v9, /device:TPU:0, one launch (start us, length us, event | category | flops | bytes accessed | tf_op | source)
XLA Modules:
  0.0 436.4 jit_solution(15412244105035123933)
XLA Ops:
  7.2 3.3 convert_bitcast_fusion.src_ref
  10.5 44.2 %shard_map.109 = bf16[4,6402,128]{2,1,0:T(8,128)(2,1)} custom-call(bf16[6402,128]{1,0:T(8,128)(2,1)} %convert_bitcast_fusion.src_ref), custom_call_target="tpu_custom_call" | custom-call | tf_op jit(solution)/shard_map/pallas_call | solution.py:130
  54.7 7.2 %reshape.718 = bf16[3277824]{0:T(1024)(128)(2,1)} reshape(bf16[4,6402,128]{2,1,0:T(8,128)(2,1)} %shard_map.109) | data formatting | bytes 13111296 | tf_op jit(solution)/shard_map/reshape | solution.py:152
  68.3 3.4 fusion.193
  71.7 9.8 %slice.233 = bf16[6402,512]{1,0:T(8,128)(2,1)} reshape(bf16[4,6402,128]{2,1,0:T(8,128)(2,1)} %shard_map.109) | data formatting | bytes 13111296 | tf_op jit(solution)/shard_map/slice | solution.py:45
  86.6 3.8 reshape.730
  91.8 3.8 reshape.731
  100.5 5.0 %conditional.13 = (f32[5,3,384]{2,1,0:T(4,128)}, f32[5,3,384]{2,1,0:T(4,128)S(1)}) conditional(s32[]{:T(128)} %bitcast.116, () %tuple.133, (pred[1,1,384,384]{2,3,1,0:T(8,128)(4,1)S(1)}, bf16[384,5,64]{0,2,1:T(8,128)(2,1)S(1)}, bf16[384,5,3,64]{0,3,2,1:T(8,128)(2,1)S(1)}) %tuple.286), branch_computations={%region_5.6_spmd, %region_6.9_spmd} | conditional | flops 298615680 | bytes 19157008 | solution.py:220
  105.5 3.1 conditional.16
  110.0 4.3 conditional.17
  110.7 3.6 fusion.32
  119.8 3.6 multiply_convert_fusion
  130.3 9.6 %conditional.21 = (f32[384,5,3,64]{0,3,2,1:T(8,128)S(1)}, f32[384,320]{0,1:T(8,128)S(1)}, f32[384,320]{0,1:T(8,128)S(1)}) conditional(s32[]{:T(128)} %bitcast.116, () %tuple.142, (pred[1,1,384,384]{2,3,1,0:T(8,128)(4,1)S(1)}, bf16[384,5,64]{0,2,1:T(8,128)(2,1)S(1)}, bf16[384,5,3,64]{0,3,2,1:T(8,128)(2,1)S(1)}, f32[5,3,384]{2,1,0:T(4,128)S(1)}, ...), branch_computations={%region_32.33_spmd, %region_33.34_spmd} | conditional | flops 1439907840 | bytes 46321176 | solution.py:340
  133.7 3.7 fusion.87
  142.2 4.8 %conditional.23 = (f32[384,5,3,64]{0,3,2,1:T(8,128)S(1)}, f32[384,320]{0,1:T(8,128)S(1)}, f32[384,320]{0,1:T(8,128)S(1)}) conditional(s32[]{:T(128)} %bitcast.114, f32[384,5,3,64]{0,3,2,1:T(8,128)S(1)} %get-tuple-element.369, (pred[1,1,384,384]{2,3,1,0:T(8,128)(4,1)}, bf16[384,5,64]{0,2,1:T(8,128)(2,1)S(1)}, ...), branch_computations={%region_36.37_spmd, %region_37.38_spmd} | conditional | flops 1440276480 | bytes 52409992 | solution.py:340
  148.0 5.8 %conditional.24 = (f32[384,5,3,64]{0,3,2,1:T(8,128)S(1)}, f32[384,320]{0,1:T(8,128)S(1)}, f32[384,320]{0,1:T(8,128)S(1)}) conditional(s32[]{:T(128)} %bitcast.113, f32[384,5,3,64]{0,3,2,1:T(8,128)S(1)} %get-tuple-element.370, (pred[1,1,384,384]{2,3,1,0:T(8,128)(4,1)}, bf16[384,5,64]{0,2,1:T(8,128)(2,1)S(1)}, ...), branch_computations={%region_38.39_spmd, %region_39.40_spmd} | conditional | flops 1440276480 | bytes 52409992 | solution.py:340
  159.8 3.8 collective-permute-start.1
  171.4 3.0 collective-permute-done
  174.4 32.7 %collective-permute-done.2 = f32[384,640]{0,1:T(8,128)S(1)} collective-permute-done((f32[384,640]{0,1:T(8,128)S(1)}, f32[384,640]{0,1:T(8,128)S(1)}, u32[]{:S(2)}, u32[]{:S(2)}) %collective-permute-start.2) | collective-permute-done | bytes 983072 | tf_op jit(solution)/shard_map/ppermute | solution.py:353
  213.0 3.4 fusion.147
  218.8 186.1 %all-reduce.3.cloned.1.call-done = (f32[512,960]{0,1:T(8,128)}, f32[512,640]{1,0:T(8,128)}, f32[962,512]{1,0:T(8,128)}, f32[512,1280]{1,0:T(8,128)}, f32[512,1280]{1,0:T(8,128)}, /*index=5*/f32[1280,512]{1,0:T(8,128)}) async-done(((f32[512,960]{0,1:T(8,128)}, f32[512,640]{1,0:T(8,128)}, f32[962,512]{1,0:T(8,128)}, f32[512,1280]{1,0:T(8,128)}, f32[512,1280]{1,0:T(8,128)}, /*index=5*/f32[1280,512]{1,0:T(8,128)}), ...) | async-done | bytes 13111312 | tf_op jit(solution)/shard_map/psum | solution.py:384
  404.9 24.3 %conditional.25 = (f32[819456]{0:T(1024)}, f32[819456]{0:T(1024)}, f32[819456]{0:T(1024)}, f32[819456]{0:T(1024)}) conditional(s32[]{:T(128)} %clamp.3, (f32[512,960]{0,1:T(8,128)}, f32[512,640]{1,0:T(8,128)}, f32[962,512]{1,0:T(8,128)}, f32[819456]{0:T(1024)}, f32[819456]{0:T(1024)}, ...), branch_computations={%region_49.50_spmd, %region_50.51_spmd, %region_51.52_spmd, %regio... | conditional | flops 17208576 | bytes 69503064 | solution.py:443
  416.0 3.2 reshape.686
  419.2 9.8 %multiply_subtract_fusion = (f32[819456]{0:T(1024)}, f32[819456]{0:T(1024)}, f32[819456]{0:T(1024)}, f32[819456]{0:T(1024)}) fusion(f32[819456]{0:T(1024)S(1)} %get-tuple-element.311, f32[256]{0:T(256)S(1)} %bitcast.574, f32[163840]{0:T(1024)} %reshape.688, f32[163840]{0:T(1024)} %reshape.687, f32[491520]{0:T(1024)} %reshape.686, ...), kind=kLoop, calls=%fused_computation.154 | loop fusion | flops 17208576 | bytes 26222592 | tf_op jit(solution)/shard_map/cond/branch_0_fun/sub | solution.py:436
  (202 shorter events, 74.6 us)
Async XLA Ops:
  7.2 90.6 %all-gather.2.cloned.1.call-start = ((), (), s32[]{:S(2)}) async-start(), calls=%async_computation | async-start | bytes 2457600 | tf_op jit(solution)/shard_map/all_gather | solution.py:173
  54.7 9.1 %copy-start.67 = (s32[1,3]{1,0:T(1,128)S(1)}, s32[1,3]{1,0:T(1,128)}, u32[]{:S(2)}) copy-start(s32[1,3]{1,0:T(1,128)} %param.36) | copy-start | bytes 40
  54.7 9.3 %copy-start.4 = (bf16[384,512]{1,0:T(8,128)(2,1)S(1)}, bf16[384,512]{1,0:T(8,128)(2,1)}, u32[]{:S(2)}) copy-start(bf16[384,512]{1,0:T(8,128)(2,1)} %param.34) | copy-start | bytes 1179652
  65.3 6.4 %copy-start.50 = (bf16[512,320]{1,0:T(8,128)(2,1)}, bf16[512,320]{1,0:T(8,128)(2,1)S(1)}, u32[]{:S(2)}) copy-start(bf16[512,320]{1,0:T(8,128)(2,1)S(1)} %reshape.720) | copy-start | bytes 983044
  68.1 336.8 %all-reduce.3.cloned.1.call-start = ((), (), s32[]{:S(2)}) async-start(), calls=%async_computation.1 | async-start | bytes 26247168 | tf_op jit(solution)/shard_map/psum | solution.py:384
  81.5 8.9 %slice-start = ((bf16[3277824]{0:T(1024)(128)(2,1)}), bf16[491520]{0:T(1024)(128)(2,1)S(1)}, s32[]{:S(2)}) async-start(bf16[3277824]{0:T(1024)(128)(2,1)} %reshape.718), calls=%async_computation.2 | async-start | bytes 1966080 | tf_op jit(solution)/shard_map/slice | solution.py:45
  91.3 5.2 %copy-start.17 = (bf16[512,960]{1,0:T(8,128)(2,1)}, bf16[512,960]{1,0:T(8,128)(2,1)S(1)}, u32[]{:S(2)}) copy-start(bf16[512,960]{1,0:T(8,128)(2,1)S(1)} %reshape.722) | copy-start | bytes 2949124
  97.6 7.9 %copy-start.33 = (pred[1,1,384,384]{2,3,1,0:T(8,128)(4,1)}, pred[1,1,384,384]{2,3,1,0:T(8,128)(4,1)S(1)}, u32[]{:S(2)}) copy-start(pred[1,1,384,384]{2,3,1,0:T(8,128)(4,1)S(1)} %get-tuple-element.528) | copy-start | bytes 442372
  97.6 7.9 %copy-start.31 = (pred[1,1,384,384]{2,3,1,0:T(8,128)(4,1)}, pred[1,1,384,384]{2,3,1,0:T(8,128)(4,1)S(1)}, u32[]{:S(2)}) copy-start(pred[1,1,384,384]{2,3,1,0:T(8,128)(4,1)S(1)} %get-tuple-element.526) | copy-start | bytes 442372
  97.6 12.4 %copy-start.35 = (pred[1,1,384,384]{2,3,1,0:T(8,128)(4,1)}, pred[1,1,384,384]{2,3,1,0:T(8,128)(4,1)S(1)}, u32[]{:S(2)}) copy-start(pred[1,1,384,384]{2,3,1,0:T(8,128)(4,1)S(1)} %get-tuple-element.527) | copy-start | bytes 442372
  97.6 17.7 %copy-start.29 = (pred[1,1,384,384]{2,3,1,0:T(8,128)(4,1)}, pred[1,1,384,384]{2,3,1,0:T(8,128)(4,1)S(1)}, u32[]{:S(2)}) copy-start(pred[1,1,384,384]{2,3,1,0:T(8,128)(4,1)S(1)} %get-tuple-element.525) | copy-start | bytes 442372
  100.5 9.5 %copy-start.12 = (bf16[384,320]{0,1:T(8,128)(2,1)}, bf16[384,320]{0,1:T(8,128)(2,1)S(1)}, u32[]{:S(2)}) copy-start(bf16[384,320]{0,1:T(8,128)(2,1)S(1)} %get-tuple-element.512) | copy-start | bytes 737284
  100.5 13.8 %copy-start.10 = (bf16[384,320]{0,1:T(8,128)(2,1)}, bf16[384,320]{0,1:T(8,128)(2,1)S(1)}, u32[]{:S(2)}) copy-start(bf16[384,320]{0,1:T(8,128)(2,1)S(1)} %get-tuple-element.511) | copy-start | bytes 737284
  117.5 7.5 %copy-start.15 = (f32[384,512]{1,0:T(8,128)}, f32[384,512]{1,0:T(8,128)S(1)}, u32[]{:S(2)}) copy-start(f32[384,512]{1,0:T(8,128)S(1)} %get-tuple-element.535) | copy-start | bytes 2359300
  125.3 5.0 %copy-start.6 = (f32[384,512]{1,0:T(8,128)}, f32[384,512]{1,0:T(8,128)S(1)}, u32[]{:S(2)}) copy-start(f32[384,512]{1,0:T(8,128)S(1)} %multiply_add_fusion.12) | copy-start | bytes 2359300
  147.0 6.8 %copy-start.57 = (f32[384,32]{0,1:T(8,128)S(1)}, f32[384,32]{0,1:T(8,128)}, u32[]{:S(2)}) copy-start(f32[384,32]{0,1:T(8,128)} %get-tuple-element.529) | copy-start | bytes 147460
  156.9 6.8 %copy-start.18 = (bf16[512,960]{1,0:T(8,128)(2,1)S(1)}, bf16[512,960]{1,0:T(8,128)(2,1)}, u32[]{:S(2)}) copy-start(bf16[512,960]{1,0:T(8,128)(2,1)} %copy-done.17) | copy-start | bytes 2949124
  156.9 7.4 %copy-start.20 = (bf16[384,1280]{1,0:T(8,128)(2,1)S(1)}, bf16[384,1280]{1,0:T(8,128)(2,1)}, u32[]{:S(2)}) copy-start(bf16[384,1280]{1,0:T(8,128)(2,1)} %copy-done.19) | copy-start | bytes 2949124
  157.1 17.3 %collective-permute-start = (f32[384,640]{0,1:T(8,128)S(1)}, f32[384,640]{0,1:T(8,128)S(1)}, u32[]{:S(2)}, u32[]{:S(2)}) collective-permute-start(f32[384,640]{0,1:T(8,128)S(1)} %get-tuple-element.499), channel_id=1, source_target_pairs={{1,0},{2,1},{3,2},{5,4},{6,5},{7,6},{9,8},{10,9},{11,10},{13,12},{... | collective-permute-start | bytes 2949128 | tf_op jit(solution)/shard_map/ppermute | solution.py:353
  158.5 48.6 %collective-permute-start.2 = (f32[384,640]{0,1:T(8,128)S(1)}, f32[384,640]{0,1:T(8,128)S(1)}, u32[]{:S(2)}, u32[]{:S(2)}) collective-permute-start(f32[384,640]{0,1:T(8,128)S(1)} %get-tuple-element.500), channel_id=1, source_target_pairs={{3,0},{7,4},{11,8},{15,12},{19,16},{23,20},{27,24},{31,28},{35,32}... | collective-permute-start | bytes 2949128 | tf_op jit(solution)/shard_map/ppermute | solution.py:353
  159.8 47.3 %collective-permute-start.1 = (f32[384,640]{0,1:T(8,128)S(1)}, f32[384,640]{0,1:T(8,128)S(1)}, u32[]{:S(2)}, u32[]{:S(2)}) collective-permute-start(f32[384,640]{0,1:T(8,128)S(1)} %get-tuple-element.501), channel_id=1, source_target_pairs={{2,0},{3,1},{6,4},{7,5},{10,8},{11,9},{14,12},{15,13},{18,16},{19,... | collective-permute-start | bytes 2949128 | tf_op jit(solution)/shard_map/ppermute | solution.py:353
  171.4 36.1 %copy-start.22 = (bf16[512,320]{1,0:T(8,128)(2,1)S(1)}, bf16[512,320]{1,0:T(8,128)(2,1)}, u32[]{:S(2)}) copy-start(bf16[512,320]{1,0:T(8,128)(2,1)} %copy-done.21) | copy-start | bytes 983044
  207.5 4.0 copy-start.8
  213.0 191.9 %copy-start = (f32[819456]{0:T(1024)S(1)}, f32[819456]{0:T(1024)}, u32[]{:S(2)}) copy-start(f32[819456]{0:T(1024)} %param.37) | copy-start | bytes 9833476
  (31 other events, 59.7 us)
Sparse Core Ops, SparseCore 0:
  68.2 29.4 all-gather.1
  213.1 191.7 all-reduce.2

commit v10 on v8

--- a/solution.py
+++ b/solution.py
@@ -351,10 +351,10 @@
     for shift in range(1, narrow_size):
         sender_block = kv_sum_in[lax.rem(narrow_rank + narrow_size - shift, narrow_size)]
         kv_grad = kv_grad + lax.ppermute(
-            sender_block,
+            sender_block.astype(jnp.bfloat16),
             "narrow",
             [(source, source - shift) for source in range(shift, narrow_size)],
-        )
+        ).astype(jnp.float32)
     key_gradient, value_gradient = kv_grad[:, :kv_width], kv_grad[:, kv_width:]
     d_query = query_gradient_running.reshape(token_rows, QUERY_HEADS * HEAD_SIZE)
     d_query_b = apply_rotary(d_query, token_position, QUERY_HEADS, -1.0).astype(jnp.bfloat16)

time: 436 us -> 418 us (0.959)
  waiting for transfers between devices: 214 us -> 204 us
    psum x1, waiting for transfers between devices: 182 us -> 173 us  [body(): lax.psum((g_query, g_key_value, out_and_gains, g_gate, g_up, g_down), ('w...]
  transfers between devices with their start and end apart: 5 -> 5, of which waited for: 2 -> 2; matrix products, arithmetic and copies ran while one was open for 9% -> 8% of each run, Pallas kernels for 0% -> 0%
where the time goes in v10:
time: 418 us; the launch traced here: 414 us
  waiting for transfers between devices  204 us (49%)
  local copies, waits for them, and re-layouts  49.9 us (12%)
  Pallas kernels  44.2 us (11%)
  matrix products  44 us (11%)
  other arithmetic  32.3 us (8%)
  between operations  19 us (5%)
  loops' own time  13.9 us (3%)
  starting transfers between devices  5.99 us (1%)
    psum x1, waiting for transfers between devices, body(): lax.psum((g_query, g_key_value, out_and_gains, g_gate, g_up, g_down), ('w...  173 us
    pallas_call x1, Pallas kernels, gather_replica(): pl.pallas_call(gather_kernel, out_shape=jax.ShapeDtypeStruct((4, count, w...  44.2 us
    ppermute x3, waiting for transfers between devices, body(): lax.ppermute(sender_block.astype(jnp.bfloat16), 'narrow', [(source, sourc...  31.4 us
    slice x5, local copies, waits for them, and re-layouts, unpack(): pieces.append(flat[offset:offset + length].reshape(layout))  13.9 us
    another operation x4, loops' own time, body(): lax.cond(needed, back_span, skip_span, query_gradient_running)  10.4 us
    sub x1, other arithmetic, body(): master - learn_rate * (first_hat / (jnp.sqrt(second_hat) + adam_eps) + de...  9.19 us
    reshape x5, local copies, waits for them, and re-layouts, unpack(): pieces.append(flat[offset:offset + length].reshape(layout))  8.71 us
  transfers between devices with their start and end apart: 5, of which 2 were waited for; matrix products, arithmetic and copies ran while one was open for 8% of the time, Pallas kernels for 0%

profile of v10, /device:TPU:0, one launch (start us, length us, event | category | flops | bytes accessed | tf_op | source)
XLA Modules:
  0.0 413.7 jit_solution(2765867799506669354)
XLA Ops:
  7.2 3.3 convert_bitcast_fusion.src_ref
  10.5 44.2 %shard_map.109 = bf16[4,6402,128]{2,1,0:T(8,128)(2,1)} custom-call(bf16[6402,128]{1,0:T(8,128)(2,1)} %convert_bitcast_fusion.src_ref), custom_call_target="tpu_custom_call" | custom-call | tf_op jit(solution)/shard_map/pallas_call | solution.py:130
  54.7 7.3 %reshape.721 = bf16[3277824]{0:T(1024)(128)(2,1)} reshape(bf16[4,6402,128]{2,1,0:T(8,128)(2,1)} %shard_map.109) | data formatting | bytes 13111296 | tf_op jit(solution)/shard_map/reshape | solution.py:152
  68.6 2.9 fusion.192
  71.6 9.9 %slice.233 = bf16[6402,512]{1,0:T(8,128)(2,1)} reshape(bf16[4,6402,128]{2,1,0:T(8,128)(2,1)} %shard_map.109) | data formatting | bytes 13111296 | tf_op jit(solution)/shard_map/slice | solution.py:45
  89.9 3.8 reshape.733
  98.1 2.8 fusion.194
  100.9 4.9 %conditional.13 = (f32[5,3,384]{2,1,0:T(4,128)}, f32[5,3,384]{2,1,0:T(4,128)S(1)}) conditional(s32[]{:T(128)} %bitcast.116, () %tuple.129, (pred[1,1,384,384]{2,3,1,0:T(8,128)(4,1)S(1)}, bf16[384,5,64]{0,2,1:T(8,128)(2,1)S(1)}, bf16[384,5,3,64]{0,3,2,1:T(8,128)(2,1)S(1)}) %tuple.269), branch_computations={%region_5.6_spmd, %region_6.9_spmd} | conditional | flops 298615680 | bytes 19157008 | solution.py:220
  103.2 2.6 fusion.3
  105.9 2.9 conditional.16
  110.1 4.3 %conditional.17 = (f32[384,5,3,64]{0,3,2,1:T(8,128)S(1)}) conditional(s32[]{:T(128)} %bitcast.116, () %tuple.128, (pred[1,1,384,384]{2,3,1,0:T(8,128)(4,1)S(1)}, bf16[384,5,64]{0,2,1:T(8,128)(2,1)S(1)}, bf16[384,5,3,64]{0,3,2,1:T(8,128)(2,1)S(1)}, f32[5,3,384]{2,1,0:T(4,128)}, bf16[384,5,64]{0,2,1:T(8,128)(2,1)}) %tuple.287), branch_computations={%region_21.22_spmd, %region_22.23_spmd} | conditional | flops 575078400 | bytes 4446784 | solution.py:245
  110.9 3.6 fusion.32
  119.6 3.5 multiply_convert_fusion
  134.4 9.5 %conditional.21 = (f32[384,5,3,64]{0,3,2,1:T(8,128)S(1)}, f32[384,320]{0,1:T(8,128)S(1)}, f32[384,320]{0,1:T(8,128)S(1)}) conditional(s32[]{:T(128)} %bitcast.116, () %tuple.138, (pred[1,1,384,384]{2,3,1,0:T(8,128)(4,1)S(1)}, bf16[384,5,64]{0,2,1:T(8,128)(2,1)S(1)}, bf16[384,5,3,64]{0,3,2,1:T(8,128)(2,1)S(1)}, f32[5,3,384]{2,1,0:T(4,128)S(1)}, ...), branch_computations={%region_32.33_spmd, %region_33.34_spmd} | conditional | flops 1439907840 | bytes 46321176 | solution.py:340
  136.0 3.7 fusion.87
  146.2 4.6 %conditional.23 = (f32[384,5,3,64]{0,3,2,1:T(8,128)S(1)}, f32[384,320]{0,1:T(8,128)S(1)}, f32[384,320]{0,1:T(8,128)S(1)}) conditional(s32[]{:T(128)} %bitcast.114, f32[384,5,3,64]{0,3,2,1:T(8,128)S(1)} %get-tuple-element.334, (pred[1,1,384,384]{2,3,1,0:T(8,128)(4,1)}, bf16[384,5,64]{0,2,1:T(8,128)(2,1)}, bf16[384,5,3,64]{0,3,2,1:T(8,128)(2,1)S(1)}, ...), branch_computations={%region_36.37_spmd, %region_37.38_spmd} | conditional | flops 1440276480 | bytes 53393060 | solution.py:340
  151.8 5.4 %conditional.24 = (f32[384,5,3,64]{0,3,2,1:T(8,128)S(1)}, f32[384,320]{0,1:T(8,128)S(1)}, f32[384,320]{0,1:T(8,128)S(1)}) conditional(s32[]{:T(128)} %bitcast.113, f32[384,5,3,64]{0,3,2,1:T(8,128)S(1)} %get-tuple-element.335, (pred[1,1,384,384]{2,3,1,0:T(8,128)(4,1)S(1)}, bf16[384,5,64]{0,2,1:T(8,128)(2,1)}, ...), branch_computations={%region_38.39_spmd, %region_39.40_spmd} | conditional | flops 1440276480 | bytes 52803208 | solution.py:340
  163.2 2.7 collective-permute-start
  171.4 31.4 %collective-permute-done.2 = bf16[384,640]{0,1:T(8,128)(2,1)S(1)} collective-permute-done((bf16[384,640]{0,1:T(8,128)(2,1)S(1)}, bf16[384,640]{0,1:T(8,128)(2,1)S(1)}, u32[]{:S(2)}, u32[]{:S(2)}) %collective-permute-start.2) | collective-permute-done | bytes 491552 | tf_op jit(solution)/shard_map/ppermute | solution.py:353
  208.7 3.0 fusion.145
  212.7 173.0 %all-reduce.3.cloned.1.call-done = (f32[512,960]{0,1:T(8,128)}, f32[512,640]{1,0:T(8,128)}, f32[962,512]{1,0:T(8,128)}, f32[512,1280]{1,0:T(8,128)}, f32[512,1280]{1,0:T(8,128)}, /*index=5*/f32[1280,512]{1,0:T(8,128)}) async-done(((f32[512,960]{0,1:T(8,128)}, f32[512,640]{1,0:T(8,128)}, f32[962,512]{1,0:T(8,128)}, f32[512,1280]{1,0:T(8,128)}, f32[512,1280]{1,0:T(8,128)}, /*index=5*/f32[1280,512]{1,0:T(8,128)}), ...) | async-done | bytes 13111312 | tf_op jit(solution)/shard_map/psum | solution.py:384
  385.7 11.8 %conditional.25 = (f32[819456]{0:T(1024)}) conditional(s32[]{:T(128)} %clamp.3, (f32[512,960]{0,1:T(8,128)}, f32[512,640]{1,0:T(8,128)}, f32[962,512]{1,0:T(8,128)}) %tuple.143, (f32[962,512]{1,0:T(8,128)}, f32[512,1280]{1,0:T(8,128)}) %tuple.144, (f32[512,1280]{1,0:T(8,128)}, f32[512,1280]{1,0:T(8,128)}) %tuple.145, ...), branch_computations={%region_49.50_spmd, %region_50.51_spmd, %region_51.52_spmd, %regio... | conditional | flops 2458368 | bytes 38695996 | solution.py:425
  393.8 3.7 pad_maximum_fusion
  397.5 9.2 %multiply_subtract_fusion = (f32[819456]{0:T(1024)}, f32[819456]{0:T(1024)}, f32[819456]{0:T(1024)}, f32[819456]{0:T(1024)}) fusion(f32[819456]{0:T(1024)} %param.37, s32[]{:T(128)S(6)} %mul.507, f32[819456]{0:T(1024)} %get-tuple-element.536, f32[819456]{0:T(1024)} %param.38, f32[819456]{0:T(1024)} %param.39), kind=kLoop, calls=%fused_computation.160 | loop fusion | flops 15569664 | bytes 26222596 | tf_op jit(solution)/shard_map/sub | solution.py:434
  (187 shorter events, 70.9 us)
Async XLA Ops:
  7.2 90.9 %all-gather.2.cloned.1.call-start = ((), (), s32[]{:S(2)}) async-start(), calls=%async_computation | async-start | bytes 2457600 | tf_op jit(solution)/shard_map/all_gather | solution.py:173
  54.7 9.2 %copy-start.56 = (s32[1,3]{1,0:T(1,128)S(1)}, s32[1,3]{1,0:T(1,128)}, u32[]{:S(2)}) copy-start(s32[1,3]{1,0:T(1,128)} %param.36) | copy-start | bytes 40
  54.7 9.9 %copy-start = (bf16[384,512]{1,0:T(8,128)(2,1)S(1)}, bf16[384,512]{1,0:T(8,128)(2,1)}, u32[]{:S(2)}) copy-start(bf16[384,512]{1,0:T(8,128)(2,1)} %param.34) | copy-start | bytes 1179652
  64.6 6.9 %copy-start.39 = (bf16[512,320]{1,0:T(8,128)(2,1)}, bf16[512,320]{1,0:T(8,128)(2,1)S(1)}, u32[]{:S(2)}) copy-start(bf16[512,320]{1,0:T(8,128)(2,1)S(1)} %reshape.723) | copy-start | bytes 983044
  65.2 6.4 %copy-start.17 = (bf16[512,320]{1,0:T(8,128)(2,1)}, bf16[512,320]{1,0:T(8,128)(2,1)S(1)}, u32[]{:S(2)}) copy-start(bf16[512,320]{1,0:T(8,128)(2,1)S(1)} %reshape.722) | copy-start | bytes 983044
  67.1 29.8 %copy-start.43 = (f32[384,32]{0,1:T(8,128)}, f32[384,32]{0,1:T(8,128)S(1)}, u32[]{:S(2)}) copy-start(f32[384,32]{0,1:T(8,128)S(1)} %get-tuple-element.471) | copy-start | bytes 147460
  68.1 317.6 %all-reduce.3.cloned.1.call-start = ((), (), s32[]{:S(2)}) async-start(), calls=%async_computation.1 | async-start | bytes 26247168 | tf_op jit(solution)/shard_map/psum | solution.py:384
  71.6 15.0 %slice-start = ((bf16[3277824]{0:T(1024)(128)(2,1)}), bf16[491520]{0:T(1024)(128)(2,1)S(1)}, s32[]{:S(2)}) async-start(bf16[3277824]{0:T(1024)(128)(2,1)} %reshape.721), calls=%async_computation.2 | async-start | bytes 1966080 | tf_op jit(solution)/shard_map/slice | solution.py:45
  98.0 7.8 %copy-start.26 = (pred[1,1,384,384]{2,3,1,0:T(8,128)(4,1)}, pred[1,1,384,384]{2,3,1,0:T(8,128)(4,1)S(1)}, u32[]{:S(2)}) copy-start(pred[1,1,384,384]{2,3,1,0:T(8,128)(4,1)S(1)} %get-tuple-element.468) | copy-start | bytes 442372
  98.0 7.8 %copy-start.24 = (pred[1,1,384,384]{2,3,1,0:T(8,128)(4,1)}, pred[1,1,384,384]{2,3,1,0:T(8,128)(4,1)S(1)}, u32[]{:S(2)}) copy-start(pred[1,1,384,384]{2,3,1,0:T(8,128)(4,1)S(1)} %get-tuple-element.466) | copy-start | bytes 442372
  98.0 12.1 %copy-start.28 = (pred[1,1,384,384]{2,3,1,0:T(8,128)(4,1)}, pred[1,1,384,384]{2,3,1,0:T(8,128)(4,1)S(1)}, u32[]{:S(2)}) copy-start(pred[1,1,384,384]{2,3,1,0:T(8,128)(4,1)S(1)} %get-tuple-element.467) | copy-start | bytes 442372
  100.9 9.3 %copy-start.9 = (bf16[384,320]{0,1:T(8,128)(2,1)}, bf16[384,320]{0,1:T(8,128)(2,1)S(1)}, u32[]{:S(2)}) copy-start(bf16[384,320]{0,1:T(8,128)(2,1)S(1)} %get-tuple-element.452) | copy-start | bytes 737284
  100.9 13.6 %copy-start.7 = (bf16[384,320]{0,1:T(8,128)(2,1)}, bf16[384,320]{0,1:T(8,128)(2,1)S(1)}, u32[]{:S(2)}) copy-start(bf16[384,320]{0,1:T(8,128)(2,1)S(1)} %get-tuple-element.451) | copy-start | bytes 737284
  100.9 13.6 %copy-start.5 = (bf16[384,320]{0,1:T(8,128)(2,1)}, bf16[384,320]{0,1:T(8,128)(2,1)S(1)}, u32[]{:S(2)}) copy-start(bf16[384,320]{0,1:T(8,128)(2,1)S(1)} %get-tuple-element.450) | copy-start | bytes 737284
  100.9 14.6 %copy-start.3 = (bf16[384,320]{0,1:T(8,128)(2,1)}, bf16[384,320]{0,1:T(8,128)(2,1)S(1)}, u32[]{:S(2)}) copy-start(bf16[384,320]{0,1:T(8,128)(2,1)S(1)} %get-tuple-element.449) | copy-start | bytes 737284
  118.0 6.7 %copy-start.12 = (f32[384,512]{1,0:T(8,128)}, f32[384,512]{1,0:T(8,128)S(1)}, u32[]{:S(2)}) copy-start(f32[384,512]{1,0:T(8,128)S(1)} %get-tuple-element.475) | copy-start | bytes 2359300
  126.9 7.5 %copy-start.19 = (bf16[384,960]{0,1:T(8,128)(2,1)}, bf16[384,960]{0,1:T(8,128)(2,1)S(1)}, u32[]{:S(2)}) copy-start(bf16[384,960]{0,1:T(8,128)(2,1)S(1)} %convolution_convert_fusion) | copy-start | bytes 2211844
  160.0 5.9 %copy-start.44 = (f32[384,32]{0,1:T(8,128)S(1)}, f32[384,32]{0,1:T(8,128)}, u32[]{:S(2)}) copy-start(f32[384,32]{0,1:T(8,128)} %copy-done.43) | copy-start | bytes 147460
  160.3 8.1 %copy-start.16 = (bf16[512,960]{1,0:T(8,128)(2,1)S(1)}, bf16[512,960]{1,0:T(8,128)(2,1)}, u32[]{:S(2)}) copy-start(bf16[512,960]{1,0:T(8,128)(2,1)} %reshape.725) | copy-start | bytes 2949124
  160.5 42.3 %collective-permute-start.2 = (bf16[384,640]{0,1:T(8,128)(2,1)S(1)}, bf16[384,640]{0,1:T(8,128)(2,1)S(1)}, u32[]{:S(2)}, u32[]{:S(2)}) collective-permute-start(bf16[384,640]{0,1:T(8,128)(2,1)S(1)} %get-tuple-element.440), channel_id=1, source_target_pairs={{3,0},{7,4},{11,8},{15,12},{19,16},{23,20},{27,24},{31,28},{35,32}... | collective-permute-start | bytes 1474568 | tf_op jit(solution)/shard_map/ppermute | solution.py:353
  161.9 40.9 %collective-permute-start.1 = (bf16[384,640]{0,1:T(8,128)(2,1)S(1)}, bf16[384,640]{0,1:T(8,128)(2,1)S(1)}, u32[]{:S(2)}, u32[]{:S(2)}) collective-permute-start(bf16[384,640]{0,1:T(8,128)(2,1)S(1)} %get-tuple-element.441), channel_id=1, source_target_pairs={{2,0},{3,1},{6,4},{7,5},{10,8},{11,9},{14,12},{15,13},{18,16},{19,... | collective-permute-start | bytes 1474568 | tf_op jit(solution)/shard_map/ppermute | solution.py:353
  163.2 39.6 %collective-permute-start = (bf16[384,640]{0,1:T(8,128)(2,1)S(1)}, bf16[384,640]{0,1:T(8,128)(2,1)S(1)}, u32[]{:S(2)}, u32[]{:S(2)}) collective-permute-start(bf16[384,640]{0,1:T(8,128)(2,1)S(1)} %get-tuple-element.439), channel_id=1, source_target_pairs={{1,0},{2,1},{3,2},{5,4},{6,5},{7,6},{9,8},{10,9},{11,10},{13,12},{... | collective-permute-start | bytes 1474568 | tf_op jit(solution)/shard_map/ppermute | solution.py:353
  169.0 34.2 %copy-start.18 = (bf16[512,320]{1,0:T(8,128)(2,1)S(1)}, bf16[512,320]{1,0:T(8,128)(2,1)}, u32[]{:S(2)}) copy-start(bf16[512,320]{1,0:T(8,128)(2,1)} %copy-done.17) | copy-start | bytes 983044
  171.4 32.3 %copy-start.40 = (bf16[512,320]{1,0:T(8,128)(2,1)S(1)}, bf16[512,320]{1,0:T(8,128)(2,1)}, u32[]{:S(2)}) copy-start(bf16[512,320]{1,0:T(8,128)(2,1)} %copy-done.39) | copy-start | bytes 983044
  (23 other events, 48.8 us)
Sparse Core Ops, SparseCore 0:
  68.2 29.4 all-gather.1
  207.7 177.9 all-reduce.2

commit v11 on v10

--- a/solution.py
+++ b/solution.py
@@ -271,7 +271,9 @@
         dn_two - normed_two * jnp.mean(dn_two * normed_two, axis=-1, keepdims=True)
     )
     d_mixed_b = d_mixed.astype(jnp.bfloat16)
-    g_out = jnp.dot(attention_output.T, d_mixed_b, preferred_element_type=jnp.float32)
+    g_out_rows = jnp.dot(
+        jnp.pad(attention_output, ((0, 0), (0, 2))).T, d_mixed_b, preferred_element_type=jnp.float32
+    )
     attention_output_gradient = jnp.dot(
         d_mixed_b, w_out.T, preferred_element_type=jnp.float32
     ).astype(jnp.bfloat16)
@@ -380,7 +382,9 @@
         + inverse_one
         * (dn_one - normed_one * jnp.mean(dn_one * normed_one, axis=-1, keepdims=True))
     ).astype(jnp.bfloat16)
-    out_and_gains = jnp.concatenate([g_out, g_gain_one[None], g_gain_two[None]], axis=0)
+    out_and_gains = lax.dynamic_update_slice(
+        g_out_rows, jnp.stack([g_gain_one, g_gain_two]), (QUERY_HEADS * HEAD_SIZE, 0)
+    )
     grad_pieces = lax.psum(
         (g_query, g_key_value, out_and_gains, g_gate, g_up, g_down), ("wide", "narrow")
     )

time: 418 us -> 416 us (level)
    ppermute x3, waiting for transfers between devices: 31.4 us -> 20.1 us  [body(): lax.ppermute(sender_block.astype(jnp.bfloat16), 'narrow', [(source, sourc...]
    psum x1, waiting for transfers between devices: 173 us -> 183 us  [body(): lax.psum((g_query, g_key_value, out_and_gains, g_gate, g_up, g_down), ('w...]
where the time goes in v11:
time: 416 us; the launch traced here: 411 us
  waiting for transfers between devices  203 us (49%)
  local copies, waits for them, and re-layouts  49.8 us (12%)
  Pallas kernels  44.2 us (11%)
  matrix products  44 us (11%)
  other arithmetic  31.4 us (8%)
  between operations  18.9 us (5%)
  loops' own time  14 us (3%)
  starting transfers between devices  5.88 us (1%)
    psum x1, waiting for transfers between devices, body(): lax.psum((g_query, g_key_value, out_and_gains, g_gate, g_up, g_down), ('w...  183 us
    pallas_call x1, Pallas kernels, gather_replica(): pl.pallas_call(gather_kernel, out_shape=jax.ShapeDtypeStruct((4, count, w...  44.2 us
    ppermute x3, waiting for transfers between devices, body(): lax.ppermute(sender_block.astype(jnp.bfloat16), 'narrow', [(source, sourc...  20.1 us
    slice x5, local copies, waits for them, and re-layouts, unpack(): pieces.append(flat[offset:offset + length].reshape(layout))  14 us
    another operation x4, loops' own time, body(): lax.cond(needed, back_span, skip_span, query_gradient_running)  10.4 us
    sub x1, other arithmetic, body(): master - learn_rate * (first_hat / (jnp.sqrt(second_hat) + adam_eps) + de...  9.19 us
    reshape x5, local copies, waits for them, and re-layouts, unpack(): pieces.append(flat[offset:offset + length].reshape(layout))  8.72 us
  transfers between devices with their start and end apart: 5, of which 2 were waited for; matrix products, arithmetic and copies ran while one was open for 8% of the time, Pallas kernels for 0%

profile of v11, /device:TPU:0, one launch (start us, length us, event | category | flops | bytes accessed | tf_op | source)
XLA Modules:
  0.0 410.9 jit_solution(4416091622226783927)
XLA Ops:
  7.2 3.3 convert_bitcast_fusion.src_ref
  10.5 44.2 %shard_map.109 = bf16[4,6402,128]{2,1,0:T(8,128)(2,1)} custom-call(bf16[6402,128]{1,0:T(8,128)(2,1)} %convert_bitcast_fusion.src_ref), custom_call_target="tpu_custom_call" | custom-call | tf_op jit(solution)/shard_map/pallas_call | solution.py:130
  54.7 7.3 %reshape.721 = bf16[3277824]{0:T(1024)(128)(2,1)} reshape(bf16[4,6402,128]{2,1,0:T(8,128)(2,1)} %shard_map.109) | data formatting | bytes 13111296 | tf_op jit(solution)/shard_map/reshape | solution.py:152
  68.6 2.9 fusion.194
  71.6 9.9 %slice.233 = bf16[6402,512]{1,0:T(8,128)(2,1)} reshape(bf16[4,6402,128]{2,1,0:T(8,128)(2,1)} %shard_map.109) | data formatting | bytes 13111296 | tf_op jit(solution)/shard_map/slice | solution.py:45
  89.7 3.8 reshape.733
  97.9 2.8 fusion.196
  100.8 4.9 %conditional.13 = (f32[5,3,384]{2,1,0:T(4,128)}, f32[5,3,384]{2,1,0:T(4,128)S(1)}) conditional(s32[]{:T(128)} %bitcast.116, () %tuple.129, (pred[1,1,384,384]{2,3,1,0:T(8,128)(4,1)S(1)}, bf16[384,5,64]{0,2,1:T(8,128)(2,1)S(1)}, bf16[384,5,3,64]{0,3,2,1:T(8,128)(2,1)S(1)}) %tuple.269), branch_computations={%region_5.6_spmd, %region_6.9_spmd} | conditional | flops 298615680 | bytes 19157008 | solution.py:220
  103.1 2.6 fusion.3
  105.7 2.9 conditional.16
  110.0 4.3 %conditional.17 = (f32[384,5,3,64]{0,3,2,1:T(8,128)S(1)}) conditional(s32[]{:T(128)} %bitcast.116, () %tuple.128, (pred[1,1,384,384]{2,3,1,0:T(8,128)(4,1)S(1)}, bf16[384,5,64]{0,2,1:T(8,128)(2,1)S(1)}, bf16[384,5,3,64]{0,3,2,1:T(8,128)(2,1)S(1)}, f32[5,3,384]{2,1,0:T(4,128)}, bf16[384,5,64]{0,2,1:T(8,128)(2,1)}) %tuple.287), branch_computations={%region_21.22_spmd, %region_22.23_spmd} | conditional | flops 575078400 | bytes 4446784 | solution.py:245
  110.7 3.6 fusion.32
  119.5 3.5 multiply_convert_fusion
  134.3 9.5 %conditional.21 = (f32[384,5,3,64]{0,3,2,1:T(8,128)S(1)}, f32[384,320]{0,1:T(8,128)S(1)}, f32[384,320]{0,1:T(8,128)S(1)}) conditional(s32[]{:T(128)} %bitcast.116, () %tuple.138, (pred[1,1,384,384]{2,3,1,0:T(8,128)(4,1)S(1)}, bf16[384,5,64]{0,2,1:T(8,128)(2,1)S(1)}, bf16[384,5,3,64]{0,3,2,1:T(8,128)(2,1)S(1)}, f32[5,3,384]{2,1,0:T(4,128)S(1)}, ...), branch_computations={%region_32.33_spmd, %region_33.34_spmd} | conditional | flops 1439907840 | bytes 46321176 | solution.py:342
  135.8 3.7 fusion.87
  146.1 4.6 %conditional.23 = (f32[384,5,3,64]{0,3,2,1:T(8,128)S(1)}, f32[384,320]{0,1:T(8,128)S(1)}, f32[384,320]{0,1:T(8,128)S(1)}) conditional(s32[]{:T(128)} %bitcast.114, f32[384,5,3,64]{0,3,2,1:T(8,128)S(1)} %get-tuple-element.334, (pred[1,1,384,384]{2,3,1,0:T(8,128)(4,1)}, bf16[384,5,64]{0,2,1:T(8,128)(2,1)}, bf16[384,5,3,64]{0,3,2,1:T(8,128)(2,1)S(1)}, ...), branch_computations={%region_36.37_spmd, %region_37.38_spmd} | conditional | flops 1440276480 | bytes 53393060 | solution.py:342
  151.6 5.5 %conditional.24 = (f32[384,5,3,64]{0,3,2,1:T(8,128)S(1)}, f32[384,320]{0,1:T(8,128)S(1)}, f32[384,320]{0,1:T(8,128)S(1)}) conditional(s32[]{:T(128)} %bitcast.113, f32[384,5,3,64]{0,3,2,1:T(8,128)S(1)} %get-tuple-element.335, (pred[1,1,384,384]{2,3,1,0:T(8,128)(4,1)S(1)}, bf16[384,5,64]{0,2,1:T(8,128)(2,1)}, ...), branch_computations={%region_38.39_spmd, %region_39.40_spmd} | conditional | flops 1440276480 | bytes 52803208 | solution.py:342
  163.1 2.6 collective-permute-start
  171.1 20.1 %collective-permute-done.2 = bf16[384,640]{0,1:T(8,128)(2,1)S(1)} collective-permute-done((bf16[384,640]{0,1:T(8,128)(2,1)S(1)}, bf16[384,640]{0,1:T(8,128)(2,1)S(1)}, u32[]{:S(2)}, u32[]{:S(2)}) %collective-permute-start.2) | collective-permute-done | bytes 491552 | tf_op jit(solution)/shard_map/ppermute | solution.py:355
  196.3 3.0 fusion.145
  200.3 182.5 %all-reduce.4.cloned.1.call-done = (f32[512,960]{0,1:T(8,128)}, f32[512,640]{1,0:T(8,128)}, f32[962,512]{1,0:T(8,128)}, f32[512,1280]{1,0:T(8,128)}, f32[512,1280]{1,0:T(8,128)}, /*index=5*/f32[1280,512]{1,0:T(8,128)}) async-done(((f32[512,960]{0,1:T(8,128)}, f32[512,640]{1,0:T(8,128)}, f32[962,512]{1,0:T(8,128)}, f32[512,1280]{1,0:T(8,128)}, f32[512,1280]{1,0:T(8,128)}, /*index=5*/f32[1280,512]{1,0:T(8,128)}), ...) | async-done | bytes 13111312 | tf_op jit(solution)/shard_map/psum | solution.py:388
  382.9 11.8 %conditional.25 = (f32[819456]{0:T(1024)}) conditional(s32[]{:T(128)} %clamp.3, (f32[512,960]{0,1:T(8,128)}, f32[512,640]{1,0:T(8,128)}, f32[962,512]{1,0:T(8,128)}) %tuple.143, (f32[962,512]{1,0:T(8,128)}, f32[512,1280]{1,0:T(8,128)}) %tuple.144, (f32[512,1280]{1,0:T(8,128)}, f32[512,1280]{1,0:T(8,128)}) %tuple.145, ...), branch_computations={%region_49.50_spmd, %region_50.51_spmd, %region_51.52_spmd, %regio... | conditional | flops 2458368 | bytes 38695996 | solution.py:429
  391.0 3.7 pad_maximum_fusion
  394.6 9.2 %multiply_subtract_fusion = (f32[819456]{0:T(1024)}, f32[819456]{0:T(1024)}, f32[819456]{0:T(1024)}, f32[819456]{0:T(1024)}) fusion(f32[819456]{0:T(1024)} %param.37, s32[]{:T(128)S(6)} %mul.507, f32[819456]{0:T(1024)} %get-tuple-element.536, f32[819456]{0:T(1024)} %param.38, f32[819456]{0:T(1024)} %param.39), kind=kLoop, calls=%fused_computation.160 | loop fusion | flops 15569664 | bytes 26222596 | tf_op jit(solution)/shard_map/sub | solution.py:438
  (185 shorter events, 69.9 us)
Async XLA Ops:
  7.2 90.8 %all-gather.2.cloned.1.call-start = ((), (), s32[]{:S(2)}) async-start(), calls=%async_computation | async-start | bytes 2457600 | tf_op jit(solution)/shard_map/all_gather | solution.py:173
  54.7 9.2 %copy-start.55 = (s32[1,3]{1,0:T(1,128)S(1)}, s32[1,3]{1,0:T(1,128)}, u32[]{:S(2)}) copy-start(s32[1,3]{1,0:T(1,128)} %param.36) | copy-start | bytes 40
  54.7 9.9 %copy-start = (bf16[384,512]{1,0:T(8,128)(2,1)S(1)}, bf16[384,512]{1,0:T(8,128)(2,1)}, u32[]{:S(2)}) copy-start(bf16[384,512]{1,0:T(8,128)(2,1)} %param.34) | copy-start | bytes 1179652
  64.6 6.9 %copy-start.38 = (bf16[512,320]{1,0:T(8,128)(2,1)}, bf16[512,320]{1,0:T(8,128)(2,1)S(1)}, u32[]{:S(2)}) copy-start(bf16[512,320]{1,0:T(8,128)(2,1)S(1)} %reshape.723) | copy-start | bytes 983044
  65.2 6.4 %copy-start.16 = (bf16[512,320]{1,0:T(8,128)(2,1)}, bf16[512,320]{1,0:T(8,128)(2,1)S(1)}, u32[]{:S(2)}) copy-start(bf16[512,320]{1,0:T(8,128)(2,1)S(1)} %reshape.722) | copy-start | bytes 983044
  67.1 29.6 %copy-start.42 = (f32[384,32]{0,1:T(8,128)}, f32[384,32]{0,1:T(8,128)S(1)}, u32[]{:S(2)}) copy-start(f32[384,32]{0,1:T(8,128)S(1)} %get-tuple-element.471) | copy-start | bytes 147460
  68.1 314.7 %all-reduce.4.cloned.1.call-start = ((), (), s32[]{:S(2)}) async-start(), calls=%async_computation.1 | async-start | bytes 26247168 | tf_op jit(solution)/shard_map/psum | solution.py:388
  71.6 14.9 %slice-start = ((bf16[3277824]{0:T(1024)(128)(2,1)}), bf16[491520]{0:T(1024)(128)(2,1)S(1)}, s32[]{:S(2)}) async-start(bf16[3277824]{0:T(1024)(128)(2,1)} %reshape.721), calls=%async_computation.2 | async-start | bytes 1966080 | tf_op jit(solution)/shard_map/slice | solution.py:45
  97.9 7.8 %copy-start.25 = (pred[1,1,384,384]{2,3,1,0:T(8,128)(4,1)}, pred[1,1,384,384]{2,3,1,0:T(8,128)(4,1)S(1)}, u32[]{:S(2)}) copy-start(pred[1,1,384,384]{2,3,1,0:T(8,128)(4,1)S(1)} %get-tuple-element.468) | copy-start | bytes 442372
  97.9 7.8 %copy-start.23 = (pred[1,1,384,384]{2,3,1,0:T(8,128)(4,1)}, pred[1,1,384,384]{2,3,1,0:T(8,128)(4,1)S(1)}, u32[]{:S(2)}) copy-start(pred[1,1,384,384]{2,3,1,0:T(8,128)(4,1)S(1)} %get-tuple-element.466) | copy-start | bytes 442372
  97.9 12.1 %copy-start.27 = (pred[1,1,384,384]{2,3,1,0:T(8,128)(4,1)}, pred[1,1,384,384]{2,3,1,0:T(8,128)(4,1)S(1)}, u32[]{:S(2)}) copy-start(pred[1,1,384,384]{2,3,1,0:T(8,128)(4,1)S(1)} %get-tuple-element.467) | copy-start | bytes 442372
  100.7 9.2 %copy-start.8 = (bf16[384,320]{0,1:T(8,128)(2,1)}, bf16[384,320]{0,1:T(8,128)(2,1)S(1)}, u32[]{:S(2)}) copy-start(bf16[384,320]{0,1:T(8,128)(2,1)S(1)} %get-tuple-element.452) | copy-start | bytes 737284
  100.7 13.6 %copy-start.6 = (bf16[384,320]{0,1:T(8,128)(2,1)}, bf16[384,320]{0,1:T(8,128)(2,1)S(1)}, u32[]{:S(2)}) copy-start(bf16[384,320]{0,1:T(8,128)(2,1)S(1)} %get-tuple-element.451) | copy-start | bytes 737284
  100.7 13.6 %copy-start.4 = (bf16[384,320]{0,1:T(8,128)(2,1)}, bf16[384,320]{0,1:T(8,128)(2,1)S(1)}, u32[]{:S(2)}) copy-start(bf16[384,320]{0,1:T(8,128)(2,1)S(1)} %get-tuple-element.450) | copy-start | bytes 737284
  100.7 14.5 %copy-start.2 = (bf16[384,320]{0,1:T(8,128)(2,1)}, bf16[384,320]{0,1:T(8,128)(2,1)S(1)}, u32[]{:S(2)}) copy-start(bf16[384,320]{0,1:T(8,128)(2,1)S(1)} %get-tuple-element.449) | copy-start | bytes 737284
  117.9 6.7 %copy-start.11 = (f32[384,512]{1,0:T(8,128)}, f32[384,512]{1,0:T(8,128)S(1)}, u32[]{:S(2)}) copy-start(f32[384,512]{1,0:T(8,128)S(1)} %get-tuple-element.475) | copy-start | bytes 2359300
  126.7 7.5 %copy-start.18 = (bf16[384,960]{0,1:T(8,128)(2,1)}, bf16[384,960]{0,1:T(8,128)(2,1)S(1)}, u32[]{:S(2)}) copy-start(bf16[384,960]{0,1:T(8,128)(2,1)S(1)} %convolution_convert_fusion) | copy-start | bytes 2211844
  159.9 5.8 %copy-start.43 = (f32[384,32]{0,1:T(8,128)S(1)}, f32[384,32]{0,1:T(8,128)}, u32[]{:S(2)}) copy-start(f32[384,32]{0,1:T(8,128)} %copy-done.42) | copy-start | bytes 147460
  160.1 8.0 %copy-start.15 = (bf16[512,960]{1,0:T(8,128)(2,1)S(1)}, bf16[512,960]{1,0:T(8,128)(2,1)}, u32[]{:S(2)}) copy-start(bf16[512,960]{1,0:T(8,128)(2,1)} %reshape.725) | copy-start | bytes 2949124
  160.3 30.9 %collective-permute-start.2 = (bf16[384,640]{0,1:T(8,128)(2,1)S(1)}, bf16[384,640]{0,1:T(8,128)(2,1)S(1)}, u32[]{:S(2)}, u32[]{:S(2)}) collective-permute-start(bf16[384,640]{0,1:T(8,128)(2,1)S(1)} %get-tuple-element.440), channel_id=1, source_target_pairs={{3,0},{7,4},{11,8},{15,12},{19,16},{23,20},{27,24},{31,28},{35,32}... | collective-permute-start | bytes 1474568 | tf_op jit(solution)/shard_map/ppermute | solution.py:355
  161.8 29.5 %collective-permute-start.1 = (bf16[384,640]{0,1:T(8,128)(2,1)S(1)}, bf16[384,640]{0,1:T(8,128)(2,1)S(1)}, u32[]{:S(2)}, u32[]{:S(2)}) collective-permute-start(bf16[384,640]{0,1:T(8,128)(2,1)S(1)} %get-tuple-element.441), channel_id=1, source_target_pairs={{2,0},{3,1},{6,4},{7,5},{10,8},{11,9},{14,12},{15,13},{18,16},{19,... | collective-permute-start | bytes 1474568 | tf_op jit(solution)/shard_map/ppermute | solution.py:355
  163.1 28.2 %collective-permute-start = (bf16[384,640]{0,1:T(8,128)(2,1)S(1)}, bf16[384,640]{0,1:T(8,128)(2,1)S(1)}, u32[]{:S(2)}, u32[]{:S(2)}) collective-permute-start(bf16[384,640]{0,1:T(8,128)(2,1)S(1)} %get-tuple-element.439), channel_id=1, source_target_pairs={{1,0},{2,1},{3,2},{5,4},{6,5},{7,6},{9,8},{10,9},{11,10},{13,12},{... | collective-permute-start | bytes 1474568 | tf_op jit(solution)/shard_map/ppermute | solution.py:355
  168.8 22.9 %copy-start.17 = (bf16[512,320]{1,0:T(8,128)(2,1)S(1)}, bf16[512,320]{1,0:T(8,128)(2,1)}, u32[]{:S(2)}) copy-start(bf16[512,320]{1,0:T(8,128)(2,1)} %copy-done.16) | copy-start | bytes 983044
  171.1 21.0 %copy-start.39 = (bf16[512,320]{1,0:T(8,128)(2,1)S(1)}, bf16[512,320]{1,0:T(8,128)(2,1)}, u32[]{:S(2)}) copy-start(bf16[512,320]{1,0:T(8,128)(2,1)} %copy-done.38) | copy-start | bytes 983044
  (22 other events, 45.7 us)
Sparse Core Ops, SparseCore 0:
  68.2 29.4 all-gather.1
  195.3 187.4 all-reduce.3

commit v12 on v10

--- a/solution.py
+++ b/solution.py
@@ -288,11 +288,26 @@
     query_gradient_running = jnp.zeros(
         (token_rows, KEYVAL_HEADS, group_width, HEAD_SIZE), jnp.float32
     )
-    key_contributions = []
-    value_contributions = []
-    for span_start in span_starts:
-        key_tensor_split, value_tensor_split, allowed, needed = span_setup(
-            span_start, key_back, value_back
+    received = []
+    own_block = None
+    for shift in reversed(range(narrow_size)):
+        span_start = (narrow_rank - shift) * range_rows
+        safe_start = jnp.maximum(span_start, 0)
+        key_tensor_split = lax.dynamic_slice_in_dim(key_back, safe_start, range_rows).reshape(
+            range_rows, KEYVAL_HEADS, HEAD_SIZE
+        )
+        value_tensor_split = lax.dynamic_slice_in_dim(value_back, safe_start, range_rows).reshape(
+            range_rows, KEYVAL_HEADS, HEAD_SIZE
+        )
+        span_segment = lax.dynamic_slice_in_dim(key_segment, safe_start, range_rows)
+        span_index = safe_start + jnp.arange(range_rows, dtype=jnp.int32)
+        allowed = (
+            (segment[:, None] == span_segment[None, :]) & (span_index[None, :] <= local_index[:, None])
+        )[None, None]
+        needed = (
+            (span_start >= 0)
+            & (span_start <= last_index)
+            & (span_start + range_rows - 1 >= first_start)
         )
 
         def back_span(carry):
@@ -340,21 +355,26 @@
         query_gradient_running, key_gradient_range, value_gradient_range = lax.cond(
             needed, back_span, skip_span, query_gradient_running
         )
-        key_contributions.append(key_gradient_range.reshape(range_rows, KEYVAL_HEADS * HEAD_SIZE))
-        value_contributions.append(
-            value_gradient_range.reshape(range_rows, KEYVAL_HEADS * HEAD_SIZE)
-        )
-    kv_sum_in = jnp.stack(
-        [jnp.concatenate(pair, axis=1) for pair in zip(key_contributions, value_contributions)]
-    )
-    kv_grad = kv_sum_in[narrow_rank]
-    for shift in range(1, narrow_size):
-        sender_block = kv_sum_in[lax.rem(narrow_rank + narrow_size - shift, narrow_size)]
-        kv_grad = kv_grad + lax.ppermute(
-            sender_block.astype(jnp.bfloat16),
-            "narrow",
-            [(source, source - shift) for source in range(shift, narrow_size)],
-        ).astype(jnp.float32)
+        kv_block = jnp.concatenate(
+            [
+                key_gradient_range.reshape(range_rows, kv_width),
+                value_gradient_range.reshape(range_rows, kv_width),
+            ],
+            axis=1,
+        )
+        if shift == 0:
+            own_block = kv_block
+        else:
+            received.append(
+                lax.ppermute(
+                    kv_block.astype(jnp.bfloat16),
+                    "narrow",
+                    [(source, source - shift) for source in range(shift, narrow_size)],
+                )
+            )
+    kv_grad = own_block
+    for block in received:
+        kv_grad = kv_grad + block.astype(jnp.float32)
     key_gradient, value_gradient = kv_grad[:, :kv_width], kv_grad[:, kv_width:]
     d_query = query_gradient_running.reshape(token_rows, QUERY_HEADS * HEAD_SIZE)
     d_query_b = apply_rotary(d_query, token_position, QUERY_HEADS, -1.0).astype(jnp.bfloat16)

time: 418 us -> 440 us (1.053)
  local copies, waits for them, and re-layouts: 49.9 us -> 55.9 us
  waiting for transfers between devices: 204 us -> 210 us
  matrix products: 44 us -> 48.9 us
    psum x1, waiting for transfers between devices: 173 us -> 190 us  [body(): lax.psum((g_query, g_key_value, out_and_gains, g_gate, g_up, g_down), ('w...]
    ppermute x3, waiting for transfers between devices: 31.4 us -> 20.4 us  [body(): lax.ppermute(kv_block.astype(jnp.bfloat16), 'narrow', [(source, source -...]
    concatenate x0 -> x3, other arithmetic: none -> 5.63 us  [body(): jnp.concatenate([key_gradient_range.reshape(range_rows, kv_width), value_...]
  transfers between devices with their start and end apart: 5 -> 5, of which waited for: 2 -> 3; matrix products, arithmetic and copies ran while one was open for 8% -> 12% of each run, Pallas kernels for 0% -> 0%
where the time goes in v12:
time: 440 us; the launch traced here: 433 us
  waiting for transfers between devices  210 us (48%)
  local copies, waits for them, and re-layouts  55.9 us (13%)
  matrix products  48.9 us (11%)
  Pallas kernels  44.2 us (10%)
  other arithmetic  35.6 us (8%)
  between operations  21.4 us (5%)
  loops' own time  12.6 us (3%)
    psum x1, waiting for transfers between devices, body(): lax.psum((g_query, g_key_value, out_and_gains, g_gate, g_up, g_down), ('w...  190 us
    pallas_call x1, Pallas kernels, gather_replica(): pl.pallas_call(gather_kernel, out_shape=jax.ShapeDtypeStruct((4, count, w...  44.2 us
    ppermute x3, waiting for transfers between devices, body(): lax.ppermute(kv_block.astype(jnp.bfloat16), 'narrow', [(source, source -...  20.4 us
    slice x5, local copies, waits for them, and re-layouts, unpack(): pieces.append(flat[offset:offset + length].reshape(layout))  14 us
  transfers between devices with their start and end apart: 5, of which 3 were waited for; matrix products, arithmetic and copies ran while one was open for 12% of the time, Pallas kernels for 0%

profile of v12, /device:TPU:0, one launch (start us, length us, event | category | flops | bytes accessed | tf_op | source)
XLA Modules:
  0.0 433.4 jit_solution(591023357521351210)
XLA Ops:
  7.2 3.3 convert_bitcast_fusion.src_ref
  10.5 44.2 %shard_map.109 = bf16[4,6402,128]{2,1,0:T(8,128)(2,1)} custom-call(bf16[6402,128]{1,0:T(8,128)(2,1)} %convert_bitcast_fusion.src_ref), custom_call_target="tpu_custom_call" | custom-call | tf_op jit(solution)/shard_map/pallas_call | solution.py:130
  54.7 7.3 %reshape.859 = bf16[3277824]{0:T(1024)(128)(2,1)} reshape(bf16[4,6402,128]{2,1,0:T(8,128)(2,1)} %shard_map.109) | data formatting | bytes 13111296 | tf_op jit(solution)/shard_map/reshape | solution.py:152
  68.6 2.9 fusion.190
  73.5 9.9 %slice.221 = bf16[6402,512]{1,0:T(8,128)(2,1)} reshape(bf16[4,6402,128]{2,1,0:T(8,128)(2,1)} %shard_map.109) | data formatting | bytes 13111296 | tf_op jit(solution)/shard_map/slice | solution.py:45
  92.4 3.9 reshape.870
  102.1 4.9 %conditional.13 = (f32[5,3,384]{2,1,0:T(4,128)}, f32[5,3,384]{2,1,0:T(4,128)S(1)}) conditional(s32[]{:T(128)} %convert_element_type.202, () %tuple.145, (pred[1,1,384,384]{2,3,1,0:T(8,128)(4,1)S(1)}, bf16[384,5,64]{0,2,1:T(8,128)(2,1)S(1)}, bf16[384,5,3,64]{0,3,2,1:T(8,128)(2,1)S(1)}) %tuple.293), branch_computations={%region_5.6_spmd, %region_6.9_spmd} | conditional | flops 298615680 | bytes 19157008 | solution.py:220
  104.4 2.6 fusion.3
  107.0 2.9 conditional.16
  111.3 5.2 %conditional.17 = (f32[384,5,3,64]{0,3,2,1:T(8,128)S(1)}) conditional(s32[]{:T(128)} %convert_element_type.202, () %tuple.144, (pred[1,1,384,384]{2,3,1,0:T(8,128)(4,1)S(1)}, bf16[384,5,64]{0,2,1:T(8,128)(2,1)S(1)}, bf16[384,5,3,64]{0,3,2,1:T(8,128)(2,1)S(1)}, f32[5,3,384]{2,1,0:T(4,128)}, bf16[1536,640]{0,1:T(8,128)(2,1)}) %tuple.294), branch_computations={%region_21.22_spmd, %region_22.23_spmd} | conditional | flops 575078400 | bytes 4348452 | solution.py:245
  113.1 3.5 fusion.32
  121.0 3.6 multiply_convert_fusion
  126.9 3.1 convolution_convert_fusion
  143.2 5.2 %conditional.22 = (f32[384,5,3,64]{0,3,2,1:T(8,128)S(1)}, bf16[384,320]{0,1:T(8,128)(2,1)}, bf16[384,320]{0,1:T(8,128)(2,1)}) conditional(s32[]{:T(128)} %convert_element_type.221, f32[384,5,3,64]{0,3,2,1:T(8,128)S(1)} %get-tuple-element.687, (s32[]{:T(128)}, s32[1536]{0:T(1024)S(1)}, s32[1,1,384,384]{2,3,1,0:T(8,128)S(1)}, s32[1,384]{1,0:T(1,128)}, ...), branch_computations={%region_34.35_spmd, %region_35.36_spmd} | conditional | flops 1440964992 | bytes 52173472 | solution.py:355
  149.0 5.6 %conditional.23 = (f32[384,5,3,64]{0,3,2,1:T(8,128)S(1)}, bf16[384,320]{0,1:T(8,128)(2,1)}, bf16[384,320]{0,1:T(8,128)(2,1)}) conditional(s32[]{:T(128)} %convert_element_type.220, f32[384,5,3,64]{0,3,2,1:T(8,128)S(1)} %get-tuple-element.688, (s32[]{:T(128)}, s32[1536]{0:T(1024)S(1)}, s32[1,1,384,384]{2,3,1,0:T(8,128)S(1)}, s32[1,384]{1,0:T(1,128)}, ...), branch_computations={%region_36.37_spmd, %region_37.38_spmd} | conditional | flops 1440964992 | bytes 52173472 | solution.py:355
  164.6 14.8 %conditional.24 = (f32[384,5,3,64]{0,3,2,1:T(8,128)S(1)}, f32[384,320]{0,1:T(8,128)S(1)}, f32[384,320]{0,1:T(8,128)}) conditional(s32[]{:T(128)} %convert_element_type.219, f32[384,5,3,64]{0,3,2,1:T(8,128)S(1)} %get-tuple-element.689, (s32[]{:T(128)}, s32[1536]{0:T(1024)S(1)}, s32[1,1,384,384]{2,3,1,0:T(8,128)S(1)}, s32[1,384]{1,0:T(1,128)}, ...), branch_computations={%region_38.39_spmd, %region_39.40_spmd} | conditional | flops 1440719232 | bytes 54631100 | solution.py:355
  168.1 4.1 fusion.137
  175.6 3.7 fusion.141
  184.9 15.9 %collective-permute-done.1 = bf16[384,640]{0,1:T(8,128)(2,1)} collective-permute-done((bf16[384,640]{0,1:T(8,128)(2,1)}, bf16[384,640]{0,1:T(8,128)(2,1)}, u32[]{:S(2)}, u32[]{:S(2)}) %collective-permute-start.1) | collective-permute-done | bytes 491552 | tf_op jit(solution)/shard_map/ppermute | solution.py:369
  200.8 4.5 %collective-permute-done = bf16[384,640]{0,1:T(8,128)(2,1)} collective-permute-done((bf16[384,640]{0,1:T(8,128)(2,1)}, bf16[384,640]{0,1:T(8,128)(2,1)}, u32[]{:S(2)}, u32[]{:S(2)}) %collective-permute-start) | collective-permute-done | bytes 491552 | tf_op jit(solution)/shard_map/ppermute | solution.py:369
  212.6 3.0 fusion.146
  216.7 189.9 %all-reduce.3.cloned.1.call-done = (f32[512,960]{0,1:T(8,128)}, f32[512,640]{1,0:T(8,128)}, f32[962,512]{1,0:T(8,128)}, f32[512,1280]{1,0:T(8,128)}, f32[512,1280]{1,0:T(8,128)}, /*index=5*/f32[1280,512]{1,0:T(8,128)}) async-done(((f32[512,960]{0,1:T(8,128)}, f32[512,640]{1,0:T(8,128)}, f32[962,512]{1,0:T(8,128)}, f32[512,1280]{1,0:T(8,128)}, f32[512,1280]{1,0:T(8,128)}, /*index=5*/f32[1280,512]{1,0:T(8,128)}), ...) | async-done | bytes 13111312 | tf_op jit(solution)/shard_map/psum | solution.py:404
  406.6 11.1 %conditional.25 = (f32[819456]{0:T(1024)S(1)}) conditional(s32[]{:T(128)} %clamp.3, (f32[512,960]{0,1:T(8,128)}, f32[512,640]{1,0:T(8,128)}, f32[962,512]{1,0:T(8,128)}) %tuple.159, (f32[962,512]{1,0:T(8,128)}, f32[512,1280]{1,0:T(8,128)}) %tuple.160, (f32[512,1280]{1,0:T(8,128)}, f32[512,1280]{1,0:T(8,128)}) %tuple.161, ...), branch_computations={%region_49.50_spmd, %region_50.51_spmd, %region_51.52_spmd, %regio... | conditional | flops 2458368 | bytes 36724772 | solution.py:445
  417.7 8.7 %multiply_subtract_fusion = (f32[819456]{0:T(1024)}, f32[819456]{0:T(1024)}, f32[819456]{0:T(1024)}, f32[819456]{0:T(1024)}) fusion(f32[819456]{0:T(1024)} %param.37, s32[]{:T(128)S(6)} %mul.544, f32[819456]{0:T(1024)S(1)} %get-tuple-element.905, f32[819456]{0:T(1024)} %param.38, f32[819456]{0:T(1024)} %param.39), kind=kLoop, calls=%fused_computation.167 | loop fusion | flops 15569664 | bytes 26222596 | tf_op jit(solution)/shard_map/sub | solution.py:454
  (179 shorter events, 87.1 us)
Async XLA Ops:
  7.2 93.4 %all-gather.2.cloned.1.call-start = ((), (), s32[]{:S(2)}) async-start(), calls=%async_computation | async-start | bytes 2457600 | tf_op jit(solution)/shard_map/all_gather | solution.py:173
  54.7 9.7 %copy-start.45 = (s32[1,3]{1,0:T(1,128)S(1)}, s32[1,3]{1,0:T(1,128)}, u32[]{:S(2)}) copy-start(s32[1,3]{1,0:T(1,128)} %param.36) | copy-start | bytes 40
  54.7 10.5 %copy-start = (bf16[384,512]{1,0:T(8,128)(2,1)S(1)}, bf16[384,512]{1,0:T(8,128)(2,1)}, u32[]{:S(2)}) copy-start(bf16[384,512]{1,0:T(8,128)(2,1)} %param.34) | copy-start | bytes 1179652
  64.8 35.0 %copy-start.27 = (s32[384]{0:T(512)}, s32[384]{0:T(512)S(1)}, u32[]{:S(2)}) copy-start(s32[384]{0:T(512)S(1)} %get-tuple-element.851) | copy-start | bytes 4612
  64.9 34.9 %copy-start.38 = (s32[384]{0:T(512)}, s32[384]{0:T(512)S(1)}, u32[]{:S(2)}) copy-start(s32[384]{0:T(512)S(1)} %get-tuple-element.775) | copy-start | bytes 4612
  65.2 6.3 %copy-start.22 = (bf16[512,320]{1,0:T(8,128)(2,1)}, bf16[512,320]{1,0:T(8,128)(2,1)S(1)}, u32[]{:S(2)}) copy-start(bf16[512,320]{1,0:T(8,128)(2,1)S(1)} %reshape.861) | copy-start | bytes 983044
  65.8 5.8 %copy-start.15 = (bf16[512,320]{1,0:T(8,128)(2,1)}, bf16[512,320]{1,0:T(8,128)(2,1)S(1)}, u32[]{:S(2)}) copy-start(bf16[512,320]{1,0:T(8,128)(2,1)S(1)} %reshape.860) | copy-start | bytes 983044
  68.1 338.5 %all-reduce.3.cloned.1.call-start = ((), (), s32[]{:S(2)}) async-start(), calls=%async_computation.1 | async-start | bytes 26247168 | tf_op jit(solution)/shard_map/psum | solution.py:404
  73.5 15.7 %slice-start = ((bf16[3277824]{0:T(1024)(128)(2,1)}), bf16[491520]{0:T(1024)(128)(2,1)S(1)}, s32[]{:S(2)}) async-start(bf16[3277824]{0:T(1024)(128)(2,1)} %reshape.859), calls=%async_computation.2 | async-start | bytes 1966080 | tf_op jit(solution)/shard_map/slice | solution.py:45
  102.0 5.0 %copy-start.20 = (bf16[384,320]{0,1:T(8,128)(2,1)}, bf16[384,320]{0,1:T(8,128)(2,1)S(1)}, u32[]{:S(2)}) copy-start(bf16[384,320]{0,1:T(8,128)(2,1)S(1)} %get-tuple-element.820) | copy-start | bytes 737284
  102.0 5.0 %copy-start.19 = (bf16[384,320]{0,1:T(8,128)(2,1)}, bf16[384,320]{0,1:T(8,128)(2,1)S(1)}, u32[]{:S(2)}) copy-start(bf16[384,320]{0,1:T(8,128)(2,1)S(1)} %get-tuple-element.819) | copy-start | bytes 737284
  119.4 7.3 %copy-start.10 = (f32[384,512]{1,0:T(8,128)}, f32[384,512]{1,0:T(8,128)S(1)}, u32[]{:S(2)}) copy-start(f32[384,512]{1,0:T(8,128)S(1)} %get-tuple-element.844) | copy-start | bytes 2359300
  126.9 7.4 %copy-start.5 = (f32[384,512]{1,0:T(8,128)}, f32[384,512]{1,0:T(8,128)S(1)}, u32[]{:S(2)}) copy-start(f32[384,512]{1,0:T(8,128)S(1)} %multiply_add_fusion.6) | copy-start | bytes 2359300
  134.3 4.3 copy-start.9
  136.7 3.4 copy-start.39
  136.7 4.0 copy-start.28
  156.5 28.5 %collective-permute-start.2 = (bf16[384,640]{0,1:T(8,128)(2,1)}, bf16[384,640]{0,1:T(8,128)(2,1)}, u32[]{:S(2)}, u32[]{:S(2)}) collective-permute-start(bf16[384,640]{0,1:T(8,128)(2,1)} %pad_maximum_fusion.9), channel_id=1, source_target_pairs={{1,0},{2,1},{3,2},{5,4},{6,5},{7,6},{9,8},{10,9},{11,10},{13,12},{... | collective-permute-start | bytes 1474568 | tf_op jit(solution)/shard_map/ppermute | solution.py:369
  159.7 41.1 %collective-permute-start.1 = (bf16[384,640]{0,1:T(8,128)(2,1)}, bf16[384,640]{0,1:T(8,128)(2,1)}, u32[]{:S(2)}, u32[]{:S(2)}) collective-permute-start(bf16[384,640]{0,1:T(8,128)(2,1)} %pad_maximum_fusion.8), channel_id=1, source_target_pairs={{2,0},{3,1},{6,4},{7,5},{10,8},{11,9},{14,12},{15,13},{18,16},{19,... | collective-permute-start | bytes 1474568 | tf_op jit(solution)/shard_map/ppermute | solution.py:369
  162.8 42.5 %collective-permute-start = (bf16[384,640]{0,1:T(8,128)(2,1)}, bf16[384,640]{0,1:T(8,128)(2,1)}, u32[]{:S(2)}, u32[]{:S(2)}) collective-permute-start(bf16[384,640]{0,1:T(8,128)(2,1)} %pad_maximum_fusion.7), channel_id=1, source_target_pairs={{3,0},{7,4},{11,8},{15,12},{19,16},{23,20},{27,24},{31,28},{35,32}... | collective-permute-start | bytes 1474568 | tf_op jit(solution)/shard_map/ppermute | solution.py:369
  175.6 3.7 copy-start.18
  179.5 3.0 copy-start.25
  182.5 24.6 %copy-start.16 = (bf16[512,320]{1,0:T(8,128)(2,1)S(1)}, bf16[512,320]{1,0:T(8,128)(2,1)}, u32[]{:S(2)}) copy-start(bf16[512,320]{1,0:T(8,128)(2,1)} %copy-done.15) | copy-start | bytes 983044
  184.9 22.7 %copy-start.23 = (bf16[512,320]{1,0:T(8,128)(2,1)S(1)}, bf16[512,320]{1,0:T(8,128)(2,1)}, u32[]{:S(2)}) copy-start(bf16[512,320]{1,0:T(8,128)(2,1)} %copy-done.22) | copy-start | bytes 983044
  211.5 4.1 copy-start.6
  (14 other events, 29.7 us)
Sparse Core Ops, SparseCore 0:
  68.2 29.4 all-gather.1
  211.6 194.9 all-reduce.2

commit v13 on v10

--- a/solution.py
+++ b/solution.py
@@ -160,6 +160,8 @@
     last_index = local_index[token_rows - 1]
     range_rows = token_rows
     span_starts = list(range(0, group_rows, range_rows))
+    forward_rows = min(512, group_rows)
+    forward_starts = list(range(0, group_rows, forward_rows))
     resid = tokens.astype(jnp.float32)
     normed_one, inverse_one = normalize(resid)
     hidden_one = (normed_one * gain_one.astype(jnp.float32)).astype(jnp.bfloat16)
@@ -176,7 +178,7 @@
     key_all, value_all = kv_all[:, :kv_width], kv_all[:, kv_width:]
     query_tensor_split = query_batch.reshape(token_rows, KEYVAL_HEADS, group_width, HEAD_SIZE)
 
-    def span_setup(span_start, key_source, value_source):
+    def span_setup(span_start, key_source, value_source, range_rows=range_rows):
         key_tensor_split = lax.slice_in_dim(
             key_source, span_start, span_start + range_rows
         ).reshape(range_rows, KEYVAL_HEADS, HEAD_SIZE)
@@ -193,9 +195,9 @@
 
     running_maximum = jnp.full((KEYVAL_HEADS, group_width, token_rows), masked_logits, jnp.float32)
     running_denominator = jnp.zeros((KEYVAL_HEADS, group_width, token_rows), jnp.float32)
-    for span_start in span_starts:
+    for span_start in forward_starts:
         key_tensor_split, value_tensor_split, allowed, needed = span_setup(
-            span_start, key_all, value_all
+            span_start, key_all, value_all, forward_rows
         )
 
         def extend(carry):
@@ -222,9 +224,9 @@
         )
     lse = running_maximum + jnp.log(running_denominator)
     running_total = jnp.zeros((token_rows, KEYVAL_HEADS, group_width, HEAD_SIZE), jnp.float32)
-    for span_start in span_starts:
+    for span_start in forward_starts:
         key_tensor_split, value_tensor_split, allowed, needed = span_setup(
-            span_start, key_all, value_all
+            span_start, key_all, value_all, forward_rows
         )
 
         def weigh_values(carry):

time: 418 us -> 428 us (1.024)
    psum x1, waiting for transfers between devices: 173 us -> 180 us  [body(): lax.psum((g_query, g_key_value, out_and_gains, g_gate, g_up, g_down), ('w...]
  transfers between devices with their start and end apart: 5 -> 5, of which waited for: 2 -> 2; matrix products, arithmetic and copies ran while one was open for 8% -> 9% of each run, Pallas kernels for 0% -> 0%
where the time goes in v13:
time: 428 us; the launch traced here: 423 us
  waiting for transfers between devices  208 us (49%)
  local copies, waits for them, and re-layouts  51.5 us (12%)
  matrix products  46.4 us (11%)
  Pallas kernels  44.2 us (10%)
  other arithmetic  32.3 us (8%)
  between operations  20.3 us (5%)
  loops' own time  13.2 us (3%)
  starting transfers between devices  6.8 us (2%)
    psum x1, waiting for transfers between devices, body(): lax.psum((g_query, g_key_value, out_and_gains, g_gate, g_up, g_down), ('w...  180 us
    pallas_call x1, Pallas kernels, gather_replica(): pl.pallas_call(gather_kernel, out_shape=jax.ShapeDtypeStruct((4, count, w...  44.2 us
    ppermute x3, waiting for transfers between devices, body(): lax.ppermute(sender_block.astype(jnp.bfloat16), 'narrow', [(source, sourc...  27.8 us
    slice x5, local copies, waits for them, and re-layouts, unpack(): pieces.append(flat[offset:offset + length].reshape(layout))  14.4 us
    another operation x4, loops' own time, body(): lax.cond(needed, back_span, skip_span, query_gradient_running)  10.5 us
    reshape x5, local copies, waits for them, and re-layouts, unpack(): pieces.append(flat[offset:offset + length].reshape(layout))  9.19 us
    sub x1, other arithmetic, body(): master - learn_rate * (first_hat / (jnp.sqrt(second_hat) + adam_eps) + de...  9.19 us
  transfers between devices with their start and end apart: 5, of which 2 were waited for; matrix products, arithmetic and copies ran while one was open for 9% of the time, Pallas kernels for 0%

profile of v13, /device:TPU:0, one launch (start us, length us, event | category | flops | bytes accessed | tf_op | source)
XLA Modules:
  0.0 422.6 jit_solution(8567240874433155938)
XLA Ops:
  7.2 3.3 convert_bitcast_fusion.src_ref
  10.5 44.2 %shard_map.109 = bf16[4,6402,128]{2,1,0:T(8,128)(2,1)} custom-call(bf16[6402,128]{1,0:T(8,128)(2,1)} %convert_bitcast_fusion.src_ref), custom_call_target="tpu_custom_call" | custom-call | tf_op jit(solution)/shard_map/pallas_call | solution.py:130
  54.7 7.3 %reshape.766 = bf16[3277824]{0:T(1024)(128)(2,1)} reshape(bf16[4,6402,128]{2,1,0:T(8,128)(2,1)} %shard_map.109) | data formatting | bytes 13111296 | tf_op jit(solution)/shard_map/reshape | solution.py:152
  68.4 3.4 fusion.156
  71.7 9.9 %slice.268 = bf16[6402,512]{1,0:T(8,128)(2,1)} reshape(bf16[4,6402,128]{2,1,0:T(8,128)(2,1)} %shard_map.109) | data formatting | bytes 13111296 | tf_op jit(solution)/shard_map/slice | solution.py:45
  88.1 3.8 reshape.775
  92.0 3.8 reshape.776
  102.2 6.3 %conditional.11 = (f32[5,3,384]{2,1,0:T(4,128)}, f32[5,3,384]{2,1,0:T(4,128)S(1)}) conditional(s32[]{:T(128)} %bitcast.115, () %tuple.117, (pred[1,1,384,512]{2,3,1,0:T(8,128)(4,1)S(1)}, bf16[512,5,64]{0,2,1:T(8,128)(2,1)S(1)}, bf16[384,5,3,64]{0,3,2,1:T(8,128)(2,1)S(1)}) %tuple.245), branch_computations={%region_5.6_spmd, %region_6.9_spmd} | conditional | flops 398148480 | bytes 25235472 | solution.py:222
  105.2 3.2 fusion.3
  111.8 6.1 %conditional.14 = (f32[384,5,3,64]{0,3,2,1:T(8,128)S(1)}) conditional(s32[]{:T(128)} %bitcast.115, () %tuple.116, (pred[1,1,384,512]{2,3,1,0:T(8,128)(4,1)S(1)}, bf16[512,5,64]{0,2,1:T(8,128)(2,1)S(1)}, bf16[384,5,3,64]{0,3,2,1:T(8,128)(2,1)S(1)}, f32[5,3,384]{2,1,0:T(4,128)}, bf16[1536,640]{0,1:T(8,128)(2,1)}) %tuple.246), branch_computations={%region_17.18_spmd, %region_18.19_spmd} | conditional | flops 766771200 | bytes 5052964 | solution.py:247
  113.6 4.3 %fusion.26 = f32[384,5,3,64]{0,3,2,1:T(8,128)S(1)} fusion(bf16[512,5,64,1]{0,2,3,1:T(8,128)(2,1)} %bitcast.517, f32[5,3,384]{2,1,0:T(4,128)} %get-tuple-element.269, pred[384,512]{0,1:T(8,128)(4,1)S(1)} %bitcast.485, bf16[384,5,3,64]{0,3,2,1:T(8,128)(2,1)S(1)} %get-tuple-element.268, bf16[512,5,64]{0,2,1:T(8,128)(2,1)} %copy-done.20), kind=kOutput, calls=%fused_computation.35 | convolution fusion | flops 766771200 | bytes 3086848 | tf_op jit(solution)/shard_map/cond/branch_1_fun/grqk,kgd->qgrd/dot_general | solution.py:243
  118.3 2.5 multiply_reduce_fusion.3
  122.4 3.6 multiply_convert_fusion
  137.8 11.2 %conditional.17 = (f32[384,5,3,64]{0,3,2,1:T(8,128)S(1)}, f32[384,320]{0,1:T(8,128)S(1)}, f32[384,320]{0,1:T(8,128)S(1)}) conditional(s32[]{:T(128)} %bitcast.131, () %tuple.124, (s32[1536]{0:T(1024)S(1)}, s32[1,1,384,384]{2,3,1,0:T(8,128)S(1)}, s32[1536]{0:T(1024)S(1)}, s32[1,1,384,384]{2,3,1,0:T(8,128)}, bf16[1536,640]{0,1:T(8,128)(2,1)}, ...), branch_computations={%region_26.27_spmd, %region_27.28_spmd} | conditional | flops 1440350208 | bytes 48640536 | solution.py:342
  141.8 3.0 fusion.63
  151.6 4.5 %conditional.19 = (f32[384,5,3,64]{0,3,2,1:T(8,128)S(1)}, f32[384,320]{0,1:T(8,128)S(1)}, f32[384,320]{0,1:T(8,128)S(1)}) conditional(s32[]{:T(128)} %bitcast.129, f32[384,5,3,64]{0,3,2,1:T(8,128)S(1)} %get-tuple-element.363, (s32[1536]{0:T(1024)S(1)}, s32[1,1,384,384]{2,3,1,0:T(8,128)S(1)}, s32[1536]{0:T(1024)S(1)}, ...), branch_computations={%region_30.31_spmd, %region_31.32_spmd} | conditional | flops 1440718848 | bytes 53064244 | solution.py:342
  157.2 5.3 %conditional.20 = (f32[384,5,3,64]{0,3,2,1:T(8,128)S(1)}, f32[384,320]{0,1:T(8,128)S(1)}, f32[384,320]{0,1:T(8,128)S(1)}) conditional(s32[]{:T(128)} %bitcast.128, f32[384,5,3,64]{0,3,2,1:T(8,128)S(1)} %get-tuple-element.364, (s32[1536]{0:T(1024)S(1)}, s32[1,1,384,384]{2,3,1,0:T(8,128)S(1)}, s32[1536]{0:T(1024)S(1)}, ...), branch_computations={%region_32.33_spmd, %region_33.34_spmd} | conditional | flops 1440718848 | bytes 53064244 | solution.py:342
  167.5 3.7 collective-permute-start
  176.7 27.7 %collective-permute-done.2 = bf16[384,640]{0,1:T(8,128)(2,1)S(1)} collective-permute-done((bf16[384,640]{0,1:T(8,128)(2,1)S(1)}, bf16[384,640]{0,1:T(8,128)(2,1)S(1)}, u32[]{:S(2)}, u32[]{:S(2)}) %collective-permute-start.2) | collective-permute-done | bytes 491552 | tf_op jit(solution)/shard_map/ppermute | solution.py:355
  210.3 3.0 fusion.105
  214.3 180.2 %all-reduce.3.cloned.1.call-done = (f32[512,960]{0,1:T(8,128)}, f32[512,640]{1,0:T(8,128)}, f32[962,512]{1,0:T(8,128)}, f32[512,1280]{1,0:T(8,128)}, f32[512,1280]{1,0:T(8,128)}, /*index=5*/f32[1280,512]{1,0:T(8,128)}) async-done(((f32[512,960]{0,1:T(8,128)}, f32[512,640]{1,0:T(8,128)}, f32[962,512]{1,0:T(8,128)}, f32[512,1280]{1,0:T(8,128)}, f32[512,1280]{1,0:T(8,128)}, /*index=5*/f32[1280,512]{1,0:T(8,128)}), ...) | async-done | bytes 13111312 | tf_op jit(solution)/shard_map/psum | solution.py:386
  394.5 11.8 %conditional.21 = (f32[819456]{0:T(1024)}) conditional(s32[]{:T(128)} %clamp.3, (f32[512,960]{0,1:T(8,128)}, f32[512,640]{1,0:T(8,128)}, f32[962,512]{1,0:T(8,128)}) %tuple.129, (f32[962,512]{1,0:T(8,128)}, f32[512,1280]{1,0:T(8,128)}) %tuple.130, (f32[512,1280]{1,0:T(8,128)}, f32[512,1280]{1,0:T(8,128)}) %tuple.131, ...), branch_computations={%region_43.44_spmd, %region_44.45_spmd, %region_45.46_spmd, %regio... | conditional | flops 2458368 | bytes 38695996 | solution.py:427
  402.6 3.7 pad_maximum_fusion
  406.3 9.2 %multiply_subtract_fusion = (f32[819456]{0:T(1024)}, f32[819456]{0:T(1024)}, f32[819456]{0:T(1024)}, f32[819456]{0:T(1024)}) fusion(f32[819456]{0:T(1024)} %param.33, s32[]{:T(128)S(6)} %mul.492, f32[819456]{0:T(1024)} %get-tuple-element.574, f32[819456]{0:T(1024)} %param.34, f32[819456]{0:T(1024)} %param.35), kind=kLoop, calls=%fused_computation.124 | loop fusion | flops 15569664 | bytes 26222596 | tf_op jit(solution)/shard_map/sub | solution.py:436
  (188 shorter events, 72.0 us)
Async XLA Ops:
  7.2 93.7 %all-gather.2.cloned.1.call-start = ((), (), s32[]{:S(2)}) async-start(), calls=%async_computation | async-start | bytes 2457600 | tf_op jit(solution)/shard_map/all_gather | solution.py:175
  54.7 9.2 %copy-start.40 = (s32[1,3]{1,0:T(1,128)S(1)}, s32[1,3]{1,0:T(1,128)}, u32[]{:S(2)}) copy-start(s32[1,3]{1,0:T(1,128)} %param.32) | copy-start | bytes 40
  54.7 9.8 %copy-start = (bf16[384,512]{1,0:T(8,128)(2,1)S(1)}, bf16[384,512]{1,0:T(8,128)(2,1)}, u32[]{:S(2)}) copy-start(bf16[384,512]{1,0:T(8,128)(2,1)} %param.30) | copy-start | bytes 1179652
  65.1 6.7 %copy-start.12 = (bf16[512,320]{1,0:T(8,128)(2,1)}, bf16[512,320]{1,0:T(8,128)(2,1)S(1)}, u32[]{:S(2)}) copy-start(bf16[512,320]{1,0:T(8,128)(2,1)S(1)} %reshape.767) | copy-start | bytes 983044
  67.1 32.8 %copy-start.35 = (f32[384,32]{0,1:T(8,128)}, f32[384,32]{0,1:T(8,128)S(1)}, u32[]{:S(2)}) copy-start(f32[384,32]{0,1:T(8,128)S(1)} %get-tuple-element.517) | copy-start | bytes 147460
  68.0 326.5 %all-reduce.3.cloned.1.call-start = ((), (), s32[]{:S(2)}) async-start(), calls=%async_computation.1 | async-start | bytes 26247168 | tf_op jit(solution)/shard_map/psum | solution.py:386
  71.7 14.2 %slice-start = ((bf16[3277824]{0:T(1024)(128)(2,1)}), bf16[491520]{0:T(1024)(128)(2,1)S(1)}, s32[]{:S(2)}) async-start(bf16[3277824]{0:T(1024)(128)(2,1)} %reshape.766), calls=%async_computation.2 | async-start | bytes 1966080 | tf_op jit(solution)/shard_map/slice | solution.py:45
  86.8 11.0 %copy-start.10 = (bf16[512,960]{1,0:T(8,128)(2,1)}, bf16[512,960]{1,0:T(8,128)(2,1)S(1)}, u32[]{:S(2)}) copy-start(bf16[512,960]{1,0:T(8,128)(2,1)S(1)} %reshape.770) | copy-start | bytes 2949124
  102.2 6.3 %copy-start.19 = (bf16[512,320]{0,1:T(8,128)(2,1)}, bf16[512,320]{0,1:T(8,128)(2,1)S(1)}, u32[]{:S(2)}) copy-start(bf16[512,320]{0,1:T(8,128)(2,1)S(1)} %get-tuple-element.499) | copy-start | bytes 983044
  118.3 3.4 copy-start.5
  120.8 6.8 %copy-start.7 = (f32[384,512]{1,0:T(8,128)}, f32[384,512]{1,0:T(8,128)S(1)}, u32[]{:S(2)}) copy-start(f32[384,512]{1,0:T(8,128)S(1)} %get-tuple-element.521) | copy-start | bytes 2359300
  127.8 6.5 %copy-start.3 = (f32[384,512]{1,0:T(8,128)}, f32[384,512]{1,0:T(8,128)S(1)}, u32[]{:S(2)}) copy-start(f32[384,512]{1,0:T(8,128)S(1)} %multiply_add_fusion.5) | copy-start | bytes 2359300
  130.0 7.8 %copy-start.14 = (bf16[384,960]{0,1:T(8,128)(2,1)}, bf16[384,960]{0,1:T(8,128)(2,1)S(1)}, u32[]{:S(2)}) copy-start(bf16[384,960]{0,1:T(8,128)(2,1)S(1)} %convolution_convert_fusion) | copy-start | bytes 2211844
  134.3 3.5 copy-start.39
  164.3 6.9 %copy-start.36 = (f32[384,32]{0,1:T(8,128)S(1)}, f32[384,32]{0,1:T(8,128)}, u32[]{:S(2)}) copy-start(f32[384,32]{0,1:T(8,128)} %copy-done.35) | copy-start | bytes 147460
  164.3 6.9 %copy-start.38 = (f32[384,32]{0,1:T(8,128)S(1)}, f32[384,32]{0,1:T(8,128)}, u32[]{:S(2)}) copy-start(f32[384,32]{0,1:T(8,128)} %get-tuple-element.515) | copy-start | bytes 147460
  164.8 8.9 %copy-start.11 = (bf16[512,960]{1,0:T(8,128)(2,1)S(1)}, bf16[512,960]{1,0:T(8,128)(2,1)}, u32[]{:S(2)}) copy-start(bf16[512,960]{1,0:T(8,128)(2,1)} %copy-done.10) | copy-start | bytes 2949124
  164.8 39.7 %collective-permute-start.2 = (bf16[384,640]{0,1:T(8,128)(2,1)S(1)}, bf16[384,640]{0,1:T(8,128)(2,1)S(1)}, u32[]{:S(2)}, u32[]{:S(2)}) collective-permute-start(bf16[384,640]{0,1:T(8,128)(2,1)S(1)} %get-tuple-element.493), channel_id=1, source_target_pairs={{3,0},{7,4},{11,8},{15,12},{19,16},{23,20},{27,24},{31,28},{35,32}... | collective-permute-start | bytes 1474568 | tf_op jit(solution)/shard_map/ppermute | solution.py:355
  166.2 38.2 %collective-permute-start.1 = (bf16[384,640]{0,1:T(8,128)(2,1)S(1)}, bf16[384,640]{0,1:T(8,128)(2,1)S(1)}, u32[]{:S(2)}, u32[]{:S(2)}) collective-permute-start(bf16[384,640]{0,1:T(8,128)(2,1)S(1)} %get-tuple-element.494), channel_id=1, source_target_pairs={{2,0},{3,1},{6,4},{7,5},{10,8},{11,9},{14,12},{15,13},{18,16},{19,... | collective-permute-start | bytes 1474568 | tf_op jit(solution)/shard_map/ppermute | solution.py:355
  167.5 36.9 %collective-permute-start = (bf16[384,640]{0,1:T(8,128)(2,1)S(1)}, bf16[384,640]{0,1:T(8,128)(2,1)S(1)}, u32[]{:S(2)}, u32[]{:S(2)}) collective-permute-start(bf16[384,640]{0,1:T(8,128)(2,1)S(1)} %get-tuple-element.492), channel_id=1, source_target_pairs={{1,0},{2,1},{3,2},{5,4},{6,5},{7,6},{9,8},{10,9},{11,10},{13,12},{... | collective-permute-start | bytes 1474568 | tf_op jit(solution)/shard_map/ppermute | solution.py:355
  176.7 28.2 %copy-start.13 = (bf16[512,320]{1,0:T(8,128)(2,1)S(1)}, bf16[512,320]{1,0:T(8,128)(2,1)}, u32[]{:S(2)}) copy-start(bf16[512,320]{1,0:T(8,128)(2,1)} %copy-done.12) | copy-start | bytes 983044
  176.7 28.6 %copy-start.32 = (bf16[512,320]{1,0:T(8,128)(2,1)S(1)}, bf16[512,320]{1,0:T(8,128)(2,1)}, u32[]{:S(2)}) copy-start(bf16[512,320]{1,0:T(8,128)(2,1)} %copy-done.31) | copy-start | bytes 983044
  204.8 2.9 copy-start.6
  209.1 4.1 copy-start.4
  (19 other events, 30.7 us)
Sparse Core Ops, SparseCore 0:
  68.2 29.4 all-gather.1
  209.3 185.1 all-reduce.2
